TPU v7x, 32 devices: a whole 2x2x4 slice. The times are simulated.
32 devices in a mesh: dp: 1, expert: 16 (over z, x, core), tensor: 2 (over y).
Axes of the slice: x: 2, y: 2, z: 4, core: 2. Of those that a mesh axis runs over, the one named last changes fastest.
Arguments:
- quant_tokens: bfloat16 [512, 5120], P(('dp', 'expert', 'tensor')), may hold values from -6 to 6
- token_scales: float32 [512, 40], P(('dp', 'expert', 'tensor')), may hold values from 0.2 to 2.5
- expert_ids: int32 [512, 6], P(('dp', 'expert', 'tensor')), may hold values from 0 to 15, all different within a row; in each aligned block of 32 rows (0 to 31, 32 to 63, ...) at most 13 rows name the same one
- gate_weights: bfloat16 [512, 6], P(('dp', 'expert', 'tensor')), may hold values from 0.049804688 to 1
- grad_out: bfloat16 [512, 5120], P(('dp', 'expert', 'tensor')), may hold values from -4 to 4
- w_in: bfloat16 [5120, 16, 2, 1536], P('dp', 'expert', None, 'tensor'), may hold values from -0.078125 to 0.078125
- w_out: bfloat16 [5120, 16, 1536], P('dp', 'expert', 'tensor'), may hold values from -0.15625 to 0.15625
Outputs:
- grad_tokens: bfloat16 [512, 5120], P(('dp', 'expert', 'tensor'))
- grad_gates: float32 [512, 6], P(('dp', 'expert', 'tensor'))
- grad_w_in: bfloat16 [5120, 16, 2, 1536], P('dp', 'expert', None, 'tensor')
- grad_w_out: bfloat16 [5120, 16, 1536], P('dp', 'expert', 'tensor')
Inputs may be any that keep to these rules, and one draw needn't show every extreme that they name: `expert_ids`: each row names 6 different experts; in each aligned block of 32 rows (the tokens of one index pair of dp and expert) no expert is named by more than 13 rows, a bound that some block reaches.
All inputs are finite; a program needn't handle non-finite values.
Results may differ from a plain program's by a relative error of at most 0.012.
Values may be sent and summed in bfloat16 or wider, within the bound.
No kernel may reach another device: no remote copies, remote signals or barrier semaphores. Data moves between devices by JAX's collectives and lax.ppermute only.
A program may use at most 128 MiB of HBM per device.

v0:
```python
import jax
import jax.numpy as jnp
from jax import lax
from jax.sharding import PartitionSpec as P


def slot_table(routes_all, experts, n_expert, capacity):
    block, top = routes_all.shape
    flat_ids = routes_all.reshape(block * top)
    onehot = (flat_ids[:, None] == jnp.arange(experts, dtype=jnp.int32)[None, :]).astype(jnp.int32)
    before = jnp.sum(onehot * (jnp.cumsum(onehot, axis=0) - 1), axis=1)
    held = experts // n_expert
    owner = flat_ids // held
    local_index = flat_ids % held
    slot_of = ((local_index * n_expert + owner) * capacity + before).reshape(block, top)
    return jnp.arange(experts * capacity, dtype=jnp.int32)[:, None, None] == slot_of[None]


def expert_math(projected, back, gate_rows):
    gate_pre = projected[:, :, 0]
    up_value = projected[:, :, 1]
    sigmoid_gate = jax.nn.sigmoid(gate_pre)
    activated = gate_pre * sigmoid_gate
    hidden = activated * up_value
    gate_piece = jnp.sum(hidden * back, axis=2).astype(jnp.bfloat16)
    grad_hidden = gate_rows * back
    grad_pre = grad_hidden * up_value * sigmoid_gate * (1.0 + gate_pre * (1.0 - sigmoid_gate))
    grad_up = grad_hidden * activated
    grad_both = jnp.stack([grad_pre, grad_up], axis=2).astype(jnp.bfloat16)
    scaled_hidden = (gate_rows * hidden).astype(jnp.bfloat16)
    return (gate_piece, grad_both, scaled_hidden)


def body(quant_tokens, token_scales, expert_ids, gate_weights, grad_out, w_in, w_out):
    tok_dev, width = quant_tokens.shape
    blocks = token_scales.shape[1]
    top = expert_ids.shape[1]
    n_tensor = lax.axis_size("tensor")
    n_expert = lax.axis_size("expert")
    held = w_in.shape[1]
    experts = held * n_expert
    block = tok_dev * n_tensor
    capacity = max(2, block * top * 13 // (12 * experts))
    rows = n_expert * capacity
    slots = experts * capacity
    share = width // n_tensor
    hidden_dev = w_out.shape[2]
    scaled = (
        (
            quant_tokens.astype(jnp.float32).reshape(tok_dev, blocks, width // blocks)
            * token_scales[:, :, None]
        )
        .reshape(tok_dev, width)
        .astype(jnp.bfloat16)
    )
    routes_all = lax.all_gather(expert_ids, "tensor", axis=0, tiled=True)
    routed = slot_table(routes_all, experts, n_expert, capacity)
    routed_float = routed.astype(jnp.float32)
    placing = jnp.any(routed, axis=2).astype(jnp.bfloat16)
    gates_all = lax.all_gather(gate_weights, "tensor", axis=0, tiled=True)
    tokens_part, cotangent_part = (
        lax.all_to_all(scaled, "tensor", split_axis=1, concat_axis=0, tiled=True),
        lax.all_to_all(grad_out, "tensor", split_axis=1, concat_axis=0, tiled=True),
    )
    slot_gates = jnp.einsum(
        "stk,tk->s", routed_float, gates_all.astype(jnp.float32), precision=lax.Precision.HIGHEST
    )
    slot_inputs = (
        jnp.dot(placing, tokens_part, preferred_element_type=jnp.float32)
        .astype(jnp.bfloat16)
        .reshape(held, n_expert, capacity, share)
    )
    slot_cotangent = (
        jnp.dot(placing, cotangent_part, preferred_element_type=jnp.float32)
        .astype(jnp.bfloat16)
        .reshape(held, n_expert, capacity, share)
    )
    part_inputs, part_cotangent, recv_gates = (
        lax.all_to_all(slot_inputs, "expert", split_axis=1, concat_axis=1, tiled=True),
        lax.all_to_all(slot_cotangent, "expert", split_axis=1, concat_axis=1, tiled=True),
        lax.all_to_all(
            slot_gates.astype(jnp.bfloat16).reshape(held, n_expert, capacity),
            "expert",
            split_axis=1,
            concat_axis=1,
            tiled=True,
        ),
    )
    recv_inputs, recv_cotangent = (
        lax.all_gather(part_inputs, "tensor", axis=3, tiled=True),
        lax.all_gather(part_cotangent, "tensor", axis=3, tiled=True),
    )
    inputs = recv_inputs.reshape(held, rows, width)
    cotangent = recv_cotangent.reshape(held, rows, width)
    gate_flat = recv_gates.reshape(held, rows).astype(jnp.float32)
    weights_in_all, weights_out_all = (
        lax.all_gather(w_in, "dp", axis=0, tiled=True),
        lax.all_gather(w_out, "dp", axis=0, tiled=True),
    )
    projected = jnp.einsum(
        "erd,dejh->erjh", inputs, weights_in_all, preferred_element_type=jnp.float32
    )
    back = jnp.einsum(
        "erd,deh->erh", cotangent, weights_out_all, preferred_element_type=jnp.float32
    )
    gate_piece, grad_both, scaled_hidden = expert_math(projected, back, gate_flat[:, :, None])
    token_piece = jnp.einsum(
        "erjh,dejh->erd", grad_both, weights_in_all, preferred_element_type=jnp.float32
    ).astype(jnp.bfloat16)
    term_in = jnp.einsum(
        "erd,erjh->dejh", inputs, grad_both, preferred_element_type=jnp.float32
    ).reshape(w_in.shape[0] * lax.axis_size("dp"), held, 2 * hidden_dev)
    term_out = jnp.einsum(
        "erd,erh->deh", cotangent, scaled_hidden, preferred_element_type=jnp.float32
    )
    summed = lax.psum_scatter(
        jnp.concatenate([term_in, term_out], axis=2).astype(jnp.bfloat16),
        "dp",
        scatter_dimension=0,
        tiled=True,
    ).astype(jnp.float32)
    grad_w_in = (
        summed[:, :, : 2 * hidden_dev]
        .astype(jnp.bfloat16)
        .reshape(w_in.shape[0], held, 2, hidden_dev)
    )
    grad_w_out = summed[:, :, 2 * hidden_dev :].astype(jnp.bfloat16)
    piece_float = (
        lax.optimization_barrier(token_piece)
        .astype(jnp.float32)
        .reshape(held, n_expert, capacity, width)
    )
    gate_float = (
        lax.optimization_barrier(gate_piece).astype(jnp.float32).reshape(held, n_expert, capacity)
    )
    slot_total = lax.psum_scatter(
        piece_float.astype(jnp.bfloat16), "tensor", scatter_dimension=3, tiled=True
    ).astype(jnp.float32)
    gate_total = lax.psum(gate_float, "tensor")
    back_cols, back_gates = (
        lax.all_to_all(
            slot_total.astype(jnp.bfloat16), "expert", split_axis=1, concat_axis=1, tiled=True
        ).astype(slot_total.dtype),
        lax.all_to_all(
            gate_total.astype(jnp.bfloat16), "expert", split_axis=1, concat_axis=1, tiled=True
        ).astype(gate_total.dtype),
    )
    token_cols_all = jnp.einsum(
        "st,sd->td",
        placing.astype(jnp.float32),
        back_cols.reshape(slots, share),
        precision=lax.Precision.HIGHEST,
    ).astype(jnp.bfloat16)
    grad_tokens = lax.all_to_all(token_cols_all, "tensor", split_axis=0, concat_axis=1, tiled=True)
    token_gate = jnp.einsum(
        "stk,s->tk", routed_float, back_gates.reshape(slots), precision=lax.Precision.HIGHEST
    )
    mine_gate = lax.dynamic_slice_in_dim(token_gate, lax.axis_index("tensor") * tok_dev, tok_dev, 0)
    return (grad_tokens, mine_gate, grad_w_in, grad_w_out)


def solution(mesh):
    in_specs = (
        P(("dp", "expert", "tensor"), None),
        P(("dp", "expert", "tensor"), None),
        P(("dp", "expert", "tensor"), None),
        P(("dp", "expert", "tensor"), None),
        P(("dp", "expert", "tensor"), None),
        P("dp", "expert", None, "tensor"),
        P("dp", "expert", "tensor"),
    )
    out_specs = (
        P(("dp", "expert", "tensor"), None),
        P(("dp", "expert", "tensor"), None),
        P("dp", "expert", None, "tensor"),
        P("dp", "expert", "tensor"),
    )
    return jax.shard_map(body, mesh=mesh, in_specs=in_specs, out_specs=out_specs, check_vma=False)
```

profile of v0, /device:TPU:0, one launch (start us, length us, event | category | flops | bytes accessed | tf_op | source)
XLA Modules:
  0.0 297.7 jit_solution(18323101432820074830)
XLA Ops:
  7.2 0.8 mul.97
  8.0 1.0 fusion.28
  9.0 0.7 copy.122
  9.7 4.2 %all-to-all-start.3 = ((bf16[16,2,2560]{2,0,1:T(8,128)(2,1)}), bf16[16,2,2560]{2,0,1:T(8,128)(2,1)S(1)}, u32[]{:S(2)}, u32[]{:S(2)}) async-start(bf16[16,2,2560]{2,0,1:T(8,128)(2,1)} %bitcast.132), calls=%async_computation.3 | async-start | bytes 327680 | tf_op jit(solution)/shard_map/all_to_all | solution.py:62
  13.9 4.9 %all-gather = s32[2,16,6]{1,2,0:T(8,128)S(1)} all-gather(s32[1,16,6]{1,2,0:T(8,128)} %bitcast.144), channel_id=1, replica_groups=mesh['dp'=1,'expert'=16,'tensor'=2] {'tensor'}, dimensions={0}, use_global_device_ids=true | all-gather | bytes 1152 | tf_op jit(solution)/shard_map/all_gather | solution.py:56
  19.0 0.1 eq.38
  19.2 0.6 reduce-window.6
  19.7 0.2 slice_reduce_fusion
  20.1 0.1 reduce_sum.21
  20.3 0.1 fusion.35
  20.4 0.5 convolution_convert_fusion.1
  20.9 1.3 reshape.233
  22.2 6.3 %all-to-all-start.4 = ((bf16[1,16,13,2560]{3,2,0,1:T(8,128)(2,1)}), bf16[1,16,13,2560]{3,2,0,1:T(8,128)(2,1)S(1)}, u32[]{:S(2)}, u32[]{:S(2)}) async-start(bf16[1,16,13,2560]{3,2,0,1:T(8,128)(2,1)} %bitcast.10), calls=%async_computation.4 | async-start | bytes 2621440 | tf_op jit(solution)/shard_map/all_to_all | solution.py:79
  28.5 0.7 copy.123
  29.2 26.7 %all-to-all-done.4 = bf16[1,16,13,2560]{3,2,0,1:T(8,128)(2,1)S(1)} async-done(((bf16[1,16,13,2560]{3,2,0,1:T(8,128)(2,1)}), bf16[1,16,13,2560]{3,2,0,1:T(8,128)(2,1)S(1)}, u32[]{:S(2)}, u32[]{:S(2)}) %all-to-all-start.4) | async-done | bytes 1064992 | tf_op jit(solution)/shard_map/all_to_all | solution.py:79
  55.9 3.4 %all-to-all-start.1 = ((bf16[16,2,2560]{2,0,1:T(8,128)(2,1)}), bf16[16,2,2560]{2,0,1:T(8,128)(2,1)S(1)}, u32[]{:S(2)}, u32[]{:S(2)}) async-start(bf16[16,2,2560]{2,0,1:T(8,128)(2,1)} %bitcast.133), calls=%async_computation.1 | async-start | bytes 327680 | tf_op jit(solution)/shard_map/all_to_all | solution.py:63
  59.4 0.7 all-gather.7.cloned.1.call-update
  60.1 4.5 %all-to-all-done.1 = bf16[16,2,2560]{2,0,1:T(8,128)(2,1)S(1)} async-done(((bf16[16,2,2560]{2,0,1:T(8,128)(2,1)}), bf16[16,2,2560]{2,0,1:T(8,128)(2,1)S(1)}, u32[]{:S(2)}, u32[]{:S(2)}) %all-to-all-start.1) | async-done | bytes 163872 | tf_op jit(solution)/shard_map/all_to_all | solution.py:63
  64.7 0.5 convolution_convert_fusion.2
  65.1 0.4 reshape.230
  65.6 39.0 %all_to_all.82 = bf16[1,16,13,2560]{3,2,0,1:T(8,128)(2,1)} all-to-all(bf16[1,16,13,2560]{3,2,0,1:T(8,128)(2,1)S(1)} %bitcast.134), channel_id=1, replica_groups=mesh['dp'=1,'expert'=16,'tensor'=2] {'expert'}, dimensions={1} | all-to-all | bytes 2129920 | tf_op jit(solution)/shard_map/all_to_all | solution.py:80
  104.6 4.3 %all-gather.1 = bf16[2,16,6]{1,2,0:T(8,128)(2,1)S(1)} all-gather(bf16[1,16,6]{1,2,0:T(8,128)(2,1)S(1)} %bitcast.145), channel_id=1, replica_groups=mesh['dp'=1,'expert'=16,'tensor'=2] {'tensor'}, dimensions={0}, use_global_device_ids=true | all-gather | bytes 576 | tf_op jit(solution)/shard_map/all_gather | solution.py:60
  109.1 0.2 fusion.34
  109.3 0.1 reshape.259
  109.4 10.2 %all_to_all.83 = bf16[1,16,13]{2,0,1:T(2,128)(2,1)S(1)} all-to-all(bf16[1,16,13]{2,0,1:T(2,128)(2,1)S(1)} %reshape.259), channel_id=1, replica_groups=mesh['dp'=1,'expert'=16,'tensor'=2] {'expert'}, dimensions={1} | all-to-all | bytes 832 | tf_op jit(solution)/shard_map/all_to_all | solution.py:81
  119.7 2.1 reshape.253
  121.9 10.4 %fusion.16 = f32[1,208,2,768]{3,1,2,0:T(8,128)S(1)} fusion(bf16[208,5120,1]{1,0,2:T(8,128)(2,1)S(1)} %reshape.253, bf16[5120,2,768]{2,1,0:T(2,128)(2,1)} %bitcast.146), kind=kOutput, calls=%fused_computation.15 | convolution fusion | flops 3271557120 | bytes 19136512 | tf_op jit(solution)/shard_map/erd,dejh->erjh/dot_general | solution.py:100
  132.3 13.6 %all-gather.5.cloned.1.call-done = bf16[1,16,13,5120]{3,2,0,1:T(8,128)(2,1)} async-done(((bf16[1,16,13,2560]{3,2,0,1:T(8,128)(2,1)}), bf16[1,16,13,5120]{3,2,0,1:T(8,128)(2,1)}) %all-gather.5.cloned.1.call-update) | async-done | bytes 2129936 | tf_op jit(solution)/shard_map/all_gather | solution.py:91
  145.8 2.1 reshape.231
  148.0 6.2 %fusion.32 = (bf16[208,1,768]{2,0,1:T(8,128)(2,1)}, bf16[208,1,768]{2,0,1:T(8,128)(2,1)}, bf16[208]{0:T(256)(128)(2,1)S(1)}) fusion(f32[1,208,2,768]{3,1,2,0:T(8,128)S(1)} %fusion.16, f32[208]{0:T(256)S(1)} %reshape.241, bf16[208,5120]{1,0:T(8,128)(2,1)S(1)} %reshape.231, bf16[5120,1,768]{2,0,1:T(8,128)(2,1)} %param.13), kind=kOutput, calls=%fused_computation.38 | convolution fusion | flops 1638493952 | bytes 11912416 | tf_op jit(solution)/shard_map/erd,deh->erh/dot_general | solution.py:103
  154.1 12.2 %fusion.13 = bf16[1,208,5120]{2,1,0:T(8,128)(2,1)} fusion(bf16[5120,2,768]{2,1,0:T(2,128)(2,1)} %bitcast.147, bf16[208,1,768]{2,0,1:T(8,128)(2,1)} %get-tuple-element.29, bf16[208,1,768]{2,0,1:T(8,128)(2,1)} %get-tuple-element.28), kind=kOutput, calls=%fused_computation.11 | convolution fusion | flops 3272941568 | bytes 18497536 | tf_op jit(solution)/shard_map/erjh,dejh->erd/dot_general | solution.py:107
  166.3 3.1 %convert_element_type.120 = bf16[1,16,13,5120]{3,2,1,0:T(8,128)(2,1)} reshape(bf16[1,208,5120]{2,1,0:T(8,128)(2,1)} %fusion.13) | data formatting | bytes 4259840 | tf_op jit(solution)/shard_map/convert_element_type | solution.py:137
  169.5 5.0 %psum.7 = bf16[1,16,13]{2,1,0:T(8,128)(2,1)S(1)} all-reduce(f32[1,16,13]{2,1,0:T(8,128)S(1)} %reshape.243), channel_id=1, replica_groups=mesh['dp'=1,'expert'=16,'tensor'=2] {'tensor'}, use_global_device_ids=true, to_apply=%region_6.7 | all-reduce | flops 208 | bytes 1248 | tf_op jit(solution)/shard_map/psum | solution.py:139
  174.5 11.8 %all_to_all.84 = bf16[1,16,13]{2,0,1:T(2,128)(2,1)S(1)} all-to-all(bf16[1,16,13]{2,0,1:T(2,128)(2,1)S(1)} %copy.94), channel_id=1, replica_groups=mesh['dp'=1,'expert'=16,'tensor'=2] {'expert'}, dimensions={1} | all-to-all | bytes 832 | tf_op jit(solution)/shard_map/all_to_all | solution.py:144
  186.4 20.8 %reduce-scatter.2.cloned.1.call-done = bf16[1,16,13,2560]{3,2,1,0:T(8,128)(2,1)} async-done(((bf16[1,16,13,5120]{3,2,1,0:T(8,128)(2,1)}), bf16[1,16,13,2560]{3,2,1,0:T(8,128)(2,1)}) %reduce-scatter.2.cloned.1.call-update) | async-done | bytes 1064976 | tf_op jit(solution)/shard_map/reduce_scatter | solution.py:136
  207.1 5.6 %all-to-all-start.5 = ((bf16[1,16,13,2560]{3,2,0,1:T(8,128)(2,1)}), bf16[1,16,13,2560]{3,2,0,1:T(8,128)(2,1)S(1)}, u32[]{:S(2)}, u32[]{:S(2)}) async-start(bf16[1,16,13,2560]{3,2,0,1:T(8,128)(2,1)} %bitcast.135), calls=%async_computation.6 | async-start | bytes 2621440 | tf_op jit(solution)/shard_map/all_to_all | solution.py:141
  212.8 11.6 %convert_bitcast_fusion = bf16[5120,1,2,768]{0,3,2,1:T(8,128)(2,1)} fusion(bf16[208,5120,1]{1,0,2:T(8,128)(2,1)} %copy-done, bf16[208,1,768]{2,0,1:T(8,128)(2,1)} %get-tuple-element.29, bf16[208,1,768]{2,0,1:T(8,128)(2,1)} %get-tuple-element.28), kind=kOutput, calls=%fused_computation | convolution fusion | flops 3279740928 | bytes 18497536 | tf_op jit(solution)/shard_map/erd,erjh->dejh/dot_general | solution.py:110
  224.4 38.5 %copy.95 = bf16[5120,1,2,768]{3,2,1,0:T(2,128)(2,1)} copy(bf16[5120,1,2,768]{0,3,2,1:T(8,128)(2,1)} %convert_bitcast_fusion) | data formatting | bytes 31457280
  262.9 6.7 %fusion.6 = bf16[5120,1,768]{0,2,1:T(8,128)(2,1)} fusion(bf16[208,5120]{1,0:T(8,128)(2,1)S(1)} %reshape.231, f32[1,208,2,768]{3,1,2,0:T(8,128)} %copy-done.2, f32[208]{0:T(256)S(1)} %reshape.241), kind=kOutput, calls=%fused_computation.8 | convolution fusion | flops 1640828928 | bytes 11273024 | tf_op jit(solution)/shard_map/erd,erh->deh/dot_general | solution.py:113
  269.6 10.6 %copy.96 = bf16[5120,1,768]{2,0,1:T(8,128)(2,1)} copy(bf16[5120,1,768]{0,2,1:T(8,128)(2,1)} %fusion.6) | data formatting | bytes 15728640
  280.3 0.2 fusion.33
  280.6 0.1 copy.98
  280.7 0.4 reshape.236
  281.1 1.0 convolution_convert_fusion.3
  282.1 3.4 %all-to-all-start.6 = ((bf16[2,16,2560]{2,1,0:T(8,128)(2,1)}), bf16[2,16,2560]{2,1,0:T(8,128)(2,1)S(1)}, u32[]{:S(2)}, u32[]{:S(2)}) async-start(bf16[2,16,2560]{2,1,0:T(8,128)(2,1)} %bitcast.20), calls=%async_computation.7 | async-start | bytes 327680 | tf_op jit(solution)/shard_map/all_to_all | solution.py:154
  285.5 0.7 constant_dynamic-slice_fusion
  286.2 4.3 %all-to-all-done.6 = bf16[2,16,2560]{2,1,0:T(8,128)(2,1)S(1)} async-done(((bf16[2,16,2560]{2,1,0:T(8,128)(2,1)}), bf16[2,16,2560]{2,1,0:T(8,128)(2,1)S(1)}, u32[]{:S(2)}, u32[]{:S(2)}) %all-to-all-start.6) | async-done | bytes 163872 | tf_op jit(solution)/shard_map/all_to_all | solution.py:154
  290.5 0.7 copy.103
  (41 shorter events, 1.1 us)
Async XLA Ops:
  9.7 10.7 %all-to-all-start.3 = ((bf16[16,2,2560]{2,0,1:T(8,128)(2,1)}), bf16[16,2,2560]{2,0,1:T(8,128)(2,1)S(1)}, u32[]{:S(2)}, u32[]{:S(2)}) async-start(bf16[16,2,2560]{2,0,1:T(8,128)(2,1)} %bitcast.132), calls=%async_computation.3 | async-start | bytes 327680 | tf_op jit(solution)/shard_map/all_to_all | solution.py:62
  20.9 7.6 %copy-start.3 = (bf16[16,5120]{1,0:T(8,128)(2,1)S(1)}, bf16[16,5120]{1,0:T(8,128)(2,1)}, u32[]{:S(2)}) copy-start(bf16[16,5120]{1,0:T(8,128)(2,1)} %param.11) | copy-start | bytes 491524
  22.2 33.8 %all-to-all-start.4 = ((bf16[1,16,13,2560]{3,2,0,1:T(8,128)(2,1)}), bf16[1,16,13,2560]{3,2,0,1:T(8,128)(2,1)S(1)}, u32[]{:S(2)}, u32[]{:S(2)}) async-start(bf16[1,16,13,2560]{3,2,0,1:T(8,128)(2,1)} %bitcast.10), calls=%async_computation.4 | async-start | bytes 2621440 | tf_op jit(solution)/shard_map/all_to_all | solution.py:79
  55.9 3.5 %copy-start.1 = (bf16[1,16,13,2560]{3,2,0,1:T(8,128)(2,1)}, bf16[1,16,13,2560]{3,2,0,1:T(8,128)(2,1)S(1)}, u32[]{:S(2)}) copy-start(bf16[1,16,13,2560]{3,2,0,1:T(8,128)(2,1)S(1)} %all-to-all-done.4) | copy-start | bytes 3194884
  55.9 8.7 %all-to-all-start.1 = ((bf16[16,2,2560]{2,0,1:T(8,128)(2,1)}), bf16[16,2,2560]{2,0,1:T(8,128)(2,1)S(1)}, u32[]{:S(2)}, u32[]{:S(2)}) async-start(bf16[16,2,2560]{2,0,1:T(8,128)(2,1)} %bitcast.133), calls=%async_computation.1 | async-start | bytes 327680 | tf_op jit(solution)/shard_map/all_to_all | solution.py:63
  59.4 60.4 %all-gather.7.cloned.1.call-start = ((), (), s32[]{:S(2)}) async-start(), calls=%async_computation.10 | async-start | bytes 3932160 | tf_op jit(solution)/shard_map/all_gather | solution.py:90
  60.1 85.7 %all-gather.5.cloned.1.call-start = ((), (), s32[]{:S(2)}) async-start(), calls=%async_computation.9 | async-start | bytes 3932160 | tf_op jit(solution)/shard_map/all_gather | solution.py:91
  65.6 39.0 %copy-start.4 = (bf16[16,6]{0,1:T(8,128)(2,1)S(1)}, bf16[16,6]{0,1:T(8,128)(2,1)}, u32[]{:S(2)}) copy-start(bf16[16,6]{0,1:T(8,128)(2,1)} %param.10) | copy-start | bytes 580
  104.6 102.6 %reduce-scatter.2.cloned.1.call-start = ((), (), s32[]{:S(2)}) async-start(), calls=%async_computation.11 | async-start | bytes 3932160 | tf_op jit(solution)/shard_map/reduce_scatter | solution.py:136
  121.8 10.4 %copy-start = (bf16[208,5120,1]{1,0,2:T(8,128)(2,1)}, bf16[208,5120,1]{1,0,2:T(8,128)(2,1)S(1)}, u32[]{:S(2)}) copy-start(bf16[208,5120,1]{1,0,2:T(8,128)(2,1)S(1)} %reshape.253) | copy-start | bytes 6389764
  132.2 15.7 %copy-start.2 = (f32[1,208,2,768]{3,1,2,0:T(8,128)}, f32[1,208,2,768]{3,1,2,0:T(8,128)S(1)}, u32[]{:S(2)}) copy-start(f32[1,208,2,768]{3,1,2,0:T(8,128)S(1)} %fusion.16) | copy-start | bytes 3833860
  207.1 73.6 %all-to-all-start.5 = ((bf16[1,16,13,2560]{3,2,0,1:T(8,128)(2,1)}), bf16[1,16,13,2560]{3,2,0,1:T(8,128)(2,1)S(1)}, u32[]{:S(2)}, u32[]{:S(2)}) async-start(bf16[1,16,13,2560]{3,2,0,1:T(8,128)(2,1)} %bitcast.135), calls=%async_computation.6 | async-start | bytes 2621440 | tf_op jit(solution)/shard_map/all_to_all | solution.py:141
  282.1 8.4 %all-to-all-start.6 = ((bf16[2,16,2560]{2,1,0:T(8,128)(2,1)}), bf16[2,16,2560]{2,1,0:T(8,128)(2,1)S(1)}, u32[]{:S(2)}, u32[]{:S(2)}) async-start(bf16[2,16,2560]{2,1,0:T(8,128)(2,1)} %bitcast.20), calls=%async_computation.7 | async-start | bytes 327680 | tf_op jit(solution)/shard_map/all_to_all | solution.py:154
Sparse Core Ops, SparseCore 0:
  62.3 42.8 all-gather.6
  106.7 39.0 all-gather.4
  169.5 37.5 reduce-scatter.1
where the time goes:
time: 300 us; the launch traced here: 298 us
  blocking collectives  75.3 us (25%)
  waiting for transfers between devices  70.6 us (24%)
  local copies, waits for them, and re-layouts  63.3 us (21%)
  matrix products  49.3 us (16%)
  starting transfers between devices  23.2 us (8%)
  between operations  14 us (5%)
    unnamed x13, local copies, waits for them, and re-layouts  49.2 us
    all_to_all x1, blocking collectives, body(): lax.all_to_all(slot_cotangent, 'expert', split_axis=1, concat_axis=1, til...  39 us
    all_to_all x1, waiting for transfers between devices, body(): lax.all_to_all(slot_inputs, 'expert', split_axis=1, concat_axis=1, tiled=...  26.7 us
    reduce_scatter x1, waiting for transfers between devices, body(): lax.psum_scatter(piece_float.astype(jnp.bfloat16), 'tensor', scatter_dime...  20.8 us
    all_gather x1, waiting for transfers between devices, body(): lax.all_gather(part_cotangent, 'tensor', axis=3, tiled=True)  13.6 us
    dot_general x1, matrix products, body(): jnp.einsum('erjh,dejh->erd', grad_both, weights_in_all, preferred_element...  12.2 us
    all_to_all x1, blocking collectives, body(): lax.all_to_all(gate_total.astype(jnp.bfloat16), 'expert', split_axis=1, c...  11.8 us
    dot_general x1, matrix products, body(): jnp.einsum('erd,erjh->dejh', inputs, grad_both, preferred_element_type=jn...  11.6 us
  transfers between devices with their start and end apart: 8, of which 5 were waited for; matrix products, arithmetic and copies ran while one was open for 28% of the time, Pallas kernels for 0%

commit v1 on v0

--- a/solution.py
+++ b/solution.py
@@ -1,7 +1,11 @@
 import jax
 import jax.numpy as jnp
 from jax import lax
+from jax.experimental import pallas as pl
+from jax.experimental.pallas import tpu as pltpu
 from jax.sharding import PartitionSpec as P
+
+LANES = 128
 
 
 def slot_table(routes_all, experts, n_expert, capacity):
@@ -31,7 +35,7 @@
     return (gate_piece, grad_both, scaled_hidden)
 
 
-def body(quant_tokens, token_scales, expert_ids, gate_weights, grad_out, w_in, w_out):
+def routed_body(quant_tokens, token_scales, expert_ids, gate_weights, grad_out, w_in, w_out):
     tok_dev, width = quant_tokens.shape
     blocks = token_scales.shape[1]
     top = expert_ids.shape[1]
@@ -159,6 +163,239 @@
     return (grad_tokens, mine_gate, grad_w_in, grad_w_out)
 
 
+def swap(array, stage):
+    axis, bit = stage
+    size = lax.axis_size(axis)
+    return lax.ppermute(array, axis, [(i, i ^ bit) for i in range(size)])
+
+
+def doubling_gather(rows, order):
+    for stage in order:
+        rows = jnp.concatenate([rows, swap(rows, stage)], axis=0)
+    return rows
+
+
+def halving_sum(total, order):
+    for stage in order:
+        half = total.shape[0] // 2
+        sent = swap(total[half:].astype(jnp.bfloat16), stage)
+        total = total[:half] + sent.astype(jnp.float32)
+    return total
+
+
+def order_matrix(order, base, tok_dev):
+    count = tok_dev << len(order)
+    position = lax.broadcasted_iota(jnp.int32, (count, count), 1)
+    block, offset = position // tok_dev, position % tok_dev
+    target = jnp.zeros_like(block)
+    for place, stage in enumerate(order):
+        target = target + ((block >> place) & 1) * (1 << base.index(stage))
+    source = lax.broadcasted_iota(jnp.int32, (count, count), 0)
+    return (source == target * tok_dev + offset).astype(jnp.bfloat16)
+
+
+def weight_grad_kernel(inputs, cotangent, gate_grad, up_grad, scaled, *rest):
+    grad_in, grad_out = rest[-2:]
+    contract = (((0,), (0,)), ((), ()))
+    x, g = inputs[...], cotangent[...]
+    grad_in[:, 0, :] = lax.dot_general(
+        x, gate_grad[...], contract, preferred_element_type=jnp.float32
+    ).astype(jnp.bfloat16)
+    grad_in[:, 1, :] = lax.dot_general(
+        x, up_grad[...], contract, preferred_element_type=jnp.float32
+    ).astype(jnp.bfloat16)
+    grad_out[...] = lax.dot_general(
+        g, scaled[...], contract, preferred_element_type=jnp.float32
+    ).astype(jnp.bfloat16)
+
+
+def weight_grads(inputs, cotangent, gate_grad, up_grad, scaled, start, width, so_far):
+    rows, columns = inputs.shape
+    hidden = gate_grad.shape[1]
+    tile = 512 if columns % 512 == 0 else columns
+    first = start // tile
+    resident = pl.BlockSpec((rows, hidden), lambda i: (0, 0))
+    stream = pl.BlockSpec((rows, tile), lambda i: (0, i))
+    kept = [pl.BlockSpec(memory_space=pl.ANY)] * len(so_far)
+    return pl.pallas_call(
+        weight_grad_kernel,
+        grid=(columns // tile,),
+        in_specs=[stream, stream, resident, resident, resident] + kept,
+        out_specs=[
+            pl.BlockSpec((tile, 2, hidden), lambda i: (first + i, 0, 0)),
+            pl.BlockSpec((tile, hidden), lambda i: (first + i, 0)),
+        ],
+        out_shape=[
+            jax.ShapeDtypeStruct((width, 2, hidden), jnp.bfloat16),
+            jax.ShapeDtypeStruct((width, hidden), jnp.bfloat16),
+        ],
+        input_output_aliases={5: 0, 6: 1} if so_far else {},
+        compiler_params=pltpu.CompilerParams(vmem_limit_bytes=24 << 20),
+        cost_estimate=pl.CostEstimate(
+            flops=6 * rows * columns * hidden,
+            bytes_accessed=6 * columns * hidden + 4 * rows * columns,
+            transcendentals=0,
+        ),
+    )(inputs, cotangent, gate_grad, up_grad, scaled, *so_far)
+
+
+def gathered_body(quant_tokens, token_scales, expert_ids, gate_weights, grad_out, w_in, w_out):
+    tok_dev, width = quant_tokens.shape
+    blocks = token_scales.shape[1]
+    top = expert_ids.shape[1]
+    n_tensor = lax.axis_size("tensor")
+    n_expert = lax.axis_size("expert")
+    tokens = tok_dev * n_tensor * n_expert
+    capacity = max(2, tok_dev * n_tensor * top * 13 // (12 * n_expert))
+    slots = n_expert * capacity
+    hidden = w_out.shape[2]
+    expert = lax.axis_index("expert")
+
+    core, across = [("expert", 1)], [("expert", 2)]
+    along = [("expert", 1 << k) for k in range(2, n_expert.bit_length() - 1)][::-1]
+    side = [("tensor", 1 << k) for k in range(n_tensor.bit_length() - 1)]
+    orders = [
+        side + along + across + core,
+        along + across + side + core,
+        along + side + across + core,
+        along + across + side + core,
+        across + side + along + core,
+    ]
+    base = orders[0]
+    chunk = width // len(orders)
+
+    scaled = (
+        (
+            quant_tokens.astype(jnp.float32).reshape(tok_dev, blocks, width // blocks)
+            * token_scales[:, :, None]
+        )
+        .reshape(tok_dev, width)
+        .astype(jnp.bfloat16)
+    )
+    routes = jnp.concatenate([expert_ids.astype(jnp.bfloat16), gate_weights], axis=1)
+    routes = jnp.pad(routes, ((0, 0), (0, LANES - 2 * top)))
+
+    gathered = []
+    for index, order in enumerate(orders):
+        lo, hi = index * chunk, (index + 1) * chunk
+        parts = [scaled[:, lo:hi], grad_out[:, lo:hi]] + ([routes] if index == 0 else [])
+        gathered.append(doubling_gather(jnp.concatenate(parts, axis=1), order))
+
+    routes_all = gathered[0][:, 2 * chunk :].astype(jnp.float32)
+    lane = lax.broadcasted_iota(jnp.int32, routes_all.shape, 1)
+    named = (routes_all == expert.astype(jnp.float32)) & (lane < top)
+    chosen = jnp.any(named, axis=1, keepdims=True)
+    gate_lanes = jnp.pad(routes_all[:, top:], ((0, 0), (0, top)))
+    token_gate = jnp.sum(jnp.where(named, gate_lanes, 0.0), axis=1, keepdims=True)
+    earlier = lax.broadcasted_iota(jnp.int32, (tokens, tokens), 0)
+    later = lax.broadcasted_iota(jnp.int32, (tokens, tokens), 1)
+    far = 2 * tokens
+    ranking = jnp.where(earlier == later, -far, (earlier < later).astype(jnp.int32))
+    rank = far + lax.dot_general(
+        chosen.astype(jnp.bfloat16),
+        ranking.astype(jnp.bfloat16),
+        (((0,), (0,)), ((), ())),
+        preferred_element_type=jnp.float32,
+    )
+    slot = lax.broadcasted_iota(jnp.int32, (slots, tokens), 0).astype(jnp.float32)
+    placing = (slot == rank).astype(jnp.bfloat16)
+    slot_gates = jnp.dot(
+        placing, token_gate.astype(jnp.bfloat16), preferred_element_type=jnp.float32
+    )
+    placings = {}
+    for order in orders:
+        key = tuple(order)
+        if key not in placings:
+            placings[key] = (
+                placing
+                if order == base
+                else jnp.dot(
+                    placing,
+                    order_matrix(order, base, tok_dev),
+                    preferred_element_type=jnp.float32,
+                ).astype(jnp.bfloat16)
+            )
+
+    gate_pre = up_value = back = None
+    inputs, cotangents = [], []
+    for index, order in enumerate(orders):
+        lo, hi = index * chunk, (index + 1) * chunk
+        picked = jnp.dot(
+            placings[tuple(order)],
+            gathered[index][:, : 2 * chunk],
+            preferred_element_type=jnp.float32,
+        ).astype(jnp.bfloat16)
+        x, g = picked[:, :chunk], picked[:, chunk:]
+        inputs.append(x)
+        cotangents.append(g)
+        part = jnp.einsum("rd,djh->rjh", x, w_in[lo:hi, 0], preferred_element_type=jnp.float32)
+        back_part = jnp.dot(g, w_out[lo:hi, 0], preferred_element_type=jnp.float32)
+        projected = part if index == 0 else projected + part
+        back = back_part if index == 0 else back + back_part
+    gate_pre, up_value = projected[:, 0], projected[:, 1]
+    sigmoid_gate = jax.nn.sigmoid(gate_pre)
+    activated = gate_pre * sigmoid_gate
+    hidden_value = activated * up_value
+    gate_piece = jnp.sum(hidden_value * back, axis=1, keepdims=True).astype(jnp.bfloat16)
+    grad_hidden = slot_gates * back
+    gate_grad = (
+        grad_hidden * up_value * sigmoid_gate * (1.0 + gate_pre * (1.0 - sigmoid_gate))
+    ).astype(jnp.bfloat16)
+    up_grad = (grad_hidden * activated).astype(jnp.bfloat16)
+    scaled_hidden = (slot_gates * hidden_value).astype(jnp.bfloat16)
+    grad_both = jnp.stack([gate_grad, up_grad], axis=1)
+
+    summed = []
+    transposed = (((0,), (0,)), ((), ()))
+    for index, order in enumerate(orders):
+        lo, hi = index * chunk, (index + 1) * chunk
+        piece = jnp.einsum(
+            "rjh,djh->rd", grad_both, w_in[lo:hi, 0], preferred_element_type=jnp.float32
+        ).astype(jnp.bfloat16)
+        total = lax.dot_general(
+            placings[tuple(order)], piece, transposed, preferred_element_type=jnp.float32
+        )
+        if index == 0:
+            token_piece = lax.dot_general(
+                placing, gate_piece, transposed, preferred_element_type=jnp.float32
+            )
+            total = jnp.concatenate([total, jnp.where(named, token_piece, 0.0)], axis=1)
+        summed.append(halving_sum(total, order[::-1]))
+    grad_gates = summed[0][:, chunk : chunk + top]
+    summed[0] = summed[0][:, :chunk]
+    grad_tokens = jnp.concatenate([s.astype(jnp.bfloat16) for s in summed], axis=1)
+
+    grads = ()
+    for index in range(len(orders)):
+        grads = weight_grads(
+            inputs[index],
+            cotangents[index],
+            gate_grad,
+            up_grad,
+            scaled_hidden,
+            index * chunk,
+            width,
+            grads,
+        )
+    return (
+        grad_tokens,
+        grad_gates,
+        grads[0].reshape(width, 1, 2, hidden),
+        grads[1].reshape(width, 1, hidden),
+    )
+
+
+def body(*arrays):
+    quant_tokens, w_in = arrays[0], arrays[5]
+    sizes = [lax.axis_size(name) for name in ("expert", "tensor")]
+    whole = lax.axis_size("dp") == 1 and w_in.shape[1] == 1
+    doubling = all(size & (size - 1) == 0 for size in sizes) and sizes[0] >= 4
+    few = quant_tokens.shape[0] * sizes[0] * sizes[1] <= 1024
+    tiled = quant_tokens.shape[1] % (5 * 512) == 0
+    chosen = gathered_body if whole and doubling and few and tiled else routed_body
+    return chosen(*arrays)
+
+
 def solution(mesh):
     in_specs = (
         P(("dp", "expert", "tensor"), None),

time: 300 us -> 204 us (0.68)
  blocking collectives: 75.3 us -> 0 us
  starting transfers between devices: 23.2 us -> 47.2 us
  local copies, waits for them, and re-layouts: 63.3 us -> 40.4 us
  waiting for transfers between devices: 70.6 us -> 50 us
  Pallas kernels: 0 us -> 18.5 us
  between operations: 14 us -> 2 us
  matrix products: 49.3 us -> 37.8 us
  other arithmetic: 1.93 us -> 7.5 us
    all_to_all x3 -> x0, blocking collectives: 61 us -> none  [the longest x1 39 us: body(): lax.all_to_all(slot_cotangent, 'expert', split_axis=1, concat_axis=1, til...]
    ppermute x0 -> x50, waiting for transfers between devices: none -> 50 us  [swap(): return lax.ppermute(array, axis, [(i, i ^ bit) for i in range(size)])]
    ppermute x0 -> x50, starting transfers between devices: none -> 47.2 us  [swap(): return lax.ppermute(array, axis, [(i, i ^ bit) for i in range(size)])]
    all_to_all x5 -> x0, waiting for transfers between devices: 35.6 us -> none  [the longest x1 26.7 us: body(): lax.all_to_all(slot_inputs, 'expert', split_axis=1, concat_axis=1, tiled=...]
    unnamed x13 -> x100, local copies, waits for them, and re-layouts: 49.2 us -> 15 us
    slice x1 -> x33, local copies, waits for them, and re-layouts: 0.18 us -> 23.5 us  [the longest x1 16.9 us: gathered_body(): w_in[lo:hi, 0]]
    all_to_all x5 -> x0, starting transfers between devices: 23.1 us -> none  [the longest x1 6.34 us: body(): lax.all_to_all(slot_inputs, 'expert', split_axis=1, concat_axis=1, tiled=...]
    reduce_scatter x1 -> x0, waiting for transfers between devices: 20.8 us -> none  [body(): lax.psum_scatter(piece_float.astype(jnp.bfloat16), 'tensor', scatter_dime...]
  transfers between devices with their start and end apart: 8 -> 50, of which waited for: 5 -> 20; matrix products, arithmetic and copies ran while one was open for 28% -> 12% of each run, Pallas kernels for 0% -> 9%
where the time goes in v1:
time: 204 us
  waiting for transfers between devices  50 us (25%)
  starting transfers between devices  47.2 us (23%)
  local copies, waits for them, and re-layouts  40.4 us (20%)
  matrix products  37.8 us (19%)
  Pallas kernels  18.5 us (9%)
  other arithmetic  7.5 us (4%)
    ppermute x50, waiting for transfers between devices, swap(): return lax.ppermute(array, axis, [(i, i ^ bit) for i in range(size)])  50 us
    ppermute x50, starting transfers between devices, swap(): return lax.ppermute(array, axis, [(i, i ^ bit) for i in range(size)])  47.2 us
    dot_general x5, matrix products, gathered_body(): lax.dot_general(placings[tuple(order)], piece, transposed, preferred_elem...  24 us
    pallas_call x5, Pallas kernels, weight_grads(): pl.pallas_call(weight_grad_kernel, grid=(columns // tile,), in_specs=[str...  18.5 us
    slice x1, local copies, waits for them, and re-layouts, gathered_body(): w_in[lo:hi, 0]  16.9 us
    unnamed x100, local copies, waits for them, and re-layouts  15 us
    dot_general x5, matrix products, gathered_body(): jnp.dot(placings[tuple(order)], gathered[index][:, :2 * chunk], preferred...  4.71 us
    slice x24, local copies, waits for them, and re-layouts, halving_sum(): sent = swap(total[half:].astype(jnp.bfloat16), stage)  4.5 us
  transfers between devices with their start and end apart: 50, of which 20 were waited for; matrix products, arithmetic and copies ran while one was open for 12% of the time, Pallas kernels for 9%

profile of v1, /device:TPU:0, one launch (start us, length us, event | category | flops | bytes accessed | tf_op | source)
XLA Modules:
  0.0 203.6 jit_solution(8446454721337844810)
XLA Ops:
  4.0 2.9 %collective-permute-start.20 = (bf16[16,2048]{1,0:T(8,128)(2,1)S(1)}, bf16[16,2048]{1,0:T(8,128)(2,1)S(1)}, u32[]{:S(2)}, u32[]{:S(2)}) collective-permute-start(bf16[16,2048]{1,0:T(8,128)(2,1)S(1)} %get-tuple-element.102), channel_id=1, source_target_pairs={{0,4},{2,6},{4,0},{6,2},{8,12},{10,14},{12,8},{14,10},{16,20},{18,... | collective-permute-start | bytes 196616 | tf_op jit(solution)/shard_map/ppermute | solution.py:169
  7.6 2.6 %collective-permute-start.15 = (bf16[16,2048]{1,0:T(8,128)(2,1)S(1)}, bf16[16,2048]{1,0:T(8,128)(2,1)S(1)}, u32[]{:S(2)}, u32[]{:S(2)}) collective-permute-start(bf16[16,2048]{1,0:T(8,128)(2,1)S(1)} %get-tuple-element.107), channel_id=1, source_target_pairs={{0,16},{2,18},{4,20},{6,22},{8,24},{10,26},{12,28},{14,30},{16,0},... | collective-permute-start | bytes 196616 | tf_op jit(solution)/shard_map/ppermute | solution.py:169
  11.8 2.6 %collective-permute-start.5 = (bf16[16,2048]{1,0:T(8,128)(2,1)S(1)}, bf16[16,2048]{1,0:T(8,128)(2,1)S(1)}, u32[]{:S(2)}, u32[]{:S(2)}) collective-permute-start(bf16[16,2048]{1,0:T(8,128)(2,1)S(1)} %get-tuple-element.117), channel_id=1, source_target_pairs={{0,16},{2,18},{4,20},{6,22},{8,24},{10,26},{12,28},{14,30},{16,0},... | collective-permute-start | bytes 196616 | tf_op jit(solution)/shard_map/ppermute | solution.py:169
  15.2 1.5 collective-permute-start
  16.8 16.9 %fusion.208 = (bf16[1024,1,2,768]{3,2,1,0:T(2,128)(2,1)}, bf16[1024,1,2,768]{3,2,1,0:T(2,128)(2,1)}, bf16[1024,1,2,768]{3,2,1,0:T(2,128)(2,1)}, bf16[1024,1,2,768]{3,2,1,0:T(2,128)(2,1)}, bf16[1024,1,2,768]{3,2,1,0:T(2,128)(2,1)}) fusion(bf16[5120,1,2,768]{3,2,1,0:T(2,128)(2,1)} %param.12), kind=kLoop, calls=%fused_computation.372 | loop fusion | bytes 31457280 | tf_op jit(solution)/shard_map/slice | solution.py:331
  34.3 1.6 collective-permute-start.16
  36.5 1.6 collective-permute-start.6
  38.8 2.6 %collective-permute-start.22 = (bf16[64,2048]{1,0:T(8,128)(2,1)S(1)}, bf16[64,2048]{1,0:T(8,128)(2,1)S(1)}, u32[]{:S(2)}, u32[]{:S(2)}) collective-permute-start(bf16[64,2048]{1,0:T(8,128)(2,1)S(1)} %pad_maximum_fusion.11), channel_id=1, source_target_pairs={{0,16},{2,18},{4,20},{6,22},{8,24},{10,26},{12,28},{14,30},{16,0},... | collective-permute-start | bytes 786440 | tf_op jit(solution)/shard_map/ppermute | solution.py:169
  41.5 2.0 %collective-permute-done.16 = bf16[32,2048]{1,0:T(8,128)(2,1)S(1)} collective-permute-done((bf16[32,2048]{1,0:T(8,128)(2,1)S(1)}, bf16[32,2048]{1,0:T(8,128)(2,1)S(1)}, u32[]{:S(2)}, u32[]{:S(2)}) %collective-permute-start.16) | collective-permute-done | bytes 131104 | tf_op jit(solution)/shard_map/ppermute | solution.py:169
  44.4 1.9 collective-permute-done.11
  46.4 1.6 collective-permute-start.12
  48.8 3.0 %collective-permute-done.1 = bf16[32,2176]{1,0:T(8,128)(2,1)S(1)} collective-permute-done((bf16[32,2176]{1,0:T(8,128)(2,1)S(1)}, bf16[32,2176]{1,0:T(8,128)(2,1)S(1)}, u32[]{:S(2)}, u32[]{:S(2)}) %collective-permute-start.1) | collective-permute-done | bytes 139296 | tf_op jit(solution)/shard_map/ppermute | solution.py:169
  51.9 4.7 %collective-permute-done.22 = bf16[64,2048]{1,0:T(8,128)(2,1)S(1)} collective-permute-done((bf16[64,2048]{1,0:T(8,128)(2,1)S(1)}, bf16[64,2048]{1,0:T(8,128)(2,1)S(1)}, u32[]{:S(2)}, u32[]{:S(2)}) %collective-permute-start.22) | collective-permute-done | bytes 262176 | tf_op jit(solution)/shard_map/ppermute | solution.py:169
  56.7 1.6 collective-permute-start.18
  59.7 2.7 %collective-permute-done.2 = bf16[64,2176]{1,0:T(8,128)(2,1)S(1)} collective-permute-done((bf16[64,2176]{1,0:T(8,128)(2,1)S(1)}, bf16[64,2176]{1,0:T(8,128)(2,1)S(1)}, u32[]{:S(2)}, u32[]{:S(2)}) %collective-permute-start.2) | collective-permute-done | bytes 278560 | tf_op jit(solution)/shard_map/ppermute | solution.py:169
  63.2 7.5 %collective-permute-done.23 = bf16[128,2048]{1,0:T(8,128)(2,1)S(1)} collective-permute-done((bf16[128,2048]{1,0:T(8,128)(2,1)S(1)}, bf16[128,2048]{1,0:T(8,128)(2,1)S(1)}, u32[]{:S(2)}, u32[]{:S(2)}) %collective-permute-start.23) | collective-permute-done | bytes 524320 | tf_op jit(solution)/shard_map/ppermute | solution.py:169
  71.9 1.4 collective-permute-done.13
  73.5 5.0 %collective-permute-done.8 = bf16[128,2048]{1,0:T(8,128)(2,1)S(1)} collective-permute-done((bf16[128,2048]{1,0:T(8,128)(2,1)S(1)}, bf16[128,2048]{1,0:T(8,128)(2,1)S(1)}, u32[]{:S(2)}, u32[]{:S(2)}) %collective-permute-start.8) | collective-permute-done | bytes 524320 | tf_op jit(solution)/shard_map/ppermute | solution.py:169
  78.7 1.9 collective-permute-done.3
  85.5 2.2 %convolution_convert_fusion.4 = bf16[208,2048]{1,0:T(8,128)(2,1)S(1)} fusion(bf16[512,2176]{1,0:T(8,128)(2,1)} %copy-done.30, f32[512]{0:T(512)S(1)} %broadcast_add_fusion.1, f32[208]{0:T(256)S(1)} %iota_convert_fusion), kind=kOutput, calls=%fused_computation.24 | convolution fusion | flops 436740096 | bytes 2952000 | tf_op jit(solution)/shard_map/dot_general | solution.py:323
  89.2 1.7 copy-done.14
  92.3 1.5 slice-done.1
  101.7 1.4 copy-done.3
  110.6 4.9 %fusion.52 = f32[512,1024]{1,0:T(8,128)} fusion(bf16[208,512]{1,0:T(8,128)(2,1)} %copy-done.28, bf16[1024,1,2,768]{3,2,1,0:T(2,128)(2,1)} %get-tuple-element.36, bf16[208,1,768]{2,0,1:T(8,128)(2,1)S(1)} %bitcast.184, bf16[208,1,768]{2,0,1:T(8,128)(2,1)S(1)} %bitcast.179), kind=kOutput, calls=%fused_computation.66 | convolution fusion | flops 872947712 | bytes 6094848 | tf_op jit(solution)/shard_map/dot_general | solution.py:355
  115.5 4.8 %fusion.56 = f32[512,1024]{1,0:T(8,128)} fusion(bf16[208,512]{1,0:T(8,128)(2,1)} %copy-done.27, bf16[1024,1,2,768]{3,2,1,0:T(2,128)(2,1)} %get-tuple-element.34, bf16[208,1,768]{2,0,1:T(8,128)(2,1)S(1)} %bitcast.185, bf16[208,1,768]{2,0,1:T(8,128)(2,1)S(1)} %bitcast.180), kind=kOutput, calls=%fused_computation.70 | convolution fusion | flops 872947712 | bytes 6094848 | tf_op jit(solution)/shard_map/dot_general | solution.py:355
  120.3 4.9 %fusion.50 = f32[512,1024]{1,0:T(8,128)} fusion(bf16[208,512]{1,0:T(8,128)(2,1)} %copy-done.25, bf16[1024,1,2,768]{3,2,1,0:T(2,128)(2,1)} %get-tuple-element.37, bf16[208,1,768]{2,0,1:T(8,128)(2,1)S(1)} %bitcast.186, bf16[208,1,768]{2,0,1:T(8,128)(2,1)S(1)} %bitcast.181), kind=kOutput, calls=%fused_computation.64 | convolution fusion | flops 872947712 | bytes 6094848 | tf_op jit(solution)/shard_map/dot_general | solution.py:355
  125.1 4.8 %fusion.54 = f32[512,1024]{1,0:T(8,128)} fusion(bf16[208,512]{1,0:T(8,128)(2,1)} %copy-done.25, bf16[1024,1,2,768]{3,2,1,0:T(2,128)(2,1)} %get-tuple-element.35, bf16[208,1,768]{2,0,1:T(8,128)(2,1)S(1)} %bitcast.187, bf16[208,1,768]{2,0,1:T(8,128)(2,1)S(1)} %bitcast.182), kind=kOutput, calls=%fused_computation.68 | convolution fusion | flops 872947712 | bytes 6094848 | tf_op jit(solution)/shard_map/dot_general | solution.py:355
  130.0 4.7 %fusion.48 = f32[512,1024]{1,0:T(8,128)} fusion(bf16[1024,1,2,768]{3,2,1,0:T(2,128)(2,1)} %get-tuple-element.38, f32[512]{0:T(512)S(1)} %broadcast_add_fusion.1, f32[208]{0:T(256)S(1)} %iota_convert_fusion, bf16[208,1,768]{2,0,1:T(8,128)(2,1)S(1)} %bitcast.188, bf16[208,1,768]{2,0,1:T(8,128)(2,1)S(1)} %bitcast.183), kind=kOutput, calls=%fused_computation.62 | convolution fusion | flops 873054208 | bytes 5884736 | tf_op jit(solution)/shard_map/dot_general | solution.py:355
  136.0 1.4 slice.610
  138.8 1.4 slice.611
  141.8 3.7 %shard_map.102 = (bf16[5120,2,768]{2,1,0:T(2,128)(2,1)}, bf16[5120,768]{1,0:T(8,128)(2,1)}) custom-call(bf16[208,1024]{1,0:T(8,128)(2,1)S(1)} %copy-done.1, bf16[208,1024]{1,0:T(8,128)(2,1)S(1)} %copy-done, bf16[208,768]{1,0:T(8,128)(2,1)S(1)} %get-tuple-element.39.gate_grad, bf16[208,768]{1,0:T(8,128)(2,1)S(1)} %get-tuple-element.40.up_grad, ...), custom_call_target="tpu_custom_call" | custom-call | flops 981467136 | bytes 5570560 | tf_op jit(solution)/shard_map/pallas_call | solution.py:220
  145.5 3.7 %shard_map.103 = (bf16[5120,2,768]{2,1,0:T(2,128)(2,1)}, bf16[5120,768]{1,0:T(8,128)(2,1)}) custom-call(bf16[208,1024]{1,0:T(8,128)(2,1)S(1)} %get-tuple-element.46.inputs, bf16[208,1024]{1,0:T(8,128)(2,1)S(1)} %get-tuple-element.45.cotangent, bf16[208,768]{1,0:T(8,128)(2,1)S(1)} %get-tuple-element.39.gate_grad, ...), custom_call_target="tpu_custom_call", output_to_operand_aliasing={{0}: (5, {}), {1}: (6, {})} | custom-call | flops 981467136 | bytes 5570560 | tf_op jit(solution)/shard_map/pallas_call | solution.py:220
  149.3 3.7 %shard_map.104 = (bf16[5120,2,768]{2,1,0:T(2,128)(2,1)}, bf16[5120,768]{1,0:T(8,128)(2,1)}) custom-call(bf16[208,1024]{1,0:T(8,128)(2,1)S(1)} %get-tuple-element.48.inputs, bf16[208,1024]{1,0:T(8,128)(2,1)S(1)} %get-tuple-element.47.cotangent, bf16[208,768]{1,0:T(8,128)(2,1)S(1)} %get-tuple-element.39.gate_grad, ...), custom_call_target="tpu_custom_call", output_to_operand_aliasing={{0}: (5, {}), {1}: (6, {})} | custom-call | flops 981467136 | bytes 5570560 | tf_op jit(solution)/shard_map/pallas_call | solution.py:220
  153.0 3.7 %shard_map.105 = (bf16[5120,2,768]{2,1,0:T(2,128)(2,1)}, bf16[5120,768]{1,0:T(8,128)(2,1)}) custom-call(bf16[208,1024]{1,0:T(8,128)(2,1)S(1)} %get-tuple-element.50.inputs, bf16[208,1024]{1,0:T(8,128)(2,1)S(1)} %get-tuple-element.49.cotangent, bf16[208,768]{1,0:T(8,128)(2,1)S(1)} %get-tuple-element.39.gate_grad, ...), custom_call_target="tpu_custom_call", output_to_operand_aliasing={{0}: (5, {}), {1}: (6, {})} | custom-call | flops 981467136 | bytes 5570560 | tf_op jit(solution)/shard_map/pallas_call | solution.py:220
  156.7 3.7 %shard_map.106 = (bf16[5120,2,768]{2,1,0:T(2,128)(2,1)}, bf16[5120,768]{1,0:T(8,128)(2,1)}) custom-call(bf16[208,1024]{1,0:T(8,128)(2,1)S(1)} %get-tuple-element.52.inputs, bf16[208,1024]{1,0:T(8,128)(2,1)S(1)} %get-tuple-element.51.cotangent, bf16[208,768]{1,0:T(8,128)(2,1)S(1)} %get-tuple-element.39.gate_grad, ...), custom_call_target="tpu_custom_call", output_to_operand_aliasing={{0}: (5, {}), {1}: (6, {})} | custom-call | flops 981467136 | bytes 5570560 | tf_op jit(solution)/shard_map/pallas_call | solution.py:220
  162.2 1.8 collective-permute-start.46
  165.2 1.4 collective-permute-start.41
  167.6 2.1 %collective-permute-done.36 = bf16[128,1024]{1,0:T(8,128)(2,1)S(1)} collective-permute-done((bf16[128,1024]{1,0:T(8,128)(2,1)S(1)}, bf16[128,1024]{1,0:T(8,128)(2,1)S(1)}, u32[]{:S(2)}, u32[]{:S(2)}) %collective-permute-start.36) | collective-permute-done | bytes 262176 | tf_op jit(solution)/shard_map/ppermute | solution.py:169
  171.3 2.2 %collective-permute-done.31 = bf16[128,1024]{1,0:T(8,128)(2,1)S(1)} collective-permute-done((bf16[128,1024]{1,0:T(8,128)(2,1)S(1)}, bf16[128,1024]{1,0:T(8,128)(2,1)S(1)}, u32[]{:S(2)}, u32[]{:S(2)}) %collective-permute-start.31) | collective-permute-done | bytes 262176 | tf_op jit(solution)/shard_map/ppermute | solution.py:169
  174.4 4.7 %collective-permute-done.41 = bf16[128,1024]{1,0:T(8,128)(2,1)S(1)} collective-permute-done((bf16[128,1024]{1,0:T(8,128)(2,1)S(1)}, bf16[128,1024]{1,0:T(8,128)(2,1)S(1)}, u32[]{:S(2)}, u32[]{:S(2)}) %collective-permute-start.41) | collective-permute-done | bytes 262176 | tf_op jit(solution)/shard_map/ppermute | solution.py:169
  180.6 1.7 collective-permute-start.38
  185.4 2.1 %collective-permute-done.38 = bf16[32,1024]{1,0:T(8,128)(2,1)S(1)} collective-permute-done((bf16[32,1024]{1,0:T(8,128)(2,1)S(1)}, bf16[32,1024]{1,0:T(8,128)(2,1)S(1)}, u32[]{:S(2)}, u32[]{:S(2)}) %collective-permute-start.38) | collective-permute-done | bytes 65568 | tf_op jit(solution)/shard_map/ppermute | solution.py:169
  188.2 1.7 collective-permute-start.49
  190.0 3.0 %collective-permute-start.28 = (bf16[32,1152]{1,0:T(8,128)(2,1)S(1)}, bf16[32,1152]{1,0:T(8,128)(2,1)S(1)}, u32[]{:S(2)}, u32[]{:S(2)}) collective-permute-start(bf16[32,1152]{1,0:T(8,128)(2,1)S(1)} %slice.623), channel_id=1, source_target_pairs={{0,16},{2,18},{4,20},{6,22},{8,24},{10,26},{12,28},{14,30},{16,0},... | collective-permute-start | bytes 221192 | tf_op jit(solution)/shard_map/ppermute | solution.py:169
  193.1 2.8 %collective-permute-done.28 = bf16[32,1152]{1,0:T(8,128)(2,1)S(1)} collective-permute-done((bf16[32,1152]{1,0:T(8,128)(2,1)S(1)}, bf16[32,1152]{1,0:T(8,128)(2,1)S(1)}, u32[]{:S(2)}, u32[]{:S(2)}) %collective-permute-start.28) | collective-permute-done | bytes 73760 | tf_op jit(solution)/shard_map/ppermute | solution.py:169
  197.0 1.5 collective-permute-start.44
  198.4 1.5 collective-permute-done.29
  200.0 2.2 %collective-permute-done.44 = bf16[16,1024]{1,0:T(8,128)(2,1)S(1)} collective-permute-done((bf16[16,1024]{1,0:T(8,128)(2,1)S(1)}, bf16[16,1024]{1,0:T(8,128)(2,1)S(1)}, u32[]{:S(2)}, u32[]{:S(2)}) %collective-permute-start.44) | collective-permute-done | bytes 32800 | tf_op jit(solution)/shard_map/ppermute | solution.py:169
  (291 shorter events, 55.4 us)
Async XLA Ops:
  4.0 29.7 %collective-permute-start.20 = (bf16[16,2048]{1,0:T(8,128)(2,1)S(1)}, bf16[16,2048]{1,0:T(8,128)(2,1)S(1)}, u32[]{:S(2)}, u32[]{:S(2)}) collective-permute-start(bf16[16,2048]{1,0:T(8,128)(2,1)S(1)} %get-tuple-element.102), channel_id=1, source_target_pairs={{0,4},{2,6},{4,0},{6,2},{8,12},{10,14},{12,8},{14,10},{16,20},{18,... | collective-permute-start | bytes 196616 | tf_op jit(solution)/shard_map/ppermute | solution.py:169
  7.6 26.7 %collective-permute-start.15 = (bf16[16,2048]{1,0:T(8,128)(2,1)S(1)}, bf16[16,2048]{1,0:T(8,128)(2,1)S(1)}, u32[]{:S(2)}, u32[]{:S(2)}) collective-permute-start(bf16[16,2048]{1,0:T(8,128)(2,1)S(1)} %get-tuple-element.107), channel_id=1, source_target_pairs={{0,16},{2,18},{4,20},{6,22},{8,24},{10,26},{12,28},{14,30},{16,0},... | collective-permute-start | bytes 196616 | tf_op jit(solution)/shard_map/ppermute | solution.py:169
  10.8 25.1 %collective-permute-start.10 = (bf16[16,2048]{1,0:T(8,128)(2,1)S(1)}, bf16[16,2048]{1,0:T(8,128)(2,1)S(1)}, u32[]{:S(2)}, u32[]{:S(2)}) collective-permute-start(bf16[16,2048]{1,0:T(8,128)(2,1)S(1)} %get-tuple-element.112), channel_id=1, source_target_pairs={{0,16},{2,18},{4,20},{6,22},{8,24},{10,26},{12,28},{14,30},{16,0},... | collective-permute-start | bytes 196616 | tf_op jit(solution)/shard_map/ppermute | solution.py:169
  11.8 24.7 %collective-permute-start.5 = (bf16[16,2048]{1,0:T(8,128)(2,1)S(1)}, bf16[16,2048]{1,0:T(8,128)(2,1)S(1)}, u32[]{:S(2)}, u32[]{:S(2)}) collective-permute-start(bf16[16,2048]{1,0:T(8,128)(2,1)S(1)} %get-tuple-element.117), channel_id=1, source_target_pairs={{0,16},{2,18},{4,20},{6,22},{8,24},{10,26},{12,28},{14,30},{16,0},... | collective-permute-start | bytes 196616 | tf_op jit(solution)/shard_map/ppermute | solution.py:169
  15.2 23.1 %collective-permute-start = (bf16[16,2176]{1,0:T(8,128)(2,1)S(1)}, bf16[16,2176]{1,0:T(8,128)(2,1)S(1)}, u32[]{:S(2)}, u32[]{:S(2)}) collective-permute-start(bf16[16,2176]{1,0:T(8,128)(2,1)S(1)} %get-tuple-element.97), channel_id=1, source_target_pairs={{0,1},{1,0},{2,3},{3,2},{4,5},{5,4},{6,7},{7,6},{8,9},{9,8},{10,11... | collective-permute-start | bytes 208904 | tf_op jit(solution)/shard_map/ppermute | solution.py:169
  33.7 5.0 %collective-permute-start.21 = (bf16[32,2048]{1,0:T(8,128)(2,1)S(1)}, bf16[32,2048]{1,0:T(8,128)(2,1)S(1)}, u32[]{:S(2)}, u32[]{:S(2)}) collective-permute-start(bf16[32,2048]{1,0:T(8,128)(2,1)S(1)} %pad_maximum_fusion.16), channel_id=1, source_target_pairs={{0,1},{1,0},{2,3},{3,2},{4,5},{5,4},{6,7},{7,6},{8,9},{9,8},{10,11... | collective-permute-start | bytes 393224 | tf_op jit(solution)/shard_map/ppermute | solution.py:169
  34.3 9.2 %collective-permute-start.16 = (bf16[32,2048]{1,0:T(8,128)(2,1)S(1)}, bf16[32,2048]{1,0:T(8,128)(2,1)S(1)}, u32[]{:S(2)}, u32[]{:S(2)}) collective-permute-start(bf16[32,2048]{1,0:T(8,128)(2,1)S(1)} %pad_maximum_fusion.15), channel_id=1, source_target_pairs={{0,8},{2,10},{4,12},{6,14},{8,0},{10,2},{12,4},{14,6},{16,24},{18,... | collective-permute-start | bytes 393224 | tf_op jit(solution)/shard_map/ppermute | solution.py:169
  36.0 10.4 %collective-permute-start.11 = (bf16[32,2048]{1,0:T(8,128)(2,1)S(1)}, bf16[32,2048]{1,0:T(8,128)(2,1)S(1)}, u32[]{:S(2)}, u32[]{:S(2)}) collective-permute-start(bf16[32,2048]{1,0:T(8,128)(2,1)S(1)} %pad_maximum_fusion.14), channel_id=1, source_target_pairs={{0,8},{2,10},{4,12},{6,14},{8,0},{10,2},{12,4},{14,6},{16,24},{18,... | collective-permute-start | bytes 393224 | tf_op jit(solution)/shard_map/ppermute | solution.py:169
  36.5 12.0 %collective-permute-start.6 = (bf16[32,2048]{1,0:T(8,128)(2,1)S(1)}, bf16[32,2048]{1,0:T(8,128)(2,1)S(1)}, u32[]{:S(2)}, u32[]{:S(2)}) collective-permute-start(bf16[32,2048]{1,0:T(8,128)(2,1)S(1)} %pad_maximum_fusion.13), channel_id=1, source_target_pairs={{0,8},{2,10},{4,12},{6,14},{8,0},{10,2},{12,4},{14,6},{16,24},{18,... | collective-permute-start | bytes 393224 | tf_op jit(solution)/shard_map/ppermute | solution.py:169
  38.3 13.4 %collective-permute-start.1 = (bf16[32,2176]{1,0:T(8,128)(2,1)S(1)}, bf16[32,2176]{1,0:T(8,128)(2,1)S(1)}, u32[]{:S(2)}, u32[]{:S(2)}) collective-permute-start(bf16[32,2176]{1,0:T(8,128)(2,1)S(1)} %pad_maximum_fusion.12), channel_id=1, source_target_pairs={{0,16},{2,18},{4,20},{6,22},{8,24},{10,26},{12,28},{14,30},{16,0},... | collective-permute-start | bytes 417800 | tf_op jit(solution)/shard_map/ppermute | solution.py:169
  38.8 17.8 %collective-permute-start.22 = (bf16[64,2048]{1,0:T(8,128)(2,1)S(1)}, bf16[64,2048]{1,0:T(8,128)(2,1)S(1)}, u32[]{:S(2)}, u32[]{:S(2)}) collective-permute-start(bf16[64,2048]{1,0:T(8,128)(2,1)S(1)} %pad_maximum_fusion.11), channel_id=1, source_target_pairs={{0,16},{2,18},{4,20},{6,22},{8,24},{10,26},{12,28},{14,30},{16,0},... | collective-permute-start | bytes 786440 | tf_op jit(solution)/shard_map/ppermute | solution.py:169
  43.5 13.2 %collective-permute-start.17 = (bf16[64,2048]{1,0:T(8,128)(2,1)S(1)}, bf16[64,2048]{1,0:T(8,128)(2,1)S(1)}, u32[]{:S(2)}, u32[]{:S(2)}) collective-permute-start(bf16[64,2048]{1,0:T(8,128)(2,1)S(1)} %pad_maximum_fusion.10), channel_id=1, source_target_pairs={{0,4},{2,6},{4,0},{6,2},{8,12},{10,14},{12,8},{14,10},{16,20},{18,... | collective-permute-start | bytes 786440 | tf_op jit(solution)/shard_map/ppermute | solution.py:169
  46.4 11.9 %collective-permute-start.12 = (bf16[64,2048]{1,0:T(8,128)(2,1)S(1)}, bf16[64,2048]{1,0:T(8,128)(2,1)S(1)}, u32[]{:S(2)}, u32[]{:S(2)}) collective-permute-start(bf16[64,2048]{1,0:T(8,128)(2,1)S(1)} %pad_maximum_fusion.9), channel_id=1, source_target_pairs={{0,1},{1,0},{2,3},{3,2},{4,5},{5,4},{6,7},{7,6},{8,9},{9,8},{10,11... | collective-permute-start | bytes 786440 | tf_op jit(solution)/shard_map/ppermute | solution.py:169
  48.6 10.3 %collective-permute-start.7 = (bf16[64,2048]{1,0:T(8,128)(2,1)S(1)}, bf16[64,2048]{1,0:T(8,128)(2,1)S(1)}, u32[]{:S(2)}, u32[]{:S(2)}) collective-permute-start(bf16[64,2048]{1,0:T(8,128)(2,1)S(1)} %pad_maximum_fusion.8), channel_id=1, source_target_pairs={{0,4},{2,6},{4,0},{6,2},{8,12},{10,14},{12,8},{14,10},{16,20},{18,... | collective-permute-start | bytes 786440 | tf_op jit(solution)/shard_map/ppermute | solution.py:169
  51.8 10.6 %collective-permute-start.2 = (bf16[64,2176]{1,0:T(8,128)(2,1)S(1)}, bf16[64,2176]{1,0:T(8,128)(2,1)S(1)}, u32[]{:S(2)}, u32[]{:S(2)}) collective-permute-start(bf16[64,2176]{1,0:T(8,128)(2,1)S(1)} %pad_maximum_fusion.7), channel_id=1, source_target_pairs={{0,8},{2,10},{4,12},{6,14},{8,0},{10,2},{12,4},{14,6},{16,24},{18,... | collective-permute-start | bytes 835592 | tf_op jit(solution)/shard_map/ppermute | solution.py:169
  56.6 14.1 %collective-permute-start.23 = (bf16[128,2048]{1,0:T(8,128)(2,1)S(1)}, bf16[128,2048]{1,0:T(8,128)(2,1)S(1)}, u32[]{:S(2)}, u32[]{:S(2)}) collective-permute-start(bf16[128,2048]{1,0:T(8,128)(2,1)S(1)} %pad_maximum_fusion.6), channel_id=1, source_target_pairs={{0,8},{2,10},{4,12},{6,14},{8,0},{10,2},{12,4},{14,6},{16,24},{18,... | collective-permute-start | bytes 1572872 | tf_op jit(solution)/shard_map/ppermute | solution.py:169
  56.7 14.9 %collective-permute-start.18 = (bf16[128,2048]{1,0:T(8,128)(2,1)S(1)}, bf16[128,2048]{1,0:T(8,128)(2,1)S(1)}, u32[]{:S(2)}, u32[]{:S(2)}) collective-permute-start(bf16[128,2048]{1,0:T(8,128)(2,1)S(1)} %pad_maximum_fusion.5), channel_id=1, source_target_pairs={{0,1},{1,0},{2,3},{3,2},{4,5},{5,4},{6,7},{7,6},{8,9},{9,8},{10,11... | collective-permute-start | bytes 1572872 | tf_op jit(solution)/shard_map/ppermute | solution.py:169
  58.4 14.9 %collective-permute-start.13 = (bf16[128,2048]{1,0:T(8,128)(2,1)S(1)}, bf16[128,2048]{1,0:T(8,128)(2,1)S(1)}, u32[]{:S(2)}, u32[]{:S(2)}) collective-permute-start(bf16[128,2048]{1,0:T(8,128)(2,1)S(1)} %pad_maximum_fusion.4), channel_id=1, source_target_pairs={{0,4},{2,6},{4,0},{6,2},{8,12},{10,14},{12,8},{14,10},{16,20},{18,... | collective-permute-start | bytes 1572872 | tf_op jit(solution)/shard_map/ppermute | solution.py:169
  59.0 19.5 %collective-permute-start.8 = (bf16[128,2048]{1,0:T(8,128)(2,1)S(1)}, bf16[128,2048]{1,0:T(8,128)(2,1)S(1)}, u32[]{:S(2)}, u32[]{:S(2)}) collective-permute-start(bf16[128,2048]{1,0:T(8,128)(2,1)S(1)} %pad_maximum_fusion.3), channel_id=1, source_target_pairs={{0,1},{1,0},{2,3},{3,2},{4,5},{5,4},{6,7},{7,6},{8,9},{9,8},{10,11... | collective-permute-start | bytes 1572872 | tf_op jit(solution)/shard_map/ppermute | solution.py:169
  62.4 18.1 %collective-permute-start.3 = (bf16[128,2176]{1,0:T(8,128)(2,1)S(1)}, bf16[128,2176]{1,0:T(8,128)(2,1)S(1)}, u32[]{:S(2)}, u32[]{:S(2)}) collective-permute-start(bf16[128,2176]{1,0:T(8,128)(2,1)S(1)} %pad_maximum_fusion.2), channel_id=1, source_target_pairs={{0,4},{2,6},{4,0},{6,2},{8,12},{10,14},{12,8},{14,10},{16,20},{18,... | collective-permute-start | bytes 1671176 | tf_op jit(solution)/shard_map/ppermute | solution.py:169
  70.8 10.0 %collective-permute-start.24 = (bf16[256,2048]{1,0:T(8,128)(2,1)S(1)}, bf16[256,2048]{1,0:T(8,128)(2,1)S(1)}, u32[]{:S(2)}, u32[]{:S(2)}) collective-permute-start(bf16[256,2048]{1,0:T(8,128)(2,1)S(1)} %get-tuple-element.55), channel_id=1, source_target_pairs={{0,2},{2,0},{4,6},{6,4},{8,10},{10,8},{12,14},{14,12},{16,18},{18,... | collective-permute-start | bytes 3145736 | tf_op jit(solution)/shard_map/ppermute | solution.py:169
  71.8 9.1 %collective-permute-start.19 = (bf16[256,2048]{1,0:T(8,128)(2,1)S(1)}, bf16[256,2048]{1,0:T(8,128)(2,1)S(1)}, u32[]{:S(2)}, u32[]{:S(2)}) collective-permute-start(bf16[256,2048]{1,0:T(8,128)(2,1)S(1)} %get-tuple-element.57), channel_id=1, source_target_pairs={{0,2},{2,0},{4,6},{6,4},{8,10},{10,8},{12,14},{14,12},{16,18},{18,... | collective-permute-start | bytes 3145736 | tf_op jit(solution)/shard_map/ppermute | solution.py:169
  73.4 7.6 %collective-permute-start.14 = (bf16[256,2048]{1,0:T(8,128)(2,1)S(1)}, bf16[256,2048]{1,0:T(8,128)(2,1)S(1)}, u32[]{:S(2)}, u32[]{:S(2)}) collective-permute-start(bf16[256,2048]{1,0:T(8,128)(2,1)S(1)} %get-tuple-element.59), channel_id=1, source_target_pairs={{0,2},{2,0},{4,6},{6,4},{8,10},{10,8},{12,14},{14,12},{16,18},{18,... | collective-permute-start | bytes 3145736 | tf_op jit(solution)/shard_map/ppermute | solution.py:169
  140.2 20.2 %collective-permute-start.35 = (bf16[256,1024]{1,0:T(8,128)(2,1)S(1)}, bf16[256,1024]{1,0:T(8,128)(2,1)S(1)}, u32[]{:S(2)}, u32[]{:S(2)}) collective-permute-start(bf16[256,1024]{1,0:T(8,128)(2,1)S(1)} %slice.611), channel_id=1, source_target_pairs={{0,2},{2,0},{4,6},{6,4},{8,10},{10,8},{12,14},{14,12},{16,18},{18,... | collective-permute-start | bytes 1572872 | tf_op jit(solution)/shard_map/ppermute | solution.py:169
  140.6 21.3 %collective-permute-start.45 = (bf16[256,1024]{1,0:T(8,128)(2,1)S(1)}, bf16[256,1024]{1,0:T(8,128)(2,1)S(1)}, u32[]{:S(2)}, u32[]{:S(2)}) collective-permute-start(bf16[256,1024]{1,0:T(8,128)(2,1)S(1)} %slice.609), channel_id=1, source_target_pairs={{0,2},{2,0},{4,6},{6,4},{8,10},{10,8},{12,14},{14,12},{16,18},{18,... | collective-permute-start | bytes 1572872 | tf_op jit(solution)/shard_map/ppermute | solution.py:169
  140.8 23.2 %collective-permute-start.30 = (bf16[256,1024]{1,0:T(8,128)(2,1)S(1)}, bf16[256,1024]{1,0:T(8,128)(2,1)S(1)}, u32[]{:S(2)}, u32[]{:S(2)}) collective-permute-start(bf16[256,1024]{1,0:T(8,128)(2,1)S(1)} %slice.612), channel_id=1, source_target_pairs={{0,2},{2,0},{4,6},{6,4},{8,10},{10,8},{12,14},{14,12},{16,18},{18,... | collective-permute-start | bytes 1572872 | tf_op jit(solution)/shard_map/ppermute | solution.py:169
  141.2 23.8 %collective-permute-start.40 = (bf16[256,1024]{1,0:T(8,128)(2,1)S(1)}, bf16[256,1024]{1,0:T(8,128)(2,1)S(1)}, u32[]{:S(2)}, u32[]{:S(2)}) collective-permute-start(bf16[256,1024]{1,0:T(8,128)(2,1)S(1)} %slice.610), channel_id=1, source_target_pairs={{0,2},{2,0},{4,6},{6,4},{8,10},{10,8},{12,14},{14,12},{16,18},{18,... | collective-permute-start | bytes 1572872 | tf_op jit(solution)/shard_map/ppermute | solution.py:169
  141.4 25.2 %collective-permute-start.25 = (bf16[256,1152]{1,0:T(8,128)(2,1)S(1)}, bf16[256,1152]{1,0:T(8,128)(2,1)S(1)}, u32[]{:S(2)}, u32[]{:S(2)}) collective-permute-start(bf16[256,1152]{1,0:T(8,128)(2,1)S(1)} %fusion.59), channel_id=1, source_target_pairs={{0,2},{2,0},{4,6},{6,4},{8,10},{10,8},{12,14},{14,12},{16,18},{18,... | collective-permute-start | bytes 1769480 | tf_op jit(solution)/shard_map/ppermute | solution.py:169
  160.6 9.0 %collective-permute-start.36 = (bf16[128,1024]{1,0:T(8,128)(2,1)S(1)}, bf16[128,1024]{1,0:T(8,128)(2,1)S(1)}, u32[]{:S(2)}, u32[]{:S(2)}) collective-permute-start(bf16[128,1024]{1,0:T(8,128)(2,1)S(1)} %slice.616), channel_id=1, source_target_pairs={{0,4},{2,6},{4,0},{6,2},{8,12},{10,14},{12,8},{14,10},{16,20},{18,... | collective-permute-start | bytes 786440 | tf_op jit(solution)/shard_map/ppermute | solution.py:169
  162.2 8.6 %collective-permute-start.46 = (bf16[128,1024]{1,0:T(8,128)(2,1)S(1)}, bf16[128,1024]{1,0:T(8,128)(2,1)S(1)}, u32[]{:S(2)}, u32[]{:S(2)}) collective-permute-start(bf16[128,1024]{1,0:T(8,128)(2,1)S(1)} %slice.614), channel_id=1, source_target_pairs={{0,8},{2,10},{4,12},{6,14},{8,0},{10,2},{12,4},{14,6},{16,24},{18,... | collective-permute-start | bytes 786440 | tf_op jit(solution)/shard_map/ppermute | solution.py:169
  164.2 9.3 %collective-permute-start.31 = (bf16[128,1024]{1,0:T(8,128)(2,1)S(1)}, bf16[128,1024]{1,0:T(8,128)(2,1)S(1)}, u32[]{:S(2)}, u32[]{:S(2)}) collective-permute-start(bf16[128,1024]{1,0:T(8,128)(2,1)S(1)} %slice.617), channel_id=1, source_target_pairs={{0,1},{1,0},{2,3},{3,2},{4,5},{5,4},{6,7},{7,6},{8,9},{9,8},{10,11... | collective-permute-start | bytes 786440 | tf_op jit(solution)/shard_map/ppermute | solution.py:169
  165.2 13.9 %collective-permute-start.41 = (bf16[128,1024]{1,0:T(8,128)(2,1)S(1)}, bf16[128,1024]{1,0:T(8,128)(2,1)S(1)}, u32[]{:S(2)}, u32[]{:S(2)}) collective-permute-start(bf16[128,1024]{1,0:T(8,128)(2,1)S(1)} %slice.615), channel_id=1, source_target_pairs={{0,1},{1,0},{2,3},{3,2},{4,5},{5,4},{6,7},{7,6},{8,9},{9,8},{10,11... | collective-permute-start | bytes 786440 | tf_op jit(solution)/shard_map/ppermute | solution.py:169
  166.7 13.2 %collective-permute-start.26 = (bf16[128,1152]{1,0:T(8,128)(2,1)S(1)}, bf16[128,1152]{1,0:T(8,128)(2,1)S(1)}, u32[]{:S(2)}, u32[]{:S(2)}) collective-permute-start(bf16[128,1152]{1,0:T(8,128)(2,1)S(1)} %slice.613), channel_id=1, source_target_pairs={{0,4},{2,6},{4,0},{6,2},{8,12},{10,14},{12,8},{14,10},{16,20},{18,... | collective-permute-start | bytes 884744 | tf_op jit(solution)/shard_map/ppermute | solution.py:169
  169.7 10.8 %collective-permute-start.37 = (bf16[64,1024]{1,0:T(8,128)(2,1)S(1)}, bf16[64,1024]{1,0:T(8,128)(2,1)S(1)}, u32[]{:S(2)}, u32[]{:S(2)}) collective-permute-start(bf16[64,1024]{1,0:T(8,128)(2,1)S(1)} %slice.621), channel_id=1, source_target_pairs={{0,1},{1,0},{2,3},{3,2},{4,5},{5,4},{6,7},{7,6},{8,9},{9,8},{10,11... | collective-permute-start | bytes 393224 | tf_op jit(solution)/shard_map/ppermute | solution.py:169
  170.8 11.5 %collective-permute-start.47 = (bf16[64,1024]{1,0:T(8,128)(2,1)S(1)}, bf16[64,1024]{1,0:T(8,128)(2,1)S(1)}, u32[]{:S(2)}, u32[]{:S(2)}) collective-permute-start(bf16[64,1024]{1,0:T(8,128)(2,1)S(1)} %slice.619), channel_id=1, source_target_pairs={{0,16},{2,18},{4,20},{6,22},{8,24},{10,26},{12,28},{14,30},{16,0},... | collective-permute-start | bytes 393224 | tf_op jit(solution)/shard_map/ppermute | solution.py:169
  173.6 9.6 %collective-permute-start.32 = (bf16[64,1024]{1,0:T(8,128)(2,1)S(1)}, bf16[64,1024]{1,0:T(8,128)(2,1)S(1)}, u32[]{:S(2)}, u32[]{:S(2)}) collective-permute-start(bf16[64,1024]{1,0:T(8,128)(2,1)S(1)} %slice.622), channel_id=1, source_target_pairs={{0,4},{2,6},{4,0},{6,2},{8,12},{10,14},{12,8},{14,10},{16,20},{18,... | collective-permute-start | bytes 393224 | tf_op jit(solution)/shard_map/ppermute | solution.py:169
  179.2 5.0 %collective-permute-start.42 = (bf16[64,1024]{1,0:T(8,128)(2,1)S(1)}, bf16[64,1024]{1,0:T(8,128)(2,1)S(1)}, u32[]{:S(2)}, u32[]{:S(2)}) collective-permute-start(bf16[64,1024]{1,0:T(8,128)(2,1)S(1)} %slice.620), channel_id=1, source_target_pairs={{0,4},{2,6},{4,0},{6,2},{8,12},{10,14},{12,8},{14,10},{16,20},{18,... | collective-permute-start | bytes 393224 | tf_op jit(solution)/shard_map/ppermute | solution.py:169
  180.1 9.9 %collective-permute-start.27 = (bf16[64,1152]{1,0:T(8,128)(2,1)S(1)}, bf16[64,1152]{1,0:T(8,128)(2,1)S(1)}, u32[]{:S(2)}, u32[]{:S(2)}) collective-permute-start(bf16[64,1152]{1,0:T(8,128)(2,1)S(1)} %slice.618), channel_id=1, source_target_pairs={{0,8},{2,10},{4,12},{6,14},{8,0},{10,2},{12,4},{14,6},{16,24},{18,... | collective-permute-start | bytes 442376 | tf_op jit(solution)/shard_map/ppermute | solution.py:169
  180.6 6.9 %collective-permute-start.38 = (bf16[32,1024]{1,0:T(8,128)(2,1)S(1)}, bf16[32,1024]{1,0:T(8,128)(2,1)S(1)}, u32[]{:S(2)}, u32[]{:S(2)}) collective-permute-start(bf16[32,1024]{1,0:T(8,128)(2,1)S(1)} %slice.626), channel_id=1, source_target_pairs={{0,8},{2,10},{4,12},{6,14},{8,0},{10,2},{12,4},{14,6},{16,24},{18,... | collective-permute-start | bytes 196616 | tf_op jit(solution)/shard_map/ppermute | solution.py:169
  182.3 5.9 %collective-permute-start.48 = (bf16[32,1024]{1,0:T(8,128)(2,1)S(1)}, bf16[32,1024]{1,0:T(8,128)(2,1)S(1)}, u32[]{:S(2)}, u32[]{:S(2)}) collective-permute-start(bf16[32,1024]{1,0:T(8,128)(2,1)S(1)} %slice.624), channel_id=1, source_target_pairs={{0,1},{1,0},{2,3},{3,2},{4,5},{5,4},{6,7},{7,6},{8,9},{9,8},{10,11... | collective-permute-start | bytes 196616 | tf_op jit(solution)/shard_map/ppermute | solution.py:169
  183.2 9.8 %collective-permute-start.33 = (bf16[32,1024]{1,0:T(8,128)(2,1)S(1)}, bf16[32,1024]{1,0:T(8,128)(2,1)S(1)}, u32[]{:S(2)}, u32[]{:S(2)}) collective-permute-start(bf16[32,1024]{1,0:T(8,128)(2,1)S(1)} %slice.627), channel_id=1, source_target_pairs={{0,8},{2,10},{4,12},{6,14},{8,0},{10,2},{12,4},{14,6},{16,24},{18,... | collective-permute-start | bytes 196616 | tf_op jit(solution)/shard_map/ppermute | solution.py:169
  184.3 12.7 %collective-permute-start.43 = (bf16[32,1024]{1,0:T(8,128)(2,1)S(1)}, bf16[32,1024]{1,0:T(8,128)(2,1)S(1)}, u32[]{:S(2)}, u32[]{:S(2)}) collective-permute-start(bf16[32,1024]{1,0:T(8,128)(2,1)S(1)} %slice.625), channel_id=1, source_target_pairs={{0,8},{2,10},{4,12},{6,14},{8,0},{10,2},{12,4},{14,6},{16,24},{18,... | collective-permute-start | bytes 196616 | tf_op jit(solution)/shard_map/ppermute | solution.py:169
  187.5 12.4 %collective-permute-start.39 = (bf16[16,1024]{1,0:T(8,128)(2,1)S(1)}, bf16[16,1024]{1,0:T(8,128)(2,1)S(1)}, u32[]{:S(2)}, u32[]{:S(2)}) collective-permute-start(bf16[16,1024]{1,0:T(8,128)(2,1)S(1)} %slice.631), channel_id=1, source_target_pairs={{0,16},{2,18},{4,20},{6,22},{8,24},{10,26},{12,28},{14,30},{16,0},... | collective-permute-start | bytes 98312 | tf_op jit(solution)/shard_map/ppermute | solution.py:169
  188.2 14.6 %collective-permute-start.49 = (bf16[16,1024]{1,0:T(8,128)(2,1)S(1)}, bf16[16,1024]{1,0:T(8,128)(2,1)S(1)}, u32[]{:S(2)}, u32[]{:S(2)}) collective-permute-start(bf16[16,1024]{1,0:T(8,128)(2,1)S(1)} %slice.629), channel_id=1, source_target_pairs={{0,4},{2,6},{4,0},{6,2},{8,12},{10,14},{12,8},{14,10},{16,20},{18,... | collective-permute-start | bytes 98312 | tf_op jit(solution)/shard_map/ppermute | solution.py:169
  190.0 5.9 %collective-permute-start.28 = (bf16[32,1152]{1,0:T(8,128)(2,1)S(1)}, bf16[32,1152]{1,0:T(8,128)(2,1)S(1)}, u32[]{:S(2)}, u32[]{:S(2)}) collective-permute-start(bf16[32,1152]{1,0:T(8,128)(2,1)S(1)} %slice.623), channel_id=1, source_target_pairs={{0,16},{2,18},{4,20},{6,22},{8,24},{10,26},{12,28},{14,30},{16,0},... | collective-permute-start | bytes 221192 | tf_op jit(solution)/shard_map/ppermute | solution.py:169
  193.0 6.9 %collective-permute-start.34 = (bf16[16,1024]{1,0:T(8,128)(2,1)S(1)}, bf16[16,1024]{1,0:T(8,128)(2,1)S(1)}, u32[]{:S(2)}, u32[]{:S(2)}) collective-permute-start(bf16[16,1024]{1,0:T(8,128)(2,1)S(1)} %slice.632), channel_id=1, source_target_pairs={{0,16},{2,18},{4,20},{6,22},{8,24},{10,26},{12,28},{14,30},{16,0},... | collective-permute-start | bytes 98312 | tf_op jit(solution)/shard_map/ppermute | solution.py:169
  195.9 4.0 %collective-permute-start.29 = (bf16[16,1152]{1,0:T(8,128)(2,1)S(1)}, bf16[16,1152]{1,0:T(8,128)(2,1)S(1)}, u32[]{:S(2)}, u32[]{:S(2)}) collective-permute-start(bf16[16,1152]{1,0:T(8,128)(2,1)S(1)} %slice.628), channel_id=1, source_target_pairs={{0,1},{1,0},{2,3},{3,2},{4,5},{5,4},{6,7},{7,6},{8,9},{9,8},{10,11... | collective-permute-start | bytes 110600 | tf_op jit(solution)/shard_map/ppermute | solution.py:169
  197.0 5.2 %collective-permute-start.44 = (bf16[16,1024]{1,0:T(8,128)(2,1)S(1)}, bf16[16,1024]{1,0:T(8,128)(2,1)S(1)}, u32[]{:S(2)}, u32[]{:S(2)}) collective-permute-start(bf16[16,1024]{1,0:T(8,128)(2,1)S(1)} %slice.630), channel_id=1, source_target_pairs={{0,16},{2,18},{4,20},{6,22},{8,24},{10,26},{12,28},{14,30},{16,0},... | collective-permute-start | bytes 98312 | tf_op jit(solution)/shard_map/ppermute | solution.py:169
  (43 other events, 308.6 us)

commit v2 on v0

--- a/solution.py
+++ b/solution.py
@@ -1,7 +1,13 @@
 import jax
 import jax.numpy as jnp
 from jax import lax
+from jax.experimental import pallas as pl
+from jax.experimental.pallas import tpu as pltpu
 from jax.sharding import PartitionSpec as P
+
+LANES = 128
+FIRST = (((0,), (0,)), ((), ()))
+LAST = (((1,), (1,)), ((), ()))
 
 
 def slot_table(routes_all, experts, n_expert, capacity):
@@ -31,7 +37,7 @@
     return (gate_piece, grad_both, scaled_hidden)
 
 
-def body(quant_tokens, token_scales, expert_ids, gate_weights, grad_out, w_in, w_out):
+def routed_body(quant_tokens, token_scales, expert_ids, gate_weights, grad_out, w_in, w_out):
     tok_dev, width = quant_tokens.shape
     blocks = token_scales.shape[1]
     top = expert_ids.shape[1]
@@ -159,6 +165,351 @@
     return (grad_tokens, mine_gate, grad_w_in, grad_w_out)
 
 
+def after(value, *others):
+    return lax.optimization_barrier((value,) + others)[0]
+
+
+def swap(array, stage):
+    n_expert, n_tensor = lax.axis_size("expert"), lax.axis_size("tensor")
+    pairs = []
+    for e in range(n_expert):
+        for t in range(n_tensor):
+            axis, bit = stage[e & 1]
+            e_to, t_to = (e ^ bit, t) if axis == "expert" else (e, t ^ bit)
+            pairs.append((e * n_tensor + t, e_to * n_tensor + t_to))
+    return lax.ppermute(array, ("expert", "tensor"), pairs)
+
+
+def order_matrix(order, base, tok_dev):
+    count = tok_dev << len(order)
+    position = lax.broadcasted_iota(jnp.int32, (count, count), 1)
+    block, offset = position // tok_dev, position % tok_dev
+    top = len(order) - 1
+    half = block >> top
+    targets = []
+    for core in range(2):
+        where = [stage[core] for stage in base]
+        target = half << top
+        for place in range(top):
+            bit = (block >> place) & 1
+            target = target + (bit << where.index(order[place][core]))
+        targets.append(target)
+    owner = half ^ (lax.axis_index("expert") & 1)
+    target = jnp.where(owner == 0, targets[0], targets[1])
+    source = lax.broadcasted_iota(jnp.int32, (count, count), 0)
+    return (source == target * tok_dev + offset).astype(jnp.bfloat16)
+
+
+def pick_kernel(place, *refs):
+    blocks, out = refs[:4], refs[-1]
+    rows = jnp.concatenate([block[...] for block in blocks], axis=0)
+    out[...] = jnp.dot(place[...], rows, preferred_element_type=jnp.float32).astype(jnp.bfloat16)
+
+
+def pick(place, blocks, columns, start, width, so_far):
+    slots, tokens = place.shape
+    tile = 512
+    first = start // tile
+    kept = [pl.BlockSpec(memory_space=pl.ANY)] * len(so_far)
+    return pl.pallas_call(
+        pick_kernel,
+        grid=(columns // tile,),
+        in_specs=[pl.BlockSpec((slots, tokens), lambda i: (0, 0))]
+        + [pl.BlockSpec((tokens // 4, tile), lambda i: (0, i))] * 4
+        + kept,
+        out_specs=pl.BlockSpec((slots, tile), lambda i: (0, first + i)),
+        out_shape=jax.ShapeDtypeStruct((slots, width), jnp.bfloat16),
+        input_output_aliases={5: 0} if so_far else {},
+        compiler_params=pltpu.CompilerParams(vmem_limit_bytes=16 << 20),
+        cost_estimate=pl.CostEstimate(
+            flops=2 * slots * columns * tokens,
+            bytes_accessed=2 * columns * (tokens + slots),
+            transcendentals=0,
+        ),
+    )(place, *blocks, *so_far)
+
+
+def weight_grad_kernel(inputs, cotangent, gate_grad, up_grad, scaled, *rest):
+    grad_in, grad_out = rest[-2:]
+    x, g = inputs[...], cotangent[...]
+    grad_in[:, 0, :] = lax.dot_general(
+        x, gate_grad[...], FIRST, preferred_element_type=jnp.float32
+    ).astype(jnp.bfloat16)
+    grad_in[:, 1, :] = lax.dot_general(
+        x, up_grad[...], FIRST, preferred_element_type=jnp.float32
+    ).astype(jnp.bfloat16)
+    grad_out[...] = lax.dot_general(
+        g, scaled[...], FIRST, preferred_element_type=jnp.float32
+    ).astype(jnp.bfloat16)
+
+
+def weight_grads(inputs, cotangent, gate_grad, up_grad, scaled, start, columns, so_far):
+    rows, hidden = gate_grad.shape
+    width = inputs.shape[1]
+    tile = 512
+    first = start // tile
+    resident = pl.BlockSpec((rows, hidden), lambda i: (0, 0))
+    stream = pl.BlockSpec((rows, tile), lambda i: (0, first + i))
+    kept = [pl.BlockSpec(memory_space=pl.ANY)] * len(so_far)
+    return pl.pallas_call(
+        weight_grad_kernel,
+        grid=(columns // tile,),
+        in_specs=[stream, stream, resident, resident, resident] + kept,
+        out_specs=[
+            pl.BlockSpec((tile, 2, hidden), lambda i: (first + i, 0, 0)),
+            pl.BlockSpec((tile, hidden), lambda i: (first + i, 0)),
+        ],
+        out_shape=[
+            jax.ShapeDtypeStruct((width, 2, hidden), jnp.bfloat16),
+            jax.ShapeDtypeStruct((width, hidden), jnp.bfloat16),
+        ],
+        input_output_aliases={5: 0, 6: 1} if so_far else {},
+        compiler_params=pltpu.CompilerParams(vmem_limit_bytes=20 << 20),
+        cost_estimate=pl.CostEstimate(
+            flops=6 * rows * columns * hidden,
+            bytes_accessed=6 * columns * hidden + 4 * rows * columns,
+            transcendentals=0,
+        ),
+    )(inputs, cotangent, gate_grad, up_grad, scaled, *so_far)
+
+
+def gathered_body(quant_tokens, token_scales, expert_ids, gate_weights, grad_out, w_in, w_out):
+    tok_dev, width = quant_tokens.shape
+    blocks = token_scales.shape[1]
+    top = expert_ids.shape[1]
+    n_tensor = lax.axis_size("tensor")
+    n_expert = lax.axis_size("expert")
+    tokens = tok_dev * n_tensor * n_expert
+    half = tokens // 2
+    capacity = max(2, tok_dev * n_tensor * top * 13 // (12 * n_expert))
+    slots = n_expert * capacity
+    hidden = w_out.shape[2]
+    expert = lax.axis_index("expert")
+
+    both = lambda *stages: [(s, s) for s in stages]
+    core, across = ("expert", 1), ("expert", 2)
+    along = both(*[("expert", 1 << k) for k in range(2, n_expert.bit_length() - 1)][::-1])
+    sides = [("tensor", 1 << k) for k in range(n_tensor.bit_length() - 1)]
+    one, two = sides + [across], [across] + sides
+    crossed = list(zip(one, two))
+    turned = list(zip(two, one))
+    last = both(core)
+    late = along + crossed + last
+    early = turned + along + last
+    mid = along[:1] + turned + along[1:] + last
+    orders = dict(p=late, d=early, q=late, r=mid, s=late)
+    unit = width // 10
+    sizes = dict(p=6 * unit, d=4 * unit, q=10 * unit)
+    starts = dict(p=0, d=6 * unit, q=0)
+    spans = dict(r=(0, 5 * unit), s=(5 * unit, 10 * unit))
+    base = orders["p"]
+
+    scaled = (
+        (
+            quant_tokens.astype(jnp.float32).reshape(tok_dev, blocks, width // blocks)
+            * token_scales[:, :, None]
+        )
+        .reshape(tok_dev, width)
+        .astype(jnp.bfloat16)
+    )
+    routes = jnp.concatenate([expert_ids.astype(jnp.bfloat16), gate_weights], axis=1)
+    routes = jnp.pad(routes, ((0, 0), (0, LANES - 2 * top)))
+
+    rows = {}
+    for name in "pdq":
+        lo, hi = starts[name], starts[name] + sizes[name]
+        part = scaled[:, lo:hi] if name in "pd" else grad_out[:, lo:hi]
+        rows[name] = jnp.concatenate([part, routes], axis=1) if name == "p" else part
+
+    tips = {}
+
+    def step(name, *others):
+        level = (rows[name].shape[0] // tok_dev).bit_length() - 1
+        sent = after(rows[name], *others) if others else rows[name]
+        got = swap(sent, orders[name][level])
+        tips[name] = sent
+        rows[name] = jnp.concatenate([sent, got], axis=0) if level < 3 else (sent, got)
+        return got
+
+    def finish(name, *others):
+        low, high = rows[name]
+        far_low = swap(after(low, *others[:-1]) if others[:-1] else low, last[0])
+        far_high = swap(after(high, *others[-1:]) if others else high, last[0])
+        rows[name] = (low, high, far_low, far_high)
+        return far_high
+
+    def make_routes():
+        routes_all = jnp.concatenate([r[:, sizes["p"] :] for r in rows["p"]], axis=0)
+        routes_all = routes_all.astype(jnp.float32)
+        lane = lax.broadcasted_iota(jnp.int32, routes_all.shape, 1)
+        named = (routes_all == expert.astype(jnp.float32)) & (lane < top)
+        chosen = jnp.any(named, axis=1, keepdims=True)
+        gate_lanes = jnp.pad(routes_all[:, top:], ((0, 0), (0, top)))
+        token_gate = jnp.sum(jnp.where(named, gate_lanes, 0.0), axis=1, keepdims=True)
+        earlier = lax.broadcasted_iota(jnp.int32, (tokens, tokens), 0)
+        later = lax.broadcasted_iota(jnp.int32, (tokens, tokens), 1)
+        far = 2 * tokens
+        ranking = jnp.where(earlier == later, -far, (earlier < later).astype(jnp.int32))
+        ranking = ranking.astype(jnp.bfloat16)
+        member = chosen.astype(jnp.bfloat16)
+        rank = far + lax.dot_general(member, ranking, FIRST, preferred_element_type=jnp.float32)
+        slot = lax.broadcasted_iota(jnp.int32, (slots, tokens), 0).astype(jnp.float32)
+        placing = (slot == rank).astype(jnp.bfloat16)
+        slot_gates = jnp.dot(
+            placing, token_gate.astype(jnp.bfloat16), preferred_element_type=jnp.float32
+        )
+        placings = {}
+        for name in orders:
+            if orders[name] == base:
+                placings[name] = placing
+                continue
+            moved = order_matrix(orders[name], base, tok_dev)
+            placings[name] = jnp.dot(
+                placing, moved, preferred_element_type=jnp.float32
+            ).astype(jnp.bfloat16)
+        return named, slot_gates, placings
+
+    picked = dict(x=(), g=())
+
+    def pick_step(name, *others):
+        kind = "x" if name in "pd" else "g"
+        place = after(placings[name], *others) if others else placings[name]
+        picked[kind] = (
+            pick(place, rows[name], sizes[name], starts[name], width, picked[kind]),
+        )
+        return picked[kind][0]
+
+    p0 = step("p")
+    q0 = step("q")
+    d0 = step("d")
+    halves = {}
+    halves["r"] = lax.optimization_barrier(after(w_in, p0)[: 5 * unit, 0])
+    halves["s"] = lax.optimization_barrier(after(w_in, q0)[5 * unit :, 0])
+    p1 = step("p")
+    d1 = step("d", p0)
+    d2 = step("d")
+    q1 = step("q", p1)
+    p2 = step("p")
+    p3 = step("p")
+    d3 = step("d", p2)
+    q2 = step("q", d2)
+    finish("p")
+    named, slot_gates, placings = make_routes()
+    pick_step("p")
+    q3 = step("q", d3)
+    finish("d")
+    inputs = pick_step("d", tips["q"])
+    projected = 0.0
+    for name in "rs":
+        lo, hi = spans[name]
+        projected += jnp.einsum(
+            "rd,djh->rjh", inputs[:, lo:hi], halves[name], preferred_element_type=jnp.float32
+        )
+    gate_pre, up_value = projected[:, 0], projected[:, 1]
+    finish("q", tips["q"], projected)
+    cotangent = pick_step("q")
+    back = jnp.dot(cotangent, w_out[:, 0], preferred_element_type=jnp.float32)
+
+    sigmoid_gate = jax.nn.sigmoid(gate_pre)
+    activated = gate_pre * sigmoid_gate
+    hidden_value = activated * up_value
+    gate_piece = jnp.sum(hidden_value * back, axis=1, keepdims=True).astype(jnp.bfloat16)
+    grad_hidden = slot_gates * back
+    gate_grad = (
+        grad_hidden * up_value * sigmoid_gate * (1.0 + gate_pre * (1.0 - sigmoid_gate))
+    ).astype(jnp.bfloat16)
+    up_grad = (grad_hidden * activated).astype(jnp.bfloat16)
+    scaled_hidden = (slot_gates * hidden_value).astype(jnp.bfloat16)
+
+    grads = ()
+    sums = {}
+
+    def grad_step(low, high, *others):
+        nonlocal grads
+        left = after(gate_grad, *others) if others else gate_grad
+        grads = weight_grads(
+            inputs, cotangent, left, up_grad, scaled_hidden, low, high - low, grads
+        )
+        return grads[1]
+
+    grad_both = jnp.stack([gate_grad, up_grad], axis=1)
+
+    def piece_step(name, *others):
+        lo, hi = spans[name]
+        place = placings[name]
+        left = after(grad_both, *others) if others else grad_both
+        part = jnp.einsum(
+            "rjh,djh->rd", left, halves[name], preferred_element_type=jnp.float32
+        ).astype(jnp.bfloat16)
+        put = lambda rows, kind: lax.dot_general(
+            rows, part, FIRST, preferred_element_type=jnp.float32
+        ).astype(kind)
+        keep, send = put(place[:, :half], jnp.float32), put(place[:, half:], jnp.bfloat16)
+        if name == "s":
+            token_piece = lax.dot_general(
+                place, gate_piece, FIRST, preferred_element_type=jnp.float32
+            )
+            extra = jnp.where(named, token_piece, 0.0)
+            send = jnp.concatenate([send, extra[half:].astype(jnp.bfloat16)], axis=1)
+            sums[name] = ([keep, extra[:half]], send)
+        else:
+            sums[name] = ([keep], send)
+        return send
+
+    def sum_step(name, *others):
+        keeps, send = sums[name]
+        level = (send.shape[0] // tok_dev).bit_length() - 1
+        send = after(send, *others) if others else send
+        got = swap(send, orders[name][level])
+        count = send.shape[0] // 2
+        at, new, out = 0, [], []
+        for keep in keeps:
+            total = keep + got[:, at : at + keep.shape[1]].astype(jnp.float32)
+            at += keep.shape[1]
+            new.append(total[:count] if level else total)
+            out.append(total[count:].astype(jnp.bfloat16))
+        send = (out[0] if len(out) == 1 else jnp.concatenate(out, axis=1)) if level else got
+        sums[name] = (new, send)
+        return send
+
+    sr = piece_step("r")
+    r4 = sum_step("r")
+    ss = piece_step("s", sr)
+    s4 = sum_step("s")
+    r3 = sum_step("r", ss)
+    s3 = sum_step("s", r4)
+    g = grad_step(0, 4 * unit, s4)
+    s2 = sum_step("s", g)
+    r2 = sum_step("r", s3)
+    g = grad_step(4 * unit, 6 * unit, r3)
+    s1 = sum_step("s", g)
+    r1 = sum_step("r", s2)
+    g = grad_step(6 * unit, 8 * unit, r2)
+    s0 = sum_step("s", g)
+    r0 = sum_step("r", s1)
+    g = grad_step(8 * unit, 10 * unit, r1)
+
+    grad_gates = sums["s"][0][1][:, :top]
+    grad_tokens = jnp.concatenate([sums[n][0][0].astype(jnp.bfloat16) for n in "rs"], axis=1)
+    return (
+        grad_tokens,
+        grad_gates,
+        grads[0].reshape(width, 1, 2, hidden),
+        grads[1].reshape(width, 1, hidden),
+    )
+
+
+def body(*arrays):
+    quant_tokens, w_in = arrays[0], arrays[5]
+    n_expert, n_tensor = lax.axis_size("expert"), lax.axis_size("tensor")
+    whole = lax.axis_size("dp") == 1 and w_in.shape[1] == 1
+    doubling = n_tensor == 2 and n_expert >= 8 and n_expert & (n_expert - 1) == 0
+    few = quant_tokens.shape[0] * n_expert * n_tensor <= 1024
+    tiled = quant_tokens.shape[1] % (10 * 512) == 0
+    chosen = gathered_body if whole and doubling and few and tiled else routed_body
+    return chosen(*arrays)
+
+
 def solution(mesh):
     in_specs = (
         P(("dp", "expert", "tensor"), None),

time: 300 us -> 149 us (0.50)
  blocking collectives: 75.3 us -> 0 us
  local copies, waits for them, and re-layouts: 63.3 us -> 19.4 us
  matrix products: 49.3 us -> 15.6 us
  Pallas kernels: 0 us -> 30.2 us
  waiting for transfers between devices: 70.6 us -> 44.5 us
  between operations: 14 us -> 1.27 us
  starting transfers between devices: 23.2 us -> 31.2 us
  other arithmetic: 1.93 us -> 5.91 us
    all_to_all x3 -> x0, blocking collectives: 61 us -> none  [the longest x1 39 us: body(): lax.all_to_all(slot_cotangent, 'expert', split_axis=1, concat_axis=1, til...]
    unnamed x13 -> x36, local copies, waits for them, and re-layouts: 49.2 us -> 3.5 us
    ppermute x0 -> x28, waiting for transfers between devices: none -> 44.5 us  [swap(): return lax.ppermute(array, ('expert', 'tensor'), pairs)]
    all_to_all x5 -> x0, waiting for transfers between devices: 35.6 us -> none  [the longest x1 26.7 us: body(): lax.all_to_all(slot_inputs, 'expert', split_axis=1, concat_axis=1, tiled=...]
    dot_general x10 -> x14, matrix products: 49.3 us -> 15.6 us  [the longest x2 5.26 us: piece_step(): jnp.einsum('rjh,djh->rd', left, halves[name], preferred_element_type=jnp....]
    ppermute x0 -> x28, starting transfers between devices: none -> 31.2 us  [swap(): return lax.ppermute(array, ('expert', 'tensor'), pairs)]
    pallas_call x0 -> x7, Pallas kernels: none -> 30.2 us  [the longest x4 17.3 us: weight_grads(): pl.pallas_call(weight_grad_kernel, grid=(columns // tile,), in_specs=[str...]
    all_to_all x5 -> x0, starting transfers between devices: 23.1 us -> none  [the longest x1 6.34 us: body(): lax.all_to_all(slot_inputs, 'expert', split_axis=1, concat_axis=1, tiled=...]
  transfers between devices with their start and end apart: 8 -> 28, of which waited for: 5 -> 14; matrix products, arithmetic and copies ran while one was open for 28% -> 21% of each run, Pallas kernels for 0% -> 16%
where the time goes in v2:
time: 149 us; the launch traced here: 148 us
  waiting for transfers between devices  44.5 us (30%)
  starting transfers between devices  31.2 us (21%)
  Pallas kernels  30.2 us (20%)
  local copies, waits for them, and re-layouts  19.4 us (13%)
  matrix products  15.6 us (10%)
  other arithmetic  5.91 us (4%)
    ppermute x28, waiting for transfers between devices, swap(): return lax.ppermute(array, ('expert', 'tensor'), pairs)  44.5 us
    ppermute x28, starting transfers between devices, swap(): return lax.ppermute(array, ('expert', 'tensor'), pairs)  31.2 us
    pallas_call x4, Pallas kernels, weight_grads(): pl.pallas_call(weight_grad_kernel, grid=(columns // tile,), in_specs=[str...  17.3 us
    pallas_call x3, Pallas kernels, pick(): pl.pallas_call(pick_kernel, grid=(columns // tile,), in_specs=[pl.BlockSp...  12.9 us
    squeeze x1, local copies, waits for them, and re-layouts, gathered_body(): halves['r'] = lax.optimization_barrier(after(w_in, p0)[:5 * unit, 0])  7.8 us
    squeeze x1, local copies, waits for them, and re-layouts, gathered_body(): halves['s'] = lax.optimization_barrier(after(w_in, q0)[5 * unit:, 0])  6.68 us
    dot_general x2, matrix products, piece_step(): jnp.einsum('rjh,djh->rd', left, halves[name], preferred_element_type=jnp....  5.26 us
    dot_general x2, matrix products, gathered_body(): jnp.einsum('rd,djh->rjh', inputs[:, lo:hi], halves[name], preferred_eleme...  3.73 us
  transfers between devices with their start and end apart: 28, of which 14 were waited for; matrix products, arithmetic and copies ran while one was open for 21% of the time, Pallas kernels for 16%

profile of v2, /device:TPU:0, one launch (start us, length us, event | category | flops | bytes accessed | tf_op | source)
XLA Modules:
  0.0 148.1 jit_solution(1263782243625218783)
XLA Ops:
  0.6 4.1 %collective-permute-start.6 = (bf16[16,5120]{1,0:T(8,128)(2,1)}, bf16[16,5120]{1,0:T(8,128)(2,1)S(1)}, u32[]{:S(2)}, u32[]{:S(2)}) collective-permute-start(bf16[16,5120]{1,0:T(8,128)(2,1)} %param.11), channel_id=1, source_target_pairs={{0,16},{1,17},{2,18},{3,19},{4,20},{5,21},{6,22},{7,23},{8,24},{9,... | collective-permute-start | bytes 491528 | tf_op jit(solution)/shard_map/ppermute | solution.py:180
  4.7 0.8 mul.55
  5.6 1.0 fusion.84
  6.6 1.6 %collective-permute-start.8 = (bf16[16,2048]{1,0:T(8,128)(2,1)S(1)}, bf16[16,2048]{1,0:T(8,128)(2,1)S(1)}, u32[]{:S(2)}, u32[]{:S(2)}) collective-permute-start(bf16[16,2048]{1,0:T(8,128)(2,1)S(1)} %slice.236), channel_id=1, source_target_pairs={{0,4},{1,5},{2,3},{3,2},{4,0},{5,1},{6,7},{7,6},{8,12},{9,13},{10,... | collective-permute-start | bytes 196616 | tf_op jit(solution)/shard_map/ppermute | solution.py:180
  8.1 0.7 convert_element_type.141
  8.9 0.8 copy.27
  11.9 5.1 %collective-permute-done = bf16[16,3200]{1,0:T(8,128)(2,1)S(1)} collective-permute-done((bf16[16,3200]{1,0:T(8,128)(2,1)S(1)}, bf16[16,3200]{1,0:T(8,128)(2,1)S(1)}, u32[]{:S(2)}, u32[]{:S(2)}) %collective-permute-start) | collective-permute-done | bytes 102432 | tf_op jit(solution)/shard_map/ppermute | solution.py:180
  17.1 0.8 collective-permute-start.1
  17.9 1.6 %collective-permute-start.9 = (bf16[32,2048]{1,0:T(8,128)(2,1)S(1)}, bf16[32,2048]{1,0:T(8,128)(2,1)S(1)}, u32[]{:S(2)}, u32[]{:S(2)}) collective-permute-start(bf16[32,2048]{1,0:T(8,128)(2,1)S(1)} %pad_maximum_fusion.14), channel_id=1, source_target_pairs={{0,1},{1,0},{2,6},{3,7},{4,5},{5,4},{6,2},{7,3},{8,9},{9,8},{10,14... | collective-permute-start | bytes 393224 | tf_op jit(solution)/shard_map/ppermute | solution.py:180
  19.5 3.7 %collective-permute-done.1 = bf16[32,3200]{1,0:T(8,128)(2,1)S(1)} collective-permute-done((bf16[32,3200]{1,0:T(8,128)(2,1)S(1)}, bf16[32,3200]{1,0:T(8,128)(2,1)S(1)}, u32[]{:S(2)}, u32[]{:S(2)}) %collective-permute-start.1) | collective-permute-done | bytes 204832 | tf_op jit(solution)/shard_map/ppermute | solution.py:180
  23.2 1.6 %collective-permute-start.2 = (bf16[64,3200]{1,0:T(8,128)(2,1)S(1)}, bf16[64,3200]{1,0:T(8,128)(2,1)S(1)}, u32[]{:S(2)}, u32[]{:S(2)}) collective-permute-start(bf16[64,3200]{1,0:T(8,128)(2,1)S(1)} %pad_maximum_fusion.7), channel_id=1, source_target_pairs={{0,1},{1,0},{2,6},{3,7},{4,5},{5,4},{6,2},{7,3},{8,9},{9,8},{10,14... | collective-permute-start | bytes 1228808 | tf_op jit(solution)/shard_map/ppermute | solution.py:180
  24.8 3.4 %collective-permute-start.10 = (bf16[64,2048]{1,0:T(8,128)(2,1)S(1)}, bf16[64,2048]{1,0:T(8,128)(2,1)S(1)}, u32[]{:S(2)}, u32[]{:S(2)}) collective-permute-start(bf16[64,2048]{1,0:T(8,128)(2,1)S(1)} %pad_maximum_fusion.10), channel_id=1, source_target_pairs={{0,16},{1,17},{2,18},{3,19},{4,20},{5,21},{6,22},{7,23},{8,24},{9,... | collective-permute-start | bytes 786440 | tf_op jit(solution)/shard_map/ppermute | solution.py:180
  28.3 1.7 %collective-permute-start.7 = (bf16[32,5120]{1,0:T(8,128)(2,1)S(1)}, bf16[32,5120]{1,0:T(8,128)(2,1)S(1)}, u32[]{:S(2)}, u32[]{:S(2)}) collective-permute-start(bf16[32,5120]{1,0:T(8,128)(2,1)S(1)} %pad_maximum_fusion.9), channel_id=1, source_target_pairs={{0,8},{1,9},{2,10},{3,11},{4,12},{5,13},{6,14},{7,15},{8,0},{9,1},... | collective-permute-start | bytes 983048 | tf_op jit(solution)/shard_map/ppermute | solution.py:180
  30.0 1.2 collective-permute-done.2
  31.2 2.1 %collective-permute-start.3 = (bf16[128,3200]{1,0:T(8,128)(2,1)S(1)}, bf16[128,3200]{1,0:T(8,128)(2,1)S(1)}, u32[]{:S(2)}, u32[]{:S(2)}) collective-permute-start(bf16[128,3200]{1,0:T(8,128)(2,1)S(1)} %pad_maximum_fusion.2.refs_0_), channel_id=1, source_target_pairs={{0,4},{1,5},{2,3},{3,2},{4,0},{5,1},{6,7},{7,6},{8,12},{9,13},{10,... | collective-permute-start | bytes 2457608 | tf_op jit(solution)/shard_map/ppermute | solution.py:180
  33.3 7.8 %slice_bitcast_fusion.1 = bf16[2560,2,768]{2,1,0:T(2,128)(2,1)} fusion(bf16[5120,1,2,768]{3,2,1,0:T(2,128)(2,1)} %param.12), kind=kLoop, calls=%fused_computation.3 | loop fusion | bytes 15728640 | tf_op jit(solution)/shard_map/squeeze | solution.py:386
  41.5 1.6 %collective-permute-start.11 = (bf16[64,5120]{1,0:T(8,128)(2,1)S(1)}, bf16[64,5120]{1,0:T(8,128)(2,1)S(1)}, u32[]{:S(2)}, u32[]{:S(2)}) collective-permute-start(bf16[64,5120]{1,0:T(8,128)(2,1)S(1)} %pad_maximum_fusion.4), channel_id=1, source_target_pairs={{0,1},{1,0},{2,6},{3,7},{4,5},{5,4},{6,2},{7,3},{8,9},{9,8},{10,14... | collective-permute-start | bytes 1966088 | tf_op jit(solution)/shard_map/ppermute | solution.py:180
  43.1 1.3 collective-permute-start.12
  44.4 2.3 %collective-permute-done.3.refs_1_ = bf16[128,3200]{1,0:T(8,128)(2,1)S(1)} collective-permute-done((bf16[128,3200]{1,0:T(8,128)(2,1)S(1)}, bf16[128,3200]{1,0:T(8,128)(2,1)S(1)}, u32[]{:S(2)}, u32[]{:S(2)}) %collective-permute-start.3) | collective-permute-done | bytes 819232 | tf_op jit(solution)/shard_map/ppermute | solution.py:180
  46.6 6.7 %slice_bitcast_fusion = bf16[2560,2,768]{2,1,0:T(2,128)(2,1)} fusion(bf16[5120,1,2,768]{3,2,1,0:T(2,128)(2,1)S(1)} %copy-done.4), kind=kLoop, calls=%fused_computation.2 | loop fusion | bytes 15728640 | tf_op jit(solution)/shard_map/squeeze | solution.py:387
  53.7 3.8 %collective-permute-done.12.refs_1_ = bf16[128,2048]{1,0:T(8,128)(2,1)} collective-permute-done((bf16[128,2048]{1,0:T(8,128)(2,1)S(1)}, bf16[128,2048]{1,0:T(8,128)(2,1)}, u32[]{:S(2)}, u32[]{:S(2)}) %collective-permute-start.12) | collective-permute-done | bytes 524320 | tf_op jit(solution)/shard_map/ppermute | solution.py:180
  58.4 0.9 copy-done
  59.4 0.9 copy-done.2
  60.9 1.2 convolution_convert_fusion.2.place
  62.4 2.7 %shard_map.102.refs_4_ = bf16[208,5120]{1,0:T(8,128)(2,1)S(1)} custom-call(bf16[208,512]{1,0:T(8,128)(2,1)S(1)} %get-tuple-element.81.place, bf16[128,3200]{1,0:T(8,128)(2,1)S(1)} %pad_maximum_fusion.2.refs_0_, bf16[128,3200]{1,0:T(8,128)(2,1)S(1)} %collective-permute-done.3.refs_1_, bf16[128,3200]{1,0:T(8,128)(2,1)S(1)} %copy-done.1, ...), custom_call_target="tpu_custom_call" | custom-call | flops 654311424 | bytes 4423680 | tf_op jit(solution)/shard_map/pallas_call | solution.py:214
  65.1 3.2 %shard_map.103.inputs = bf16[208,5120]{1,0:T(8,128)(2,1)S(1)} custom-call(bf16[208,512]{1,0:T(8,128)(2,1)S(1)} %convolution_convert_fusion.2.place, bf16[128,2048]{1,0:T(8,128)(2,1)S(1)} %pad_maximum_fusion.6.refs_0_, bf16[128,2048]{1,0:T(8,128)(2,1)} %collective-permute-done.12.refs_1_, ...), custom_call_target="tpu_custom_call", output_to_operand_aliasing={{}: (5, {})} | custom-call | flops 436207616 | bytes 2949120 | tf_op jit(solution)/shard_map/pallas_call | solution.py:214
  68.4 1.9 %fusion.4 = f32[208,2,768]{2,0,1:T(8,128)S(1)} fusion(bf16[2560,2,768]{2,1,0:T(2,128)(2,1)S(1)} %bitcast.77, bf16[208,5120]{1,0:T(8,128)(2,1)S(1)} %shard_map.103.inputs), kind=kOutput, calls=%fused_computation.6 | convolution fusion | flops 1635778560 | bytes 10207232 | tf_op jit(solution)/shard_map/rd,djh->rjh/dot_general | solution.py:405
  70.4 1.9 %fusion.22 = f32[208,2,768]{2,0,1:T(8,128)S(1)} fusion(f32[208,2,768]{2,0,1:T(8,128)S(1)} %fusion.4, bf16[2560,2,768]{2,1,0:T(2,128)(2,1)S(1)} %bitcast.75, bf16[208,5120]{1,0:T(8,128)(2,1)S(1)} %shard_map.103.inputs), kind=kOutput, calls=%fused_computation.29 | convolution fusion | flops 1636098048 | bytes 11485184 | tf_op jit(solution)/shard_map/rd,djh->rjh/dot_general | solution.py:405
  72.3 3.1 %collective-permute-done.13.refs_1_ = bf16[128,5120]{1,0:T(8,128)(2,1)} collective-permute-done((bf16[128,5120]{1,0:T(8,128)(2,1)S(1)}, bf16[128,5120]{1,0:T(8,128)(2,1)}, u32[]{:S(2)}, u32[]{:S(2)}) %collective-permute-start.13) | collective-permute-done | bytes 1310752 | tf_op jit(solution)/shard_map/ppermute | solution.py:180
  76.1 2.5 %collective-permute-done.17.refs_3_ = bf16[128,5120]{1,0:T(8,128)(2,1)S(1)} collective-permute-done((bf16[128,5120]{1,0:T(8,128)(2,1)}, bf16[128,5120]{1,0:T(8,128)(2,1)S(1)}, u32[]{:S(2)}, u32[]{:S(2)}) %collective-permute-start.17) | collective-permute-done | bytes 1310752 | tf_op jit(solution)/shard_map/ppermute | solution.py:180
  78.6 7.0 %shard_map.104.cotangent = bf16[208,5120]{1,0:T(8,128)(2,1)S(1)} custom-call(bf16[208,512]{1,0:T(8,128)(2,1)S(1)} %get-tuple-element.81.place, bf16[128,5120]{1,0:T(8,128)(2,1)S(1)} %pad_maximum_fusion.1.refs_0_, bf16[128,5120]{1,0:T(8,128)(2,1)} %collective-permute-done.13.refs_1_, bf16[128,5120]{1,0:T(8,128)(2,1)} %collective-permute-done.14.refs_2_, ...), custom_call_target="tpu_custom_call" | custom-call | flops 1090519040 | bytes 7372800 | tf_op jit(solution)/shard_map/pallas_call | solution.py:214
  85.7 2.1 %multiply_convert_fusion.2 = (bf16[208,768]{1,0:T(8,128)(2,1)S(1)}, bf16[208,768]{1,0:T(8,128)(2,1)S(1)}, bf16[208]{0:T(256)(128)(2,1)S(1)}, bf16[208,768]{1,0:T(8,128)(2,1)S(1)}) fusion(f32[208,2,768]{2,0,1:T(8,128)S(1)} %fusion.22, f32[208]{0:T(256)S(1)} %bitcast.83, bf16[208,5120]{1,0:T(8,128)(2,1)S(1)} %shard_map.104.cotangent, ...), kind=kOutput, calls=%fused_computation.78 | convolution fusion | flops 1638813440 | bytes 12231904 | tf_op jit(solution)/shard_map/dot_general | solution.py:411
  87.8 2.6 %fusion.19 = bf16[208,2560]{1,0:T(8,128)(2,1)S(1)} fusion(bf16[2560,2,768]{2,1,0:T(2,128)(2,1)S(1)} %bitcast.75, bf16[208,1,768]{2,0,1:T(8,128)(2,1)S(1)} %bitcast.70, bf16[208,1,768]{2,0,1:T(8,128)(2,1)S(1)} %bitcast.68), kind=kOutput, calls=%fused_computation.17 | convolution fusion | flops 1636630528 | bytes 9568256 | tf_op jit(solution)/shard_map/rjh,djh->rd/dot_general | solution.py:441
  91.7 2.6 %fusion.16 = bf16[208,2560]{1,0:T(8,128)(2,1)S(1)} fusion(bf16[208,2,768]{2,0,1:T(8,128)(2,1)S(1)} %pad_maximum_fusion.5, bf16[2560,2,768]{2,1,0:T(2,128)(2,1)S(1)} %bitcast.77), kind=kOutput, calls=%fused_computation.16 | convolution fusion | flops 1636311040 | bytes 9568256 | tf_op jit(solution)/shard_map/rjh,djh->rd/dot_general | solution.py:441
  96.0 1.3 collective-permute-start.19
  97.4 0.8 collective-permute-done.20
  99.5 13.3 %collective-permute-done.19 = bf16[128,2560]{1,0:T(8,128)(2,1)S(1)} collective-permute-done((bf16[128,2560]{1,0:T(8,128)(2,1)S(1)}, bf16[128,2560]{1,0:T(8,128)(2,1)S(1)}, u32[]{:S(2)}, u32[]{:S(2)}) %collective-permute-start.19) | collective-permute-done | bytes 655392 | tf_op jit(solution)/shard_map/ppermute | solution.py:180
  113.9 6.2 %shard_map.105 = (bf16[5120,2,768]{2,1,0:T(2,128)(2,1)}, bf16[5120,768]{1,0:T(8,128)(2,1)}) custom-call(bf16[208,5120]{1,0:T(8,128)(2,1)S(1)} %shard_map.103.inputs, bf16[208,5120]{1,0:T(8,128)(2,1)S(1)} %shard_map.104.cotangent, bf16[208,768]{1,0:T(8,128)(2,1)S(1)} %get-tuple-element.62.gate_grad, bf16[208,768]{1,0:T(8,128)(2,1)S(1)} %get-tuple-element.77.up_grad, ...), custom_call_target="tpu_custom_call" | custom-call | flops 1962934272 | bytes 11141120 | tf_op jit(solution)/shard_map/pallas_call | solution.py:254
  120.1 1.5 %collective-permute-start.23 = (bf16[64,2688]{1,0:T(8,128)(2,1)S(1)}, bf16[64,2688]{1,0:T(8,128)(2,1)S(1)}, u32[]{:S(2)}, u32[]{:S(2)}) collective-permute-start(bf16[64,2688]{1,0:T(8,128)(2,1)S(1)} %pad_maximum_fusion.8), channel_id=1, source_target_pairs={{0,1},{1,0},{2,6},{3,7},{4,5},{5,4},{6,2},{7,3},{8,9},{9,8},{10,14... | collective-permute-start | bytes 1032200 | tf_op jit(solution)/shard_map/ppermute | solution.py:180
  121.7 5.6 %collective-permute-done.23 = bf16[64,2688]{1,0:T(8,128)(2,1)S(1)} collective-permute-done((bf16[64,2688]{1,0:T(8,128)(2,1)S(1)}, bf16[64,2688]{1,0:T(8,128)(2,1)S(1)}, u32[]{:S(2)}, u32[]{:S(2)}) %collective-permute-start.23) | collective-permute-done | bytes 344096 | tf_op jit(solution)/shard_map/ppermute | solution.py:180
  128.0 3.7 %shard_map.106 = (bf16[5120,2,768]{2,1,0:T(2,128)(2,1)}, bf16[5120,768]{1,0:T(8,128)(2,1)}) custom-call(bf16[208,5120]{1,0:T(8,128)(2,1)S(1)} %shard_map.103.inputs, bf16[208,5120]{1,0:T(8,128)(2,1)S(1)} %shard_map.104.cotangent, bf16[208,768]{1,0:T(8,128)(2,1)S(1)} %get-tuple-element.62.gate_grad, ...), custom_call_target="tpu_custom_call", output_to_operand_aliasing={{0}: (5, {}), {1}: (6, {})} | custom-call | flops 981467136 | bytes 5570560 | tf_op jit(solution)/shard_map/pallas_call | solution.py:254
  131.8 1.3 collective-permute-start.25
  133.0 3.7 %shard_map.107 = (bf16[5120,2,768]{2,1,0:T(2,128)(2,1)}, bf16[5120,768]{1,0:T(8,128)(2,1)}) custom-call(bf16[208,5120]{1,0:T(8,128)(2,1)S(1)} %shard_map.103.inputs, bf16[208,5120]{1,0:T(8,128)(2,1)S(1)} %shard_map.104.cotangent, bf16[208,768]{1,0:T(8,128)(2,1)S(1)} %get-tuple-element.62.gate_grad, ...), custom_call_target="tpu_custom_call", output_to_operand_aliasing={{0}: (5, {}), {1}: (6, {})} | custom-call | flops 981467136 | bytes 5570560 | tf_op jit(solution)/shard_map/pallas_call | solution.py:254
  137.3 3.2 %collective-permute-start.26 = (bf16[16,2560]{1,0:T(8,128)(2,1)S(1)}, bf16[16,2560]{1,0:T(8,128)(2,1)S(1)}, u32[]{:S(2)}, u32[]{:S(2)}) collective-permute-start(bf16[16,2560]{1,0:T(8,128)(2,1)S(1)} %slice.367), channel_id=1, source_target_pairs={{0,16},{1,17},{2,18},{3,19},{4,20},{5,21},{6,22},{7,23},{8,24},{9,... | collective-permute-start | bytes 245768 | tf_op jit(solution)/shard_map/ppermute | solution.py:180
  140.5 3.7 %shard_map.108 = (bf16[5120,2,768]{2,1,0:T(2,128)(2,1)}, bf16[5120,768]{1,0:T(8,128)(2,1)}) custom-call(bf16[208,5120]{1,0:T(8,128)(2,1)S(1)} %shard_map.103.inputs, bf16[208,5120]{1,0:T(8,128)(2,1)S(1)} %shard_map.104.cotangent, bf16[208,768]{1,0:T(8,128)(2,1)S(1)} %get-tuple-element.62.gate_grad, ...), custom_call_target="tpu_custom_call", output_to_operand_aliasing={{0}: (5, {}), {1}: (6, {})} | custom-call | flops 981467136 | bytes 5570560 | tf_op jit(solution)/shard_map/pallas_call | solution.py:254
  144.5 2.2 %collective-permute-done.27 = bf16[16,2688]{1,0:T(8,128)(2,1)S(1)} collective-permute-done((bf16[16,2688]{1,0:T(8,128)(2,1)S(1)}, bf16[16,2688]{1,0:T(8,128)(2,1)S(1)}, u32[]{:S(2)}, u32[]{:S(2)}) %collective-permute-start.27) | collective-permute-done | bytes 86048 | tf_op jit(solution)/shard_map/ppermute | solution.py:180
  146.7 0.7 copy.32
  147.4 0.7 pad_maximum_fusion.13
  (141 shorter events, 12.6 us)
Async XLA Ops:
  0.6 24.1 %copy-start.5 = (bf16[16,5120]{1,0:T(8,128)(2,1)S(1)}, bf16[16,5120]{1,0:T(8,128)(2,1)}, u32[]{:S(2)}) copy-start(bf16[16,5120]{1,0:T(8,128)(2,1)} %param.11) | copy-start | bytes 491524
  0.6 24.1 %collective-permute-start.6 = (bf16[16,5120]{1,0:T(8,128)(2,1)}, bf16[16,5120]{1,0:T(8,128)(2,1)S(1)}, u32[]{:S(2)}, u32[]{:S(2)}) collective-permute-start(bf16[16,5120]{1,0:T(8,128)(2,1)} %param.11), channel_id=1, source_target_pairs={{0,16},{1,17},{2,18},{3,19},{4,20},{5,21},{6,22},{7,23},{8,24},{9,... | collective-permute-start | bytes 491528 | tf_op jit(solution)/shard_map/ppermute | solution.py:180
  6.6 11.3 %collective-permute-start.8 = (bf16[16,2048]{1,0:T(8,128)(2,1)S(1)}, bf16[16,2048]{1,0:T(8,128)(2,1)S(1)}, u32[]{:S(2)}, u32[]{:S(2)}) collective-permute-start(bf16[16,2048]{1,0:T(8,128)(2,1)S(1)} %slice.236), channel_id=1, source_target_pairs={{0,4},{1,5},{2,3},{3,2},{4,0},{5,1},{6,7},{7,6},{8,12},{9,13},{10,... | collective-permute-start | bytes 196616 | tf_op jit(solution)/shard_map/ppermute | solution.py:180
  9.8 7.3 %collective-permute-start = (bf16[16,3200]{1,0:T(8,128)(2,1)S(1)}, bf16[16,3200]{1,0:T(8,128)(2,1)S(1)}, u32[]{:S(2)}, u32[]{:S(2)}) collective-permute-start(bf16[16,3200]{1,0:T(8,128)(2,1)S(1)} %pad_maximum_fusion.15), channel_id=1, source_target_pairs={{0,16},{1,17},{2,18},{3,19},{4,20},{5,21},{6,22},{7,23},{8,24},{9,... | collective-permute-start | bytes 307208 | tf_op jit(solution)/shard_map/ppermute | solution.py:180
  17.1 6.0 %collective-permute-start.1 = (bf16[32,3200]{1,0:T(8,128)(2,1)S(1)}, bf16[32,3200]{1,0:T(8,128)(2,1)S(1)}, u32[]{:S(2)}, u32[]{:S(2)}) collective-permute-start(bf16[32,3200]{1,0:T(8,128)(2,1)S(1)} %pad_maximum_fusion.11), channel_id=1, source_target_pairs={{0,8},{1,9},{2,10},{3,11},{4,12},{5,13},{6,14},{7,15},{8,0},{9,1},... | collective-permute-start | bytes 614408 | tf_op jit(solution)/shard_map/ppermute | solution.py:180
  17.9 6.9 %collective-permute-start.9 = (bf16[32,2048]{1,0:T(8,128)(2,1)S(1)}, bf16[32,2048]{1,0:T(8,128)(2,1)S(1)}, u32[]{:S(2)}, u32[]{:S(2)}) collective-permute-start(bf16[32,2048]{1,0:T(8,128)(2,1)S(1)} %pad_maximum_fusion.14), channel_id=1, source_target_pairs={{0,1},{1,0},{2,6},{3,7},{4,5},{5,4},{6,2},{7,3},{8,9},{9,8},{10,14... | collective-permute-start | bytes 393224 | tf_op jit(solution)/shard_map/ppermute | solution.py:180
  23.2 8.0 %collective-permute-start.2 = (bf16[64,3200]{1,0:T(8,128)(2,1)S(1)}, bf16[64,3200]{1,0:T(8,128)(2,1)S(1)}, u32[]{:S(2)}, u32[]{:S(2)}) collective-permute-start(bf16[64,3200]{1,0:T(8,128)(2,1)S(1)} %pad_maximum_fusion.7), channel_id=1, source_target_pairs={{0,1},{1,0},{2,6},{3,7},{4,5},{5,4},{6,2},{7,3},{8,9},{9,8},{10,14... | collective-permute-start | bytes 1228808 | tf_op jit(solution)/shard_map/ppermute | solution.py:180
  24.8 16.3 %collective-permute-start.10 = (bf16[64,2048]{1,0:T(8,128)(2,1)S(1)}, bf16[64,2048]{1,0:T(8,128)(2,1)S(1)}, u32[]{:S(2)}, u32[]{:S(2)}) collective-permute-start(bf16[64,2048]{1,0:T(8,128)(2,1)S(1)} %pad_maximum_fusion.10), channel_id=1, source_target_pairs={{0,16},{1,17},{2,18},{3,19},{4,20},{5,21},{6,22},{7,23},{8,24},{9,... | collective-permute-start | bytes 786440 | tf_op jit(solution)/shard_map/ppermute | solution.py:180
  28.3 13.2 %collective-permute-start.7 = (bf16[32,5120]{1,0:T(8,128)(2,1)S(1)}, bf16[32,5120]{1,0:T(8,128)(2,1)S(1)}, u32[]{:S(2)}, u32[]{:S(2)}) collective-permute-start(bf16[32,5120]{1,0:T(8,128)(2,1)S(1)} %pad_maximum_fusion.9), channel_id=1, source_target_pairs={{0,8},{1,9},{2,10},{3,11},{4,12},{5,13},{6,14},{7,15},{8,0},{9,1},... | collective-permute-start | bytes 983048 | tf_op jit(solution)/shard_map/ppermute | solution.py:180
  31.2 15.4 %collective-permute-start.3 = (bf16[128,3200]{1,0:T(8,128)(2,1)S(1)}, bf16[128,3200]{1,0:T(8,128)(2,1)S(1)}, u32[]{:S(2)}, u32[]{:S(2)}) collective-permute-start(bf16[128,3200]{1,0:T(8,128)(2,1)S(1)} %pad_maximum_fusion.2.refs_0_), channel_id=1, source_target_pairs={{0,4},{1,5},{2,3},{3,2},{4,0},{5,1},{6,7},{7,6},{8,12},{9,13},{10,... | collective-permute-start | bytes 2457608 | tf_op jit(solution)/shard_map/ppermute | solution.py:180
  33.3 13.3 %copy-start.4 = (bf16[5120,1,2,768]{3,2,1,0:T(2,128)(2,1)S(1)}, bf16[5120,1,2,768]{3,2,1,0:T(2,128)(2,1)}, u32[]{:S(2)}) copy-start(bf16[5120,1,2,768]{3,2,1,0:T(2,128)(2,1)} %param.12) | copy-start | bytes 47185924
  41.5 16.0 %collective-permute-start.11 = (bf16[64,5120]{1,0:T(8,128)(2,1)S(1)}, bf16[64,5120]{1,0:T(8,128)(2,1)S(1)}, u32[]{:S(2)}, u32[]{:S(2)}) collective-permute-start(bf16[64,5120]{1,0:T(8,128)(2,1)S(1)} %pad_maximum_fusion.4), channel_id=1, source_target_pairs={{0,1},{1,0},{2,6},{3,7},{4,5},{5,4},{6,2},{7,3},{8,9},{9,8},{10,14... | collective-permute-start | bytes 1966088 | tf_op jit(solution)/shard_map/ppermute | solution.py:180
  43.1 15.2 %collective-permute-start.4 = (bf16[128,3200]{1,0:T(8,128)(2,1)S(1)}, bf16[128,3200]{1,0:T(8,128)(2,1)S(1)}, u32[]{:S(2)}, u32[]{:S(2)}) collective-permute-start(bf16[128,3200]{1,0:T(8,128)(2,1)S(1)} %pad_maximum_fusion.2.refs_0_), channel_id=1, source_target_pairs={{0,2},{1,3},{2,0},{3,1},{4,6},{5,7},{6,4},{7,5},{8,10},{9,11},{10,... | collective-permute-start | bytes 2457608 | tf_op jit(solution)/shard_map/ppermute | solution.py:180
  43.1 14.4 %collective-permute-start.12 = (bf16[128,2048]{1,0:T(8,128)(2,1)S(1)}, bf16[128,2048]{1,0:T(8,128)(2,1)}, u32[]{:S(2)}, u32[]{:S(2)}) collective-permute-start(bf16[128,2048]{1,0:T(8,128)(2,1)S(1)} %pad_maximum_fusion.6.refs_0_), channel_id=1, source_target_pairs={{0,8},{1,9},{2,10},{3,11},{4,12},{5,13},{6,14},{7,15},{8,0},{9,1},... | collective-permute-start | bytes 1572872 | tf_op jit(solution)/shard_map/ppermute | solution.py:180
  46.6 12.7 %collective-permute-start.5 = (bf16[128,3200]{1,0:T(8,128)(2,1)S(1)}, bf16[128,3200]{1,0:T(8,128)(2,1)S(1)}, u32[]{:S(2)}, u32[]{:S(2)}) collective-permute-start(bf16[128,3200]{1,0:T(8,128)(2,1)S(1)} %collective-permute-done.3.refs_1_), channel_id=1, source_target_pairs={{0,2},{1,3},{2,0},{3,1},{4,6},{5,7},{6,4},{7,5},{8,10},{9,11},{10,... | collective-permute-start | bytes 2457608 | tf_op jit(solution)/shard_map/ppermute | solution.py:180
  53.3 11.8 %collective-permute-start.15 = (bf16[128,2048]{1,0:T(8,128)(2,1)S(1)}, bf16[128,2048]{1,0:T(8,128)(2,1)}, u32[]{:S(2)}, u32[]{:S(2)}) collective-permute-start(bf16[128,2048]{1,0:T(8,128)(2,1)S(1)} %pad_maximum_fusion.6.refs_0_), channel_id=1, source_target_pairs={{0,2},{1,3},{2,0},{3,1},{4,6},{5,7},{6,4},{7,5},{8,10},{9,11},{10,... | collective-permute-start | bytes 1572872 | tf_op jit(solution)/shard_map/ppermute | solution.py:180
  57.5 7.6 %collective-permute-start.16 = (bf16[128,2048]{1,0:T(8,128)(2,1)}, bf16[128,2048]{1,0:T(8,128)(2,1)}, u32[]{:S(2)}, u32[]{:S(2)}) collective-permute-start(bf16[128,2048]{1,0:T(8,128)(2,1)} %collective-permute-done.12.refs_1_), channel_id=1, source_target_pairs={{0,2},{1,3},{2,0},{3,1},{4,6},{5,7},{6,4},{7,5},{8,10},{9,11},{10,... | collective-permute-start | bytes 1572872 | tf_op jit(solution)/shard_map/ppermute | solution.py:180
  57.6 17.8 %collective-permute-start.13 = (bf16[128,5120]{1,0:T(8,128)(2,1)S(1)}, bf16[128,5120]{1,0:T(8,128)(2,1)}, u32[]{:S(2)}, u32[]{:S(2)}) collective-permute-start(bf16[128,5120]{1,0:T(8,128)(2,1)S(1)} %pad_maximum_fusion.1.refs_0_), channel_id=1, source_target_pairs={{0,4},{1,5},{2,3},{3,2},{4,0},{5,1},{6,7},{7,6},{8,12},{9,13},{10,... | collective-permute-start | bytes 3932168 | tf_op jit(solution)/shard_map/ppermute | solution.py:180
  58.2 17.9 %collective-permute-start.14 = (bf16[128,5120]{1,0:T(8,128)(2,1)S(1)}, bf16[128,5120]{1,0:T(8,128)(2,1)}, u32[]{:S(2)}, u32[]{:S(2)}) collective-permute-start(bf16[128,5120]{1,0:T(8,128)(2,1)S(1)} %pad_maximum_fusion.1.refs_0_), channel_id=1, source_target_pairs={{0,2},{1,3},{2,0},{3,1},{4,6},{5,7},{6,4},{7,5},{8,10},{9,11},{10,... | collective-permute-start | bytes 3932168 | tf_op jit(solution)/shard_map/ppermute | solution.py:180
  58.4 0.9 copy-start
  59.3 0.9 copy-start.2
  60.9 1.3 copy-start.8
  60.9 1.4 copy-start.1
  60.9 1.4 copy-start.3
  60.9 7.4 %slice-start.2 = ((s8[7864320]{0:T(1024)(128)(4,1)}), s8[4194304]{0:T(1024)(128)(4,1)S(1)}, s32[]{:S(2)}) async-start(s8[7864320]{0:T(1024)(128)(4,1)} %bitcast.76), calls=%async_computation.2 | async-start | bytes 8388608
  62.4 6.0 %slice-start.3 = ((s8[7864320]{0:T(1024)(128)(4,1)}), s8[3670016]{0:T(1024)(128)(4,1)S(1)}, s32[]{:S(2)}) async-start(s8[7864320]{0:T(1024)(128)(4,1)} %bitcast.76), calls=%async_computation.3 | async-start | bytes 7340032
  65.1 5.2 %slice-start = ((s8[7864320]{0:T(1024)(128)(4,1)}), s8[4194304]{0:T(1024)(128)(4,1)S(1)}, s32[]{:S(2)}) async-start(s8[7864320]{0:T(1024)(128)(4,1)} %bitcast.74), calls=%async_computation | async-start | bytes 8388608
  68.4 2.0 %slice-start.1 = ((s8[7864320]{0:T(1024)(128)(4,1)}), s8[3670016]{0:T(1024)(128)(4,1)S(1)}, s32[]{:S(2)}) async-start(s8[7864320]{0:T(1024)(128)(4,1)} %bitcast.74), calls=%async_computation.1 | async-start | bytes 7340032
  70.4 5.2 %copy-start.6 = (s32[512]{0:T(512)S(1)}, s32[512]{0:T(512)}, u32[]{:S(2)}) copy-start(s32[512]{0:T(512)} %get-tuple-element.82) | copy-start | bytes 6148
  70.4 5.2 %copy-start.7 = (s32[512]{0:T(512)S(1)}, s32[512]{0:T(512)}, u32[]{:S(2)}) copy-start(s32[512]{0:T(512)} %get-tuple-element.83) | copy-start | bytes 6148
  70.4 5.2 %copy-start.9 = (pred[512]{0:T(512)(128)(4,1)S(1)}, pred[512]{0:T(512)(128)(4,1)}, u32[]{:S(2)}) copy-start(pred[512]{0:T(512)(128)(4,1)} %get-tuple-element.86) | copy-start | bytes 1540
  70.4 5.2 %copy-start.10 = (pred[512]{0:T(512)(128)(4,1)S(1)}, pred[512]{0:T(512)(128)(4,1)}, u32[]{:S(2)}) copy-start(pred[512]{0:T(512)(128)(4,1)} %get-tuple-element.87) | copy-start | bytes 1540
  75.4 3.2 %collective-permute-start.17 = (bf16[128,5120]{1,0:T(8,128)(2,1)}, bf16[128,5120]{1,0:T(8,128)(2,1)S(1)}, u32[]{:S(2)}, u32[]{:S(2)}) collective-permute-start(bf16[128,5120]{1,0:T(8,128)(2,1)} %collective-permute-done.13.refs_1_), channel_id=1, source_target_pairs={{0,2},{1,3},{2,0},{3,1},{4,6},{5,7},{6,4},{7,5},{8,10},{9,11},{10,... | collective-permute-start | bytes 3932168 | tf_op jit(solution)/shard_map/ppermute | solution.py:180
  75.7 10.0 %slice-start.4 = ((s8[7864320]{0:T(1024)(128)(4,1)}), s8[4194304]{0:T(1024)(128)(4,1)S(1)}, s32[]{:S(2)}) async-start(s8[7864320]{0:T(1024)(128)(4,1)} %bitcast.81), calls=%async_computation.4 | async-start | bytes 8388608
  76.1 9.6 %slice-start.5 = ((s8[7864320]{0:T(1024)(128)(4,1)}), s8[3670016]{0:T(1024)(128)(4,1)S(1)}, s32[]{:S(2)}) async-start(s8[7864320]{0:T(1024)(128)(4,1)} %bitcast.81), calls=%async_computation.5 | async-start | bytes 7340032
  91.5 4.0 %collective-permute-start.18 = (bf16[256,2560]{1,0:T(8,128)(2,1)S(1)}, bf16[256,2560]{1,0:T(8,128)(2,1)S(1)}, u32[]{:S(2)}, u32[]{:S(2)}) collective-permute-start(bf16[256,2560]{1,0:T(8,128)(2,1)S(1)} %convolution_convert_fusion.1), channel_id=1, source_target_pairs={{0,2},{1,3},{2,0},{3,1},{4,6},{5,7},{6,4},{7,5},{8,10},{9,11},{10,... | collective-permute-start | bytes 3932168 | tf_op jit(solution)/shard_map/ppermute | solution.py:180
  95.0 3.2 %collective-permute-start.20 = (bf16[256,2688]{1,0:T(8,128)(2,1)S(1)}, bf16[256,2688]{1,0:T(8,128)(2,1)S(1)}, u32[]{:S(2)}, u32[]{:S(2)}) collective-permute-start(bf16[256,2688]{1,0:T(8,128)(2,1)S(1)} %pad_maximum_fusion), channel_id=1, source_target_pairs={{0,2},{1,3},{2,0},{3,1},{4,6},{5,7},{6,4},{7,5},{8,10},{9,11},{10,... | collective-permute-start | bytes 4128776 | tf_op jit(solution)/shard_map/ppermute | solution.py:180
  96.0 16.8 %collective-permute-start.19 = (bf16[128,2560]{1,0:T(8,128)(2,1)S(1)}, bf16[128,2560]{1,0:T(8,128)(2,1)S(1)}, u32[]{:S(2)}, u32[]{:S(2)}) collective-permute-start(bf16[128,2560]{1,0:T(8,128)(2,1)S(1)} %slice.361), channel_id=1, source_target_pairs={{0,8},{1,9},{2,10},{3,11},{4,12},{5,13},{6,14},{7,15},{8,0},{9,1},... | collective-permute-start | bytes 1966088 | tf_op jit(solution)/shard_map/ppermute | solution.py:180
  98.9 14.1 %collective-permute-start.21 = (bf16[128,2688]{1,0:T(8,128)(2,1)S(1)}, bf16[128,2688]{1,0:T(8,128)(2,1)S(1)}, u32[]{:S(2)}, u32[]{:S(2)}) collective-permute-start(bf16[128,2688]{1,0:T(8,128)(2,1)S(1)} %pad_maximum_fusion.3), channel_id=1, source_target_pairs={{0,4},{1,5},{2,3},{3,2},{4,0},{5,1},{6,7},{7,6},{8,12},{9,13},{10,... | collective-permute-start | bytes 2064392 | tf_op jit(solution)/shard_map/ppermute | solution.py:180
  113.3 8.3 %collective-permute-start.22 = (bf16[64,2560]{1,0:T(8,128)(2,1)S(1)}, bf16[64,2560]{1,0:T(8,128)(2,1)S(1)}, u32[]{:S(2)}, u32[]{:S(2)}) collective-permute-start(bf16[64,2560]{1,0:T(8,128)(2,1)S(1)} %slice.363), channel_id=1, source_target_pairs={{0,1},{1,0},{2,6},{3,7},{4,5},{5,4},{6,2},{7,3},{8,9},{9,8},{10,14... | collective-permute-start | bytes 983048 | tf_op jit(solution)/shard_map/ppermute | solution.py:180
  120.1 7.2 %collective-permute-start.23 = (bf16[64,2688]{1,0:T(8,128)(2,1)S(1)}, bf16[64,2688]{1,0:T(8,128)(2,1)S(1)}, u32[]{:S(2)}, u32[]{:S(2)}) collective-permute-start(bf16[64,2688]{1,0:T(8,128)(2,1)S(1)} %pad_maximum_fusion.8), channel_id=1, source_target_pairs={{0,1},{1,0},{2,6},{3,7},{4,5},{5,4},{6,2},{7,3},{8,9},{9,8},{10,14... | collective-permute-start | bytes 1032200 | tf_op jit(solution)/shard_map/ppermute | solution.py:180
  127.4 9.3 %collective-permute-start.24 = (bf16[32,2560]{1,0:T(8,128)(2,1)S(1)}, bf16[32,2560]{1,0:T(8,128)(2,1)S(1)}, u32[]{:S(2)}, u32[]{:S(2)}) collective-permute-start(bf16[32,2560]{1,0:T(8,128)(2,1)S(1)} %slice.365), channel_id=1, source_target_pairs={{0,4},{1,5},{2,3},{3,2},{4,0},{5,1},{6,7},{7,6},{8,12},{9,13},{10,... | collective-permute-start | bytes 491528 | tf_op jit(solution)/shard_map/ppermute | solution.py:180
  131.8 5.4 %collective-permute-start.25 = (bf16[32,2688]{1,0:T(8,128)(2,1)S(1)}, bf16[32,2688]{1,0:T(8,128)(2,1)S(1)}, u32[]{:S(2)}, u32[]{:S(2)}) collective-permute-start(bf16[32,2688]{1,0:T(8,128)(2,1)S(1)} %pad_maximum_fusion.12), channel_id=1, source_target_pairs={{0,8},{1,9},{2,10},{3,11},{4,12},{5,13},{6,14},{7,15},{8,0},{9,1},... | collective-permute-start | bytes 516104 | tf_op jit(solution)/shard_map/ppermute | solution.py:180
  137.3 7.2 %collective-permute-start.26 = (bf16[16,2560]{1,0:T(8,128)(2,1)S(1)}, bf16[16,2560]{1,0:T(8,128)(2,1)S(1)}, u32[]{:S(2)}, u32[]{:S(2)}) collective-permute-start(bf16[16,2560]{1,0:T(8,128)(2,1)S(1)} %slice.367), channel_id=1, source_target_pairs={{0,16},{1,17},{2,18},{3,19},{4,20},{5,21},{6,22},{7,23},{8,24},{9,... | collective-permute-start | bytes 245768 | tf_op jit(solution)/shard_map/ppermute | solution.py:180
  140.4 6.3 %collective-permute-start.27 = (bf16[16,2688]{1,0:T(8,128)(2,1)S(1)}, bf16[16,2688]{1,0:T(8,128)(2,1)S(1)}, u32[]{:S(2)}, u32[]{:S(2)}) collective-permute-start(bf16[16,2688]{1,0:T(8,128)(2,1)S(1)} %pad_maximum_fusion.16), channel_id=1, source_target_pairs={{0,16},{1,17},{2,18},{3,19},{4,20},{5,21},{6,22},{7,23},{8,24},{9,... | collective-permute-start | bytes 258056 | tf_op jit(solution)/shard_map/ppermute | solution.py:180

commit v3 on v2

--- a/solution.py
+++ b/solution.py
@@ -6,6 +6,7 @@
 from jax.sharding import PartitionSpec as P
 
 LANES = 128
+BRIEF = pl.CostEstimate(flops=1, bytes_accessed=1, transcendentals=0)
 FIRST = (((0,), (0,)), ((), ()))
 LAST = (((1,), (1,)), ((), ()))
 
@@ -265,11 +266,7 @@
         ],
         input_output_aliases={5: 0, 6: 1} if so_far else {},
         compiler_params=pltpu.CompilerParams(vmem_limit_bytes=20 << 20),
-        cost_estimate=pl.CostEstimate(
-            flops=6 * rows * columns * hidden,
-            bytes_accessed=6 * columns * hidden + 4 * rows * columns,
-            transcendentals=0,
-        ),
+        cost_estimate=BRIEF,
     )(inputs, cotangent, gate_grad, up_grad, scaled, *so_far)
 
 
@@ -319,7 +316,7 @@
     for name in "pdq":
         lo, hi = starts[name], starts[name] + sizes[name]
         part = scaled[:, lo:hi] if name in "pd" else grad_out[:, lo:hi]
-        rows[name] = jnp.concatenate([part, routes], axis=1) if name == "p" else part
+        rows[name] = jnp.concatenate([part, routes], axis=1) if name == "d" else part
 
     tips = {}
 
@@ -339,8 +336,12 @@
         return far_high
 
     def make_routes():
-        routes_all = jnp.concatenate([r[:, sizes["p"] :] for r in rows["p"]], axis=0)
-        routes_all = routes_all.astype(jnp.float32)
+        routes_all = jnp.concatenate([block[:, sizes["d"] :] for block in rows["d"]], axis=0)
+        routes_all = jnp.dot(
+            order_matrix(orders["d"], base, tok_dev),
+            routes_all,
+            preferred_element_type=jnp.float32,
+        )
         lane = lax.broadcasted_iota(jnp.int32, routes_all.shape, 1)
         named = (routes_all == expert.astype(jnp.float32)) & (lane < top)
         chosen = jnp.any(named, axis=1, keepdims=True)
@@ -379,25 +380,29 @@
         )
         return picked[kind][0]
 
+    def cut(name, *others):
+        lo, hi = spans[name]
+        return lax.optimization_barrier(after(w_in, *others)[lo:hi, 0])
+
+    halves = {}
     p0 = step("p")
-    q0 = step("q")
-    d0 = step("d")
-    halves = {}
-    halves["r"] = lax.optimization_barrier(after(w_in, p0)[: 5 * unit, 0])
-    halves["s"] = lax.optimization_barrier(after(w_in, q0)[5 * unit :, 0])
+    q0 = step("q", tips["p"])
+    d0 = step("d", tips["q"])
     p1 = step("p")
     d1 = step("d", p0)
     d2 = step("d")
     q1 = step("q", p1)
     p2 = step("p")
-    p3 = step("p")
+    halves["r"] = cut("r", tips["p"], tips["q"])
+    p3 = step("p", halves["r"])
     d3 = step("d", p2)
     q2 = step("q", d2)
-    finish("p")
+    halves["s"] = cut("s", tips["q"], tips["d"])
+    finish("p", halves["s"])
+    q3 = step("q", d3, halves["s"])
+    finish("d")
     named, slot_gates, placings = make_routes()
-    pick_step("p")
-    q3 = step("q", d3)
-    finish("d")
+    pick_step("p", tips["q"])
     inputs = pick_step("d", tips["q"])
     projected = 0.0
     for name in "rs":
@@ -459,8 +464,8 @@
     def sum_step(name, *others):
         keeps, send = sums[name]
         level = (send.shape[0] // tok_dev).bit_length() - 1
-        send = after(send, *others) if others else send
         got = swap(send, orders[name][level])
+        got = after(got, *others) if others else got
         count = send.shape[0] // 2
         at, new, out = 0, [], []
         for keep in keeps:
@@ -473,21 +478,21 @@
         return send
 
     sr = piece_step("r")
-    r4 = sum_step("r")
     ss = piece_step("s", sr)
-    s4 = sum_step("s")
-    r3 = sum_step("r", ss)
-    s3 = sum_step("s", r4)
-    g = grad_step(0, 4 * unit, s4)
-    s2 = sum_step("s", g)
-    r2 = sum_step("r", s3)
-    g = grad_step(4 * unit, 6 * unit, r3)
-    s1 = sum_step("s", g)
-    r1 = sum_step("r", s2)
-    g = grad_step(6 * unit, 8 * unit, r2)
-    s0 = sum_step("s", g)
-    r0 = sum_step("r", s1)
-    g = grad_step(8 * unit, 10 * unit, r1)
+    r3 = sum_step("r")
+    s3 = sum_step("s")
+    g1 = grad_step(0, 4 * unit, s3)
+    s2 = sum_step("s", g1)
+    r2 = sum_step("r")
+    g2 = grad_step(4 * unit, 6 * unit, r2)
+    s1 = sum_step("s")
+    r1 = sum_step("r", g2)
+    g3 = grad_step(6 * unit, 8 * unit, r1)
+    s0 = sum_step("s")
+    r0 = sum_step("r", g3)
+    g4 = grad_step(8 * unit, 10 * unit, r0)
+    sum_step("s")
+    sum_step("r", g4)
 
     grad_gates = sums["s"][0][1][:, :top]
     grad_tokens = jnp.concatenate([sums[n][0][0].astype(jnp.bfloat16) for n in "rs"], axis=1)

time: 149 us -> 140 us (0.940)
  waiting for transfers between devices: 44.5 us -> 41.2 us
  starting transfers between devices: 31.2 us -> 28.7 us
  other arithmetic: 5.91 us -> 4.15 us
    ppermute x28, waiting for transfers between devices: 44.5 us -> 41.2 us  [swap(): return lax.ppermute(array, ('expert', 'tensor'), pairs)]
    ppermute x28, starting transfers between devices: 31.2 us -> 28.7 us  [swap(): return lax.ppermute(array, ('expert', 'tensor'), pairs)]
    unnamed x36 -> x30, local copies, waits for them, and re-layouts: 3.5 us -> 2.27 us
  transfers between devices with their start and end apart: 28 -> 28, of which waited for: 14 -> 15; matrix products, arithmetic and copies ran while one was open for 21% -> 20% of each run, Pallas kernels for 16% -> 17%
where the time goes in v3:
time: 140 us
  waiting for transfers between devices  41.2 us (29%)
  Pallas kernels  31.1 us (22%)
  starting transfers between devices  28.7 us (20%)
  local copies, waits for them, and re-layouts  18.1 us (13%)
  matrix products  15 us (11%)
  other arithmetic  4.15 us (3%)
    ppermute x28, waiting for transfers between devices, swap(): return lax.ppermute(array, ('expert', 'tensor'), pairs)  41.2 us
    ppermute x28, starting transfers between devices, swap(): return lax.ppermute(array, ('expert', 'tensor'), pairs)  28.7 us
    pallas_call x4, Pallas kernels, weight_grads(): pl.pallas_call(weight_grad_kernel, grid=(columns // tile,), in_specs=[str...  17.3 us
    squeeze x2, local copies, waits for them, and re-layouts, cut(): return lax.optimization_barrier(after(w_in, *others)[lo:hi, 0])  14.4 us
    pallas_call x3, Pallas kernels, pick(): pl.pallas_call(pick_kernel, grid=(columns // tile,), in_specs=[pl.BlockSp...  13.8 us
    dot_general x2, matrix products, piece_step(): jnp.einsum('rjh,djh->rd', left, halves[name], preferred_element_type=jnp....  5.26 us
    dot_general x2, matrix products, gathered_body(): jnp.einsum('rd,djh->rjh', inputs[:, lo:hi], halves[name], preferred_eleme...  3.7 us
  transfers between devices with their start and end apart: 28, of which 15 were waited for; matrix products, arithmetic and copies ran while one was open for 20% of the time, Pallas kernels for 17%

profile of v3, /device:TPU:0, one launch (start us, length us, event | category | flops | bytes accessed | tf_op | source)
XLA Modules:
  0.0 139.7 jit_solution(16547875295809217809)
XLA Ops:
  0.6 0.9 mul.59
  1.5 1.0 fusion.71
  2.5 4.1 %collective-permute-start.1 = (bf16[16,3072]{1,0:T(8,128)(2,1)S(1)}, bf16[16,3072]{1,0:T(8,128)(2,1)S(1)}, u32[]{:S(2)}, u32[]{:S(2)}) collective-permute-start(bf16[16,3072]{1,0:T(8,128)(2,1)S(1)} %slice.230), channel_id=1, source_target_pairs={{0,16},{1,17},{2,18},{3,19},{4,20},{5,21},{6,22},{7,23},{8,24},{9,... | collective-permute-start | bytes 294920 | tf_op jit(solution)/shard_map/ppermute | solution.py:181
  6.7 0.7 convert_element_type.139
  7.5 0.8 copy.27
  8.4 1.8 %collective-permute-start = (bf16[16,2176]{1,0:T(8,128)(2,1)S(1)}, bf16[16,2176]{1,0:T(8,128)(2,1)S(1)}, u32[]{:S(2)}, u32[]{:S(2)}) collective-permute-start(bf16[16,2176]{1,0:T(8,128)(2,1)S(1)} %pad_maximum_fusion.16), channel_id=1, source_target_pairs={{0,4},{1,5},{2,3},{3,2},{4,0},{5,1},{6,7},{7,6},{8,12},{9,13},{10,... | collective-permute-start | bytes 208904 | tf_op jit(solution)/shard_map/ppermute | solution.py:181
  10.2 2.5 %collective-permute-done = bf16[16,2176]{1,0:T(8,128)(2,1)S(1)} collective-permute-done((bf16[16,2176]{1,0:T(8,128)(2,1)S(1)}, bf16[16,2176]{1,0:T(8,128)(2,1)S(1)}, u32[]{:S(2)}, u32[]{:S(2)}) %collective-permute-start) | collective-permute-done | bytes 69664 | tf_op jit(solution)/shard_map/ppermute | solution.py:181
  12.7 3.1 %collective-permute-done.1 = bf16[16,3072]{1,0:T(8,128)(2,1)S(1)} collective-permute-done((bf16[16,3072]{1,0:T(8,128)(2,1)S(1)}, bf16[16,3072]{1,0:T(8,128)(2,1)S(1)}, u32[]{:S(2)}, u32[]{:S(2)}) %collective-permute-start.1) | collective-permute-done | bytes 98336 | tf_op jit(solution)/shard_map/ppermute | solution.py:181
  15.9 1.7 %collective-permute-start.2 = (bf16[32,2176]{1,0:T(8,128)(2,1)S(1)}, bf16[32,2176]{1,0:T(8,128)(2,1)S(1)}, u32[]{:S(2)}, u32[]{:S(2)}) collective-permute-start(bf16[32,2176]{1,0:T(8,128)(2,1)S(1)} %pad_maximum_fusion.14), channel_id=1, source_target_pairs={{0,1},{1,0},{2,6},{3,7},{4,5},{5,4},{6,2},{7,3},{8,9},{9,8},{10,14... | collective-permute-start | bytes 417800 | tf_op jit(solution)/shard_map/ppermute | solution.py:181
  17.7 0.9 collective-permute-done.9
  18.6 2.3 %collective-permute-done.2 = bf16[32,2176]{1,0:T(8,128)(2,1)S(1)} collective-permute-done((bf16[32,2176]{1,0:T(8,128)(2,1)S(1)}, bf16[32,2176]{1,0:T(8,128)(2,1)S(1)}, u32[]{:S(2)}, u32[]{:S(2)}) %collective-permute-start.2) | collective-permute-done | bytes 139296 | tf_op jit(solution)/shard_map/ppermute | solution.py:181
  21.0 7.5 %collective-permute-done.4 = bf16[32,3072]{1,0:T(8,128)(2,1)S(1)} collective-permute-done((bf16[32,3072]{1,0:T(8,128)(2,1)S(1)}, bf16[32,3072]{1,0:T(8,128)(2,1)S(1)}, u32[]{:S(2)}, u32[]{:S(2)}) %collective-permute-start.4) | collective-permute-done | bytes 196640 | tf_op jit(solution)/shard_map/ppermute | solution.py:181
  28.7 7.8 %slice_bitcast_fusion = bf16[2560,2,768]{2,1,0:T(2,128)(2,1)} fusion(bf16[5120,1,2,768]{3,2,1,0:T(2,128)(2,1)} %param.12), kind=kLoop, calls=%fused_computation.2 | loop fusion | bytes 15728640 | tf_op jit(solution)/shard_map/squeeze | solution.py:385
  37.2 1.5 %collective-permute-start.11 = (bf16[64,5120]{1,0:T(8,128)(2,1)S(1)}, bf16[64,5120]{1,0:T(8,128)(2,1)S(1)}, u32[]{:S(2)}, u32[]{:S(2)}) collective-permute-start(bf16[64,5120]{1,0:T(8,128)(2,1)S(1)} %pad_maximum_fusion.4), channel_id=1, source_target_pairs={{0,1},{1,0},{2,6},{3,7},{4,5},{5,4},{6,2},{7,3},{8,9},{9,8},{10,14... | collective-permute-start | bytes 1966088 | tf_op jit(solution)/shard_map/ppermute | solution.py:181
  38.7 2.1 %collective-permute-start.6 = (bf16[128,2176]{1,0:T(8,128)(2,1)S(1)}, bf16[128,2176]{1,0:T(8,128)(2,1)S(1)}, u32[]{:S(2)}, u32[]{:S(2)}) collective-permute-start(bf16[128,2176]{1,0:T(8,128)(2,1)S(1)} %pad_maximum_fusion.6.refs_0_), channel_id=1, source_target_pairs={{0,8},{1,9},{2,10},{3,11},{4,12},{5,13},{6,14},{7,15},{8,0},{9,1},... | collective-permute-start | bytes 1671176 | tf_op jit(solution)/shard_map/ppermute | solution.py:181
  41.0 0.9 collective-permute-start.14
  41.9 6.6 %slice_bitcast_fusion.1 = bf16[2560,2,768]{2,1,0:T(2,128)(2,1)} fusion(bf16[5120,1,2,768]{3,2,1,0:T(2,128)(2,1)S(1)} %copy-done.6), kind=kLoop, calls=%fused_computation.3 | loop fusion | bytes 15728640 | tf_op jit(solution)/shard_map/squeeze | solution.py:385
  48.5 5.5 %collective-permute-done.6.refs_1_ = bf16[128,2176]{1,0:T(8,128)(2,1)S(1)} collective-permute-done((bf16[128,2176]{1,0:T(8,128)(2,1)S(1)}, bf16[128,2176]{1,0:T(8,128)(2,1)S(1)}, u32[]{:S(2)}, u32[]{:S(2)}) %collective-permute-start.6) | collective-permute-done | bytes 557088 | tf_op jit(solution)/shard_map/ppermute | solution.py:181
  54.1 1.0 collective-permute-start.12
  55.1 1.1 collective-permute-start.16
  58.3 1.3 collective-permute-done.16.refs_3_
  59.6 5.0 %shard_map.102.refs_4_ = bf16[208,5120]{1,0:T(8,128)(2,1)S(1)} custom-call(bf16[208,512]{1,0:T(8,128)(2,1)S(1)} %get-tuple-element.46.place, bf16[128,3072]{1,0:T(8,128)(2,1)S(1)} %pad_maximum_fusion.2.refs_0_, bf16[128,3072]{1,0:T(8,128)(2,1)} %collective-permute-done.14.refs_1_, bf16[128,3072]{1,0:T(8,128)(2,1)S(1)} %collective-permute-done.15.refs_2_, ...), custom_call_target="tpu_custom_call" | custom-call | flops 654311424 | bytes 4423680 | tf_op jit(solution)/shard_map/pallas_call | solution.py:215
  64.6 1.8 %shard_map.103.inputs = bf16[208,5120]{1,0:T(8,128)(2,1)S(1)} custom-call(bf16[208,512]{1,0:T(8,128)(2,1)S(1)} %convolution_convert_fusion.2.place, bf16[128,2176]{1,0:T(8,128)(2,1)S(1)} %pad_maximum_fusion.6.refs_0_, bf16[128,2176]{1,0:T(8,128)(2,1)S(1)} %copy-done.3, bf16[128,2176]{1,0:T(8,128)(2,1)S(1)} %copy-done.1, ...), custom_call_target="tpu_custom_call", output_to_operand_aliasing={{}: (5, {})} | custom-call | flops 436207616 | bytes 2949120 | tf_op jit(solution)/shard_map/pallas_call | solution.py:215
  66.4 1.8 %fusion.4 = f32[208,2,768]{2,0,1:T(8,128)S(1)} fusion(bf16[2560,2,768]{2,1,0:T(2,128)(2,1)S(1)} %bitcast.77, bf16[208,5120]{1,0:T(8,128)(2,1)S(1)} %shard_map.103.inputs), kind=kOutput, calls=%fused_computation.6 | convolution fusion | flops 1635778560 | bytes 10207232 | tf_op jit(solution)/shard_map/rd,djh->rjh/dot_general | solution.py:410
  68.6 1.9 %fusion.22 = f32[208,2,768]{2,0,1:T(8,128)S(1)} fusion(f32[208,2,768]{2,0,1:T(8,128)S(1)} %fusion.4, bf16[2560,2,768]{2,1,0:T(2,128)(2,1)S(1)} %bitcast.75, bf16[208,5120]{1,0:T(8,128)(2,1)S(1)} %shard_map.103.inputs), kind=kOutput, calls=%fused_computation.29 | convolution fusion | flops 1636098048 | bytes 11485184 | tf_op jit(solution)/shard_map/rd,djh->rjh/dot_general | solution.py:410
  70.4 1.4 %collective-permute-done.12.refs_1_ = bf16[128,5120]{1,0:T(8,128)(2,1)} collective-permute-done((bf16[128,5120]{1,0:T(8,128)(2,1)S(1)}, bf16[128,5120]{1,0:T(8,128)(2,1)}, u32[]{:S(2)}, u32[]{:S(2)}) %collective-permute-start.12) | collective-permute-done | bytes 1310752 | tf_op jit(solution)/shard_map/ppermute | solution.py:181
  72.5 2.6 %collective-permute-done.17.refs_3_ = bf16[128,5120]{1,0:T(8,128)(2,1)S(1)} collective-permute-done((bf16[128,5120]{1,0:T(8,128)(2,1)}, bf16[128,5120]{1,0:T(8,128)(2,1)S(1)}, u32[]{:S(2)}, u32[]{:S(2)}) %collective-permute-start.17) | collective-permute-done | bytes 1310752 | tf_op jit(solution)/shard_map/ppermute | solution.py:181
  75.1 7.0 %shard_map.104.cotangent = bf16[208,5120]{1,0:T(8,128)(2,1)S(1)} custom-call(bf16[208,512]{1,0:T(8,128)(2,1)S(1)} %get-tuple-element.46.place, bf16[128,5120]{1,0:T(8,128)(2,1)S(1)} %pad_maximum_fusion.1.refs_0_, bf16[128,5120]{1,0:T(8,128)(2,1)} %collective-permute-done.12.refs_1_, bf16[128,5120]{1,0:T(8,128)(2,1)} %collective-permute-done.13.refs_2_, ...), custom_call_target="tpu_custom_call" | custom-call | flops 1090519040 | bytes 7372800 | tf_op jit(solution)/shard_map/pallas_call | solution.py:215
  82.2 2.1 %multiply_convert_fusion.2 = (bf16[208,768]{1,0:T(8,128)(2,1)S(1)}, bf16[208,768]{1,0:T(8,128)(2,1)S(1)}, bf16[208]{0:T(256)(128)(2,1)S(1)}, bf16[208,768]{1,0:T(8,128)(2,1)S(1)}) fusion(f32[208,2,768]{2,0,1:T(8,128)S(1)} %fusion.22, f32[208]{0:T(256)S(1)} %bitcast.83, bf16[208,5120]{1,0:T(8,128)(2,1)S(1)} %shard_map.104.cotangent, ...), kind=kOutput, calls=%fused_computation.78 | convolution fusion | flops 1638813440 | bytes 12231904 | tf_op jit(solution)/shard_map/dot_general | solution.py:416
  84.3 2.6 %fusion.19 = bf16[208,2560]{1,0:T(8,128)(2,1)S(1)} fusion(bf16[2560,2,768]{2,1,0:T(2,128)(2,1)S(1)} %bitcast.75, bf16[208,1,768]{2,0,1:T(8,128)(2,1)S(1)} %bitcast.70, bf16[208,1,768]{2,0,1:T(8,128)(2,1)S(1)} %bitcast.68), kind=kOutput, calls=%fused_computation.17 | convolution fusion | flops 1636630528 | bytes 9568256 | tf_op jit(solution)/shard_map/rjh,djh->rd/dot_general | solution.py:446
  88.1 2.6 %fusion.16 = bf16[208,2560]{1,0:T(8,128)(2,1)S(1)} fusion(bf16[208,2,768]{2,0,1:T(8,128)(2,1)S(1)} %pad_maximum_fusion.5, bf16[2560,2,768]{2,1,0:T(2,128)(2,1)S(1)} %bitcast.77), kind=kOutput, calls=%fused_computation.16 | convolution fusion | flops 1636311040 | bytes 9568256 | tf_op jit(solution)/shard_map/rjh,djh->rd/dot_general | solution.py:446
  92.5 1.8 %collective-permute-start.19 = (bf16[128,2560]{1,0:T(8,128)(2,1)S(1)}, bf16[128,2560]{1,0:T(8,128)(2,1)S(1)}, u32[]{:S(2)}, u32[]{:S(2)}) collective-permute-start(bf16[128,2560]{1,0:T(8,128)(2,1)S(1)} %slice.358), channel_id=1, source_target_pairs={{0,8},{1,9},{2,10},{3,11},{4,12},{5,13},{6,14},{7,15},{8,0},{9,1},... | collective-permute-start | bytes 1966088 | tf_op jit(solution)/shard_map/ppermute | solution.py:181
  95.4 1.0 collective-permute-start.24
  96.4 6.2 %shard_map.105 = (bf16[5120,2,768]{2,1,0:T(2,128)(2,1)}, bf16[5120,768]{1,0:T(8,128)(2,1)}) custom-call(bf16[208,5120]{1,0:T(8,128)(2,1)S(1)} %shard_map.103.inputs, bf16[208,5120]{1,0:T(8,128)(2,1)S(1)} %shard_map.104.cotangent, bf16[208,768]{1,0:T(8,128)(2,1)S(1)} %get-tuple-element.62.gate_grad, bf16[208,768]{1,0:T(8,128)(2,1)S(1)} %get-tuple-element.79.up_grad, ...), custom_call_target="tpu_custom_call" | custom-call | flops 1 | bytes 1 | tf_op jit(solution)/shard_map/pallas_call | solution.py:255
  102.6 6.8 %collective-permute-done.19 = bf16[128,2560]{1,0:T(8,128)(2,1)S(1)} collective-permute-done((bf16[128,2560]{1,0:T(8,128)(2,1)S(1)}, bf16[128,2560]{1,0:T(8,128)(2,1)S(1)}, u32[]{:S(2)}, u32[]{:S(2)}) %collective-permute-start.19) | collective-permute-done | bytes 655392 | tf_op jit(solution)/shard_map/ppermute | solution.py:181
  109.5 2.2 %collective-permute-start.20 = (bf16[64,2560]{1,0:T(8,128)(2,1)S(1)}, bf16[64,2560]{1,0:T(8,128)(2,1)S(1)}, u32[]{:S(2)}, u32[]{:S(2)}) collective-permute-start(bf16[64,2560]{1,0:T(8,128)(2,1)S(1)} %slice.360), channel_id=1, source_target_pairs={{0,1},{1,0},{2,6},{3,7},{4,5},{5,4},{6,2},{7,3},{8,9},{9,8},{10,14... | collective-permute-start | bytes 983048 | tf_op jit(solution)/shard_map/ppermute | solution.py:181
  112.1 3.7 %shard_map.106 = (bf16[5120,2,768]{2,1,0:T(2,128)(2,1)}, bf16[5120,768]{1,0:T(8,128)(2,1)}) custom-call(bf16[208,5120]{1,0:T(8,128)(2,1)S(1)} %shard_map.103.inputs, bf16[208,5120]{1,0:T(8,128)(2,1)S(1)} %shard_map.104.cotangent, bf16[208,768]{1,0:T(8,128)(2,1)S(1)} %get-tuple-element.62.gate_grad, ...), custom_call_target="tpu_custom_call", output_to_operand_aliasing={{0}: (5, {}), {1}: (6, {})} | custom-call | flops 1 | bytes 1 | tf_op jit(solution)/shard_map/pallas_call | solution.py:255
  115.8 1.0 collective-permute-done.20
  116.9 0.8 collective-permute-start.22
  117.7 3.7 %shard_map.107 = (bf16[5120,2,768]{2,1,0:T(2,128)(2,1)}, bf16[5120,768]{1,0:T(8,128)(2,1)}) custom-call(bf16[208,5120]{1,0:T(8,128)(2,1)S(1)} %shard_map.103.inputs, bf16[208,5120]{1,0:T(8,128)(2,1)S(1)} %shard_map.104.cotangent, bf16[208,768]{1,0:T(8,128)(2,1)S(1)} %get-tuple-element.62.gate_grad, ...), custom_call_target="tpu_custom_call", output_to_operand_aliasing={{0}: (5, {}), {1}: (6, {})} | custom-call | flops 1 | bytes 1 | tf_op jit(solution)/shard_map/pallas_call | solution.py:255
  121.4 0.8 collective-permute-done.25
  122.4 1.8 %collective-permute-start.26 = (bf16[32,2688]{1,0:T(8,128)(2,1)S(1)}, bf16[32,2688]{1,0:T(8,128)(2,1)S(1)}, u32[]{:S(2)}, u32[]{:S(2)}) collective-permute-start(bf16[32,2688]{1,0:T(8,128)(2,1)S(1)} %pad_maximum_fusion.12), channel_id=1, source_target_pairs={{0,8},{1,9},{2,10},{3,11},{4,12},{5,13},{6,14},{7,15},{8,0},{9,1},... | collective-permute-start | bytes 516104 | tf_op jit(solution)/shard_map/ppermute | solution.py:181
  124.2 3.9 %collective-permute-start.23 = (bf16[16,2560]{1,0:T(8,128)(2,1)S(1)}, bf16[16,2560]{1,0:T(8,128)(2,1)S(1)}, u32[]{:S(2)}, u32[]{:S(2)}) collective-permute-start(bf16[16,2560]{1,0:T(8,128)(2,1)S(1)} %slice.364), channel_id=1, source_target_pairs={{0,16},{1,17},{2,18},{3,19},{4,20},{5,21},{6,22},{7,23},{8,24},{9,... | collective-permute-start | bytes 245768 | tf_op jit(solution)/shard_map/ppermute | solution.py:181
  128.1 3.7 %shard_map.108 = (bf16[5120,2,768]{2,1,0:T(2,128)(2,1)}, bf16[5120,768]{1,0:T(8,128)(2,1)}) custom-call(bf16[208,5120]{1,0:T(8,128)(2,1)S(1)} %shard_map.103.inputs, bf16[208,5120]{1,0:T(8,128)(2,1)S(1)} %shard_map.104.cotangent, bf16[208,768]{1,0:T(8,128)(2,1)S(1)} %get-tuple-element.62.gate_grad, ...), custom_call_target="tpu_custom_call", output_to_operand_aliasing={{0}: (5, {}), {1}: (6, {})} | custom-call | flops 1 | bytes 1 | tf_op jit(solution)/shard_map/pallas_call | solution.py:255
  131.9 1.7 %collective-permute-start.27 = (bf16[16,2688]{1,0:T(8,128)(2,1)S(1)}, bf16[16,2688]{1,0:T(8,128)(2,1)S(1)}, u32[]{:S(2)}, u32[]{:S(2)}) collective-permute-start(bf16[16,2688]{1,0:T(8,128)(2,1)S(1)} %pad_maximum_fusion.15), channel_id=1, source_target_pairs={{0,16},{1,17},{2,18},{3,19},{4,20},{5,21},{6,22},{7,23},{8,24},{9,... | collective-permute-start | bytes 258056 | tf_op jit(solution)/shard_map/ppermute | solution.py:181
  133.6 4.7 %collective-permute-done.27 = bf16[16,2688]{1,0:T(8,128)(2,1)S(1)} collective-permute-done((bf16[16,2688]{1,0:T(8,128)(2,1)S(1)}, bf16[16,2688]{1,0:T(8,128)(2,1)S(1)}, u32[]{:S(2)}, u32[]{:S(2)}) %collective-permute-start.27) | collective-permute-done | bytes 86048 | tf_op jit(solution)/shard_map/ppermute | solution.py:181
  138.3 0.7 copy.32
  139.0 0.7 pad_maximum_fusion.13
  (135 shorter events, 9.4 us)
Async XLA Ops:
  0.6 18.0 %copy-start.7 = (bf16[16,5120]{1,0:T(8,128)(2,1)S(1)}, bf16[16,5120]{1,0:T(8,128)(2,1)}, u32[]{:S(2)}) copy-start(bf16[16,5120]{1,0:T(8,128)(2,1)} %param.11) | copy-start | bytes 491524
  2.5 13.3 %collective-permute-start.1 = (bf16[16,3072]{1,0:T(8,128)(2,1)S(1)}, bf16[16,3072]{1,0:T(8,128)(2,1)S(1)}, u32[]{:S(2)}, u32[]{:S(2)}) collective-permute-start(bf16[16,3072]{1,0:T(8,128)(2,1)S(1)} %slice.230), channel_id=1, source_target_pairs={{0,16},{1,17},{2,18},{3,19},{4,20},{5,21},{6,22},{7,23},{8,24},{9,... | collective-permute-start | bytes 294920 | tf_op jit(solution)/shard_map/ppermute | solution.py:181
  6.6 12.0 %collective-permute-start.9 = (bf16[16,5120]{1,0:T(8,128)(2,1)}, bf16[16,5120]{1,0:T(8,128)(2,1)S(1)}, u32[]{:S(2)}, u32[]{:S(2)}) collective-permute-start(bf16[16,5120]{1,0:T(8,128)(2,1)} %param.11), channel_id=1, source_target_pairs={{0,16},{1,17},{2,18},{3,19},{4,20},{5,21},{6,22},{7,23},{8,24},{9,... | collective-permute-start | bytes 491528 | tf_op jit(solution)/shard_map/ppermute | solution.py:181
  8.4 4.4 %collective-permute-start = (bf16[16,2176]{1,0:T(8,128)(2,1)S(1)}, bf16[16,2176]{1,0:T(8,128)(2,1)S(1)}, u32[]{:S(2)}, u32[]{:S(2)}) collective-permute-start(bf16[16,2176]{1,0:T(8,128)(2,1)S(1)} %pad_maximum_fusion.16), channel_id=1, source_target_pairs={{0,4},{1,5},{2,3},{3,2},{4,0},{5,1},{6,7},{7,6},{8,12},{9,13},{10,... | collective-permute-start | bytes 208904 | tf_op jit(solution)/shard_map/ppermute | solution.py:181
  15.9 5.1 %collective-permute-start.2 = (bf16[32,2176]{1,0:T(8,128)(2,1)S(1)}, bf16[32,2176]{1,0:T(8,128)(2,1)S(1)}, u32[]{:S(2)}, u32[]{:S(2)}) collective-permute-start(bf16[32,2176]{1,0:T(8,128)(2,1)S(1)} %pad_maximum_fusion.14), channel_id=1, source_target_pairs={{0,1},{1,0},{2,6},{3,7},{4,5},{5,4},{6,2},{7,3},{8,9},{9,8},{10,14... | collective-permute-start | bytes 417800 | tf_op jit(solution)/shard_map/ppermute | solution.py:181
  17.6 10.9 %collective-permute-start.4 = (bf16[32,3072]{1,0:T(8,128)(2,1)S(1)}, bf16[32,3072]{1,0:T(8,128)(2,1)S(1)}, u32[]{:S(2)}, u32[]{:S(2)}) collective-permute-start(bf16[32,3072]{1,0:T(8,128)(2,1)S(1)} %pad_maximum_fusion.11), channel_id=1, source_target_pairs={{0,8},{1,9},{2,10},{3,11},{4,12},{5,13},{6,14},{7,15},{8,0},{9,1},... | collective-permute-start | bytes 589832 | tf_op jit(solution)/shard_map/ppermute | solution.py:181
  20.9 15.5 %collective-permute-start.3 = (bf16[64,2176]{1,0:T(8,128)(2,1)S(1)}, bf16[64,2176]{1,0:T(8,128)(2,1)S(1)}, u32[]{:S(2)}, u32[]{:S(2)}) collective-permute-start(bf16[64,2176]{1,0:T(8,128)(2,1)S(1)} %pad_maximum_fusion.10), channel_id=1, source_target_pairs={{0,16},{1,17},{2,18},{3,19},{4,20},{5,21},{6,22},{7,23},{8,24},{9,... | collective-permute-start | bytes 835592 | tf_op jit(solution)/shard_map/ppermute | solution.py:181
  28.5 8.6 %collective-permute-start.10 = (bf16[32,5120]{1,0:T(8,128)(2,1)S(1)}, bf16[32,5120]{1,0:T(8,128)(2,1)S(1)}, u32[]{:S(2)}, u32[]{:S(2)}) collective-permute-start(bf16[32,5120]{1,0:T(8,128)(2,1)S(1)} %pad_maximum_fusion.9), channel_id=1, source_target_pairs={{0,8},{1,9},{2,10},{3,11},{4,12},{5,13},{6,14},{7,15},{8,0},{9,1},... | collective-permute-start | bytes 983048 | tf_op jit(solution)/shard_map/ppermute | solution.py:181
  28.5 10.1 %collective-permute-start.5 = (bf16[64,3072]{1,0:T(8,128)(2,1)S(1)}, bf16[64,3072]{1,0:T(8,128)(2,1)S(1)}, u32[]{:S(2)}, u32[]{:S(2)}) collective-permute-start(bf16[64,3072]{1,0:T(8,128)(2,1)S(1)} %pad_maximum_fusion.7), channel_id=1, source_target_pairs={{0,1},{1,0},{2,6},{3,7},{4,5},{5,4},{6,2},{7,3},{8,9},{9,8},{10,14... | collective-permute-start | bytes 1179656 | tf_op jit(solution)/shard_map/ppermute | solution.py:181
  28.7 13.2 %copy-start.6 = (bf16[5120,1,2,768]{3,2,1,0:T(2,128)(2,1)S(1)}, bf16[5120,1,2,768]{3,2,1,0:T(2,128)(2,1)}, u32[]{:S(2)}) copy-start(bf16[5120,1,2,768]{3,2,1,0:T(2,128)(2,1)} %param.12) | copy-start | bytes 47185924
  37.2 16.8 %collective-permute-start.11 = (bf16[64,5120]{1,0:T(8,128)(2,1)S(1)}, bf16[64,5120]{1,0:T(8,128)(2,1)S(1)}, u32[]{:S(2)}, u32[]{:S(2)}) collective-permute-start(bf16[64,5120]{1,0:T(8,128)(2,1)S(1)} %pad_maximum_fusion.4), channel_id=1, source_target_pairs={{0,1},{1,0},{2,6},{3,7},{4,5},{5,4},{6,2},{7,3},{8,9},{9,8},{10,14... | collective-permute-start | bytes 1966088 | tf_op jit(solution)/shard_map/ppermute | solution.py:181
  38.6 15.3 %collective-permute-start.7 = (bf16[128,2176]{1,0:T(8,128)(2,1)S(1)}, bf16[128,2176]{1,0:T(8,128)(2,1)S(1)}, u32[]{:S(2)}, u32[]{:S(2)}) collective-permute-start(bf16[128,2176]{1,0:T(8,128)(2,1)S(1)} %pad_maximum_fusion.6.refs_0_), channel_id=1, source_target_pairs={{0,2},{1,3},{2,0},{3,1},{4,6},{5,7},{6,4},{7,5},{8,10},{9,11},{10,... | collective-permute-start | bytes 1671176 | tf_op jit(solution)/shard_map/ppermute | solution.py:181
  38.7 15.3 %collective-permute-start.6 = (bf16[128,2176]{1,0:T(8,128)(2,1)S(1)}, bf16[128,2176]{1,0:T(8,128)(2,1)S(1)}, u32[]{:S(2)}, u32[]{:S(2)}) collective-permute-start(bf16[128,2176]{1,0:T(8,128)(2,1)S(1)} %pad_maximum_fusion.6.refs_0_), channel_id=1, source_target_pairs={{0,8},{1,9},{2,10},{3,11},{4,12},{5,13},{6,14},{7,15},{8,0},{9,1},... | collective-permute-start | bytes 1671176 | tf_op jit(solution)/shard_map/ppermute | solution.py:181
  40.8 17.5 %collective-permute-start.15 = (bf16[128,3072]{1,0:T(8,128)(2,1)S(1)}, bf16[128,3072]{1,0:T(8,128)(2,1)S(1)}, u32[]{:S(2)}, u32[]{:S(2)}) collective-permute-start(bf16[128,3072]{1,0:T(8,128)(2,1)S(1)} %pad_maximum_fusion.2.refs_0_), channel_id=1, source_target_pairs={{0,2},{1,3},{2,0},{3,1},{4,6},{5,7},{6,4},{7,5},{8,10},{9,11},{10,... | collective-permute-start | bytes 2359304 | tf_op jit(solution)/shard_map/ppermute | solution.py:181
  41.0 14.1 %collective-permute-start.14 = (bf16[128,3072]{1,0:T(8,128)(2,1)S(1)}, bf16[128,3072]{1,0:T(8,128)(2,1)}, u32[]{:S(2)}, u32[]{:S(2)}) collective-permute-start(bf16[128,3072]{1,0:T(8,128)(2,1)S(1)} %pad_maximum_fusion.2.refs_0_), channel_id=1, source_target_pairs={{0,4},{1,5},{2,3},{3,2},{4,0},{5,1},{6,7},{7,6},{8,12},{9,13},{10,... | collective-permute-start | bytes 2359304 | tf_op jit(solution)/shard_map/ppermute | solution.py:181
  53.9 2.6 %copy-start.2 = (bf16[128,2176]{1,0:T(8,128)(2,1)}, bf16[128,2176]{1,0:T(8,128)(2,1)S(1)}, u32[]{:S(2)}) copy-start(bf16[128,2176]{1,0:T(8,128)(2,1)S(1)} %collective-permute-done.6.refs_1_) | copy-start | bytes 1671172
  53.9 2.2 %collective-permute-start.8 = (bf16[128,2176]{1,0:T(8,128)(2,1)S(1)}, bf16[128,2176]{1,0:T(8,128)(2,1)S(1)}, u32[]{:S(2)}, u32[]{:S(2)}) collective-permute-start(bf16[128,2176]{1,0:T(8,128)(2,1)S(1)} %collective-permute-done.6.refs_1_), channel_id=1, source_target_pairs={{0,2},{1,3},{2,0},{3,1},{4,6},{5,7},{6,4},{7,5},{8,10},{9,11},{10,... | collective-permute-start | bytes 1671176 | tf_op jit(solution)/shard_map/ppermute | solution.py:181
  54.0 2.6 %copy-start = (bf16[128,2176]{1,0:T(8,128)(2,1)}, bf16[128,2176]{1,0:T(8,128)(2,1)S(1)}, u32[]{:S(2)}) copy-start(bf16[128,2176]{1,0:T(8,128)(2,1)S(1)} %collective-permute-done.7.refs_2_) | copy-start | bytes 1671172
  54.1 17.8 %collective-permute-start.12 = (bf16[128,5120]{1,0:T(8,128)(2,1)S(1)}, bf16[128,5120]{1,0:T(8,128)(2,1)}, u32[]{:S(2)}, u32[]{:S(2)}) collective-permute-start(bf16[128,5120]{1,0:T(8,128)(2,1)S(1)} %pad_maximum_fusion.1.refs_0_), channel_id=1, source_target_pairs={{0,4},{1,5},{2,3},{3,2},{4,0},{5,1},{6,7},{7,6},{8,12},{9,13},{10,... | collective-permute-start | bytes 3932168 | tf_op jit(solution)/shard_map/ppermute | solution.py:181
  55.1 17.5 %collective-permute-start.13 = (bf16[128,5120]{1,0:T(8,128)(2,1)S(1)}, bf16[128,5120]{1,0:T(8,128)(2,1)}, u32[]{:S(2)}, u32[]{:S(2)}) collective-permute-start(bf16[128,5120]{1,0:T(8,128)(2,1)S(1)} %pad_maximum_fusion.1.refs_0_), channel_id=1, source_target_pairs={{0,2},{1,3},{2,0},{3,1},{4,6},{5,7},{6,4},{7,5},{8,10},{9,11},{10,... | collective-permute-start | bytes 3932168 | tf_op jit(solution)/shard_map/ppermute | solution.py:181
  55.1 4.5 %collective-permute-start.16 = (bf16[128,3072]{1,0:T(8,128)(2,1)}, bf16[128,3072]{1,0:T(8,128)(2,1)}, u32[]{:S(2)}, u32[]{:S(2)}) collective-permute-start(bf16[128,3072]{1,0:T(8,128)(2,1)} %collective-permute-done.14.refs_1_), channel_id=1, source_target_pairs={{0,2},{1,3},{2,0},{3,1},{4,6},{5,7},{6,4},{7,5},{8,10},{9,11},{10,... | collective-permute-start | bytes 2359304 | tf_op jit(solution)/shard_map/ppermute | solution.py:181
  56.2 0.8 copy-start.4
  57.8 8.6 %slice-start.2 = ((s8[7864320]{0:T(1024)(128)(4,1)}), s8[4194304]{0:T(1024)(128)(4,1)S(1)}, s32[]{:S(2)}) async-start(s8[7864320]{0:T(1024)(128)(4,1)} %bitcast.76), calls=%async_computation.2 | async-start | bytes 8388608
  58.2 6.3 %copy-start.1 = (bf16[128,2176]{1,0:T(8,128)(2,1)S(1)}, bf16[128,2176]{1,0:T(8,128)(2,1)}, u32[]{:S(2)}) copy-start(bf16[128,2176]{1,0:T(8,128)(2,1)} %copy-done) | copy-start | bytes 1671172
  58.2 6.3 %copy-start.3 = (bf16[128,2176]{1,0:T(8,128)(2,1)S(1)}, bf16[128,2176]{1,0:T(8,128)(2,1)}, u32[]{:S(2)}) copy-start(bf16[128,2176]{1,0:T(8,128)(2,1)} %copy-done.2) | copy-start | bytes 1671172
  58.2 6.3 %copy-start.5 = (bf16[128,2176]{1,0:T(8,128)(2,1)S(1)}, bf16[128,2176]{1,0:T(8,128)(2,1)}, u32[]{:S(2)}) copy-start(bf16[128,2176]{1,0:T(8,128)(2,1)} %copy-done.4) | copy-start | bytes 1671172
  58.2 8.2 %slice-start.3 = ((s8[7864320]{0:T(1024)(128)(4,1)}), s8[3670016]{0:T(1024)(128)(4,1)S(1)}, s32[]{:S(2)}) async-start(s8[7864320]{0:T(1024)(128)(4,1)} %bitcast.76), calls=%async_computation.3 | async-start | bytes 7340032
  64.6 3.7 %slice-start = ((s8[7864320]{0:T(1024)(128)(4,1)}), s8[4194304]{0:T(1024)(128)(4,1)S(1)}, s32[]{:S(2)}) async-start(s8[7864320]{0:T(1024)(128)(4,1)} %bitcast.74), calls=%async_computation | async-start | bytes 8388608
  66.4 2.1 %slice-start.1 = ((s8[7864320]{0:T(1024)(128)(4,1)}), s8[3670016]{0:T(1024)(128)(4,1)S(1)}, s32[]{:S(2)}) async-start(s8[7864320]{0:T(1024)(128)(4,1)} %bitcast.74), calls=%async_computation.1 | async-start | bytes 7340032
  71.9 3.2 %collective-permute-start.17 = (bf16[128,5120]{1,0:T(8,128)(2,1)}, bf16[128,5120]{1,0:T(8,128)(2,1)S(1)}, u32[]{:S(2)}, u32[]{:S(2)}) collective-permute-start(bf16[128,5120]{1,0:T(8,128)(2,1)} %collective-permute-done.12.refs_1_), channel_id=1, source_target_pairs={{0,2},{1,3},{2,0},{3,1},{4,6},{5,7},{6,4},{7,5},{8,10},{9,11},{10,... | collective-permute-start | bytes 3932168 | tf_op jit(solution)/shard_map/ppermute | solution.py:181
  72.1 10.0 %slice-start.4 = ((s8[7864320]{0:T(1024)(128)(4,1)}), s8[4194304]{0:T(1024)(128)(4,1)S(1)}, s32[]{:S(2)}) async-start(s8[7864320]{0:T(1024)(128)(4,1)} %bitcast.81), calls=%async_computation.4 | async-start | bytes 8388608
  72.5 9.6 %slice-start.5 = ((s8[7864320]{0:T(1024)(128)(4,1)}), s8[3670016]{0:T(1024)(128)(4,1)S(1)}, s32[]{:S(2)}) async-start(s8[7864320]{0:T(1024)(128)(4,1)} %bitcast.81), calls=%async_computation.5 | async-start | bytes 7340032
  87.9 4.0 %collective-permute-start.18 = (bf16[256,2560]{1,0:T(8,128)(2,1)S(1)}, bf16[256,2560]{1,0:T(8,128)(2,1)S(1)}, u32[]{:S(2)}, u32[]{:S(2)}) collective-permute-start(bf16[256,2560]{1,0:T(8,128)(2,1)S(1)} %convolution_convert_fusion.1), channel_id=1, source_target_pairs={{0,2},{1,3},{2,0},{3,1},{4,6},{5,7},{6,4},{7,5},{8,10},{9,11},{10,... | collective-permute-start | bytes 3932168 | tf_op jit(solution)/shard_map/ppermute | solution.py:181
  91.4 3.2 %collective-permute-start.21 = (bf16[256,2688]{1,0:T(8,128)(2,1)S(1)}, bf16[256,2688]{1,0:T(8,128)(2,1)S(1)}, u32[]{:S(2)}, u32[]{:S(2)}) collective-permute-start(bf16[256,2688]{1,0:T(8,128)(2,1)S(1)} %pad_maximum_fusion), channel_id=1, source_target_pairs={{0,2},{1,3},{2,0},{3,1},{4,6},{5,7},{6,4},{7,5},{8,10},{9,11},{10,... | collective-permute-start | bytes 4128776 | tf_op jit(solution)/shard_map/ppermute | solution.py:181
  92.5 16.8 %collective-permute-start.19 = (bf16[128,2560]{1,0:T(8,128)(2,1)S(1)}, bf16[128,2560]{1,0:T(8,128)(2,1)S(1)}, u32[]{:S(2)}, u32[]{:S(2)}) collective-permute-start(bf16[128,2560]{1,0:T(8,128)(2,1)S(1)} %slice.358), channel_id=1, source_target_pairs={{0,8},{1,9},{2,10},{3,11},{4,12},{5,13},{6,14},{7,15},{8,0},{9,1},... | collective-permute-start | bytes 1966088 | tf_op jit(solution)/shard_map/ppermute | solution.py:181
  95.4 16.3 %collective-permute-start.24 = (bf16[128,2688]{1,0:T(8,128)(2,1)S(1)}, bf16[128,2688]{1,0:T(8,128)(2,1)S(1)}, u32[]{:S(2)}, u32[]{:S(2)}) collective-permute-start(bf16[128,2688]{1,0:T(8,128)(2,1)S(1)} %pad_maximum_fusion.3), channel_id=1, source_target_pairs={{0,4},{1,5},{2,3},{3,2},{4,0},{5,1},{6,7},{7,6},{8,12},{9,13},{10,... | collective-permute-start | bytes 2064392 | tf_op jit(solution)/shard_map/ppermute | solution.py:181
  109.5 7.3 %collective-permute-start.20 = (bf16[64,2560]{1,0:T(8,128)(2,1)S(1)}, bf16[64,2560]{1,0:T(8,128)(2,1)S(1)}, u32[]{:S(2)}, u32[]{:S(2)}) collective-permute-start(bf16[64,2560]{1,0:T(8,128)(2,1)S(1)} %slice.360), channel_id=1, source_target_pairs={{0,1},{1,0},{2,6},{3,7},{4,5},{5,4},{6,2},{7,3},{8,9},{9,8},{10,14... | collective-permute-start | bytes 983048 | tf_op jit(solution)/shard_map/ppermute | solution.py:181
  112.0 10.3 %collective-permute-start.25 = (bf16[64,2688]{1,0:T(8,128)(2,1)S(1)}, bf16[64,2688]{1,0:T(8,128)(2,1)S(1)}, u32[]{:S(2)}, u32[]{:S(2)}) collective-permute-start(bf16[64,2688]{1,0:T(8,128)(2,1)S(1)} %pad_maximum_fusion.8), channel_id=1, source_target_pairs={{0,1},{1,0},{2,6},{3,7},{4,5},{5,4},{6,2},{7,3},{8,9},{9,8},{10,14... | collective-permute-start | bytes 1032200 | tf_op jit(solution)/shard_map/ppermute | solution.py:181
  116.9 7.3 %collective-permute-start.22 = (bf16[32,2560]{1,0:T(8,128)(2,1)S(1)}, bf16[32,2560]{1,0:T(8,128)(2,1)S(1)}, u32[]{:S(2)}, u32[]{:S(2)}) collective-permute-start(bf16[32,2560]{1,0:T(8,128)(2,1)S(1)} %slice.362), channel_id=1, source_target_pairs={{0,4},{1,5},{2,3},{3,2},{4,0},{5,1},{6,7},{7,6},{8,12},{9,13},{10,... | collective-permute-start | bytes 491528 | tf_op jit(solution)/shard_map/ppermute | solution.py:181
  122.4 9.5 %collective-permute-start.26 = (bf16[32,2688]{1,0:T(8,128)(2,1)S(1)}, bf16[32,2688]{1,0:T(8,128)(2,1)S(1)}, u32[]{:S(2)}, u32[]{:S(2)}) collective-permute-start(bf16[32,2688]{1,0:T(8,128)(2,1)S(1)} %pad_maximum_fusion.12), channel_id=1, source_target_pairs={{0,8},{1,9},{2,10},{3,11},{4,12},{5,13},{6,14},{7,15},{8,0},{9,1},... | collective-permute-start | bytes 516104 | tf_op jit(solution)/shard_map/ppermute | solution.py:181
  124.2 7.6 %collective-permute-start.23 = (bf16[16,2560]{1,0:T(8,128)(2,1)S(1)}, bf16[16,2560]{1,0:T(8,128)(2,1)S(1)}, u32[]{:S(2)}, u32[]{:S(2)}) collective-permute-start(bf16[16,2560]{1,0:T(8,128)(2,1)S(1)} %slice.364), channel_id=1, source_target_pairs={{0,16},{1,17},{2,18},{3,19},{4,20},{5,21},{6,22},{7,23},{8,24},{9,... | collective-permute-start | bytes 245768 | tf_op jit(solution)/shard_map/ppermute | solution.py:181
  131.9 6.4 %collective-permute-start.27 = (bf16[16,2688]{1,0:T(8,128)(2,1)S(1)}, bf16[16,2688]{1,0:T(8,128)(2,1)S(1)}, u32[]{:S(2)}, u32[]{:S(2)}) collective-permute-start(bf16[16,2688]{1,0:T(8,128)(2,1)S(1)} %pad_maximum_fusion.15), channel_id=1, source_target_pairs={{0,16},{1,17},{2,18},{3,19},{4,20},{5,21},{6,22},{7,23},{8,24},{9,... | collective-permute-start | bytes 258056 | tf_op jit(solution)/shard_map/ppermute | solution.py:181

commit v4 on v3

--- a/solution.py
+++ b/solution.py
@@ -209,7 +209,7 @@
 
 def pick(place, blocks, columns, start, width, so_far):
     slots, tokens = place.shape
-    tile = 512
+    tile = 1024
     first = start // tile
     kept = [pl.BlockSpec(memory_space=pl.ANY)] * len(so_far)
     return pl.pallas_call(
@@ -221,12 +221,8 @@
         out_specs=pl.BlockSpec((slots, tile), lambda i: (0, first + i)),
         out_shape=jax.ShapeDtypeStruct((slots, width), jnp.bfloat16),
         input_output_aliases={5: 0} if so_far else {},
-        compiler_params=pltpu.CompilerParams(vmem_limit_bytes=16 << 20),
-        cost_estimate=pl.CostEstimate(
-            flops=2 * slots * columns * tokens,
-            bytes_accessed=2 * columns * (tokens + slots),
-            transcendentals=0,
-        ),
+        compiler_params=pltpu.CompilerParams(vmem_limit_bytes=7 << 20),
+        cost_estimate=BRIEF,
     )(place, *blocks, *so_far)
 
 

time: 140 us -> 138 us (0.986)
  Pallas kernels: 31.1 us -> 27 us
  waiting for transfers between devices: 41.2 us -> 42.9 us
    pallas_call x3, Pallas kernels: 13.8 us -> 9.64 us  [pick(): pl.pallas_call(pick_kernel, grid=(columns // tile,), in_specs=[pl.BlockSp...]
    ppermute x28, waiting for transfers between devices: 41.2 us -> 42.9 us  [swap(): return lax.ppermute(array, ('expert', 'tensor'), pairs)]
  transfers between devices with their start and end apart: 28 -> 28, of which waited for: 15 -> 15; matrix products, arithmetic and copies ran while one was open for 20% -> 20% of each run, Pallas kernels for 17% -> 16%
where the time goes in v4:
time: 138 us; the launch traced here: 137 us
  waiting for transfers between devices  42.9 us (31%)
  starting transfers between devices  28.7 us (21%)
  Pallas kernels  27 us (20%)
  local copies, waits for them, and re-layouts  18.2 us (13%)
  matrix products  15 us (11%)
  other arithmetic  4.15 us (3%)
    ppermute x28, waiting for transfers between devices, swap(): return lax.ppermute(array, ('expert', 'tensor'), pairs)  42.9 us
    ppermute x28, starting transfers between devices, swap(): return lax.ppermute(array, ('expert', 'tensor'), pairs)  28.7 us
    pallas_call x4, Pallas kernels, weight_grads(): pl.pallas_call(weight_grad_kernel, grid=(columns // tile,), in_specs=[str...  17.3 us
    squeeze x2, local copies, waits for them, and re-layouts, cut(): return lax.optimization_barrier(after(w_in, *others)[lo:hi, 0])  14.4 us
    pallas_call x3, Pallas kernels, pick(): pl.pallas_call(pick_kernel, grid=(columns // tile,), in_specs=[pl.BlockSp...  9.64 us
    dot_general x2, matrix products, piece_step(): jnp.einsum('rjh,djh->rd', left, halves[name], preferred_element_type=jnp....  5.26 us
    dot_general x2, matrix products, gathered_body(): jnp.einsum('rd,djh->rjh', inputs[:, lo:hi], halves[name], preferred_eleme...  3.7 us
  transfers between devices with their start and end apart: 28, of which 15 were waited for; matrix products, arithmetic and copies ran while one was open for 20% of the time, Pallas kernels for 16%

profile of v4, /device:TPU:0, one launch (start us, length us, event | category | flops | bytes accessed | tf_op | source)
XLA Modules:
  0.0 137.3 jit_solution(17338991092592712524)
XLA Ops:
  0.6 0.9 mul.59
  1.5 1.0 fusion.71
  2.5 4.1 %collective-permute-start.1 = (bf16[16,3072]{1,0:T(8,128)(2,1)S(1)}, bf16[16,3072]{1,0:T(8,128)(2,1)S(1)}, u32[]{:S(2)}, u32[]{:S(2)}) collective-permute-start(bf16[16,3072]{1,0:T(8,128)(2,1)S(1)} %slice.230), channel_id=1, source_target_pairs={{0,16},{1,17},{2,18},{3,19},{4,20},{5,21},{6,22},{7,23},{8,24},{9,... | collective-permute-start | bytes 294920 | tf_op jit(solution)/shard_map/ppermute | solution.py:181
  6.7 0.7 convert_element_type.139
  7.5 0.8 copy.27
  8.4 1.8 %collective-permute-start = (bf16[16,2176]{1,0:T(8,128)(2,1)S(1)}, bf16[16,2176]{1,0:T(8,128)(2,1)S(1)}, u32[]{:S(2)}, u32[]{:S(2)}) collective-permute-start(bf16[16,2176]{1,0:T(8,128)(2,1)S(1)} %pad_maximum_fusion.16), channel_id=1, source_target_pairs={{0,4},{1,5},{2,3},{3,2},{4,0},{5,1},{6,7},{7,6},{8,12},{9,13},{10,... | collective-permute-start | bytes 208904 | tf_op jit(solution)/shard_map/ppermute | solution.py:181
  10.2 2.5 %collective-permute-done = bf16[16,2176]{1,0:T(8,128)(2,1)S(1)} collective-permute-done((bf16[16,2176]{1,0:T(8,128)(2,1)S(1)}, bf16[16,2176]{1,0:T(8,128)(2,1)S(1)}, u32[]{:S(2)}, u32[]{:S(2)}) %collective-permute-start) | collective-permute-done | bytes 69664 | tf_op jit(solution)/shard_map/ppermute | solution.py:181
  12.7 3.1 %collective-permute-done.1 = bf16[16,3072]{1,0:T(8,128)(2,1)S(1)} collective-permute-done((bf16[16,3072]{1,0:T(8,128)(2,1)S(1)}, bf16[16,3072]{1,0:T(8,128)(2,1)S(1)}, u32[]{:S(2)}, u32[]{:S(2)}) %collective-permute-start.1) | collective-permute-done | bytes 98336 | tf_op jit(solution)/shard_map/ppermute | solution.py:181
  15.9 1.7 %collective-permute-start.2 = (bf16[32,2176]{1,0:T(8,128)(2,1)S(1)}, bf16[32,2176]{1,0:T(8,128)(2,1)S(1)}, u32[]{:S(2)}, u32[]{:S(2)}) collective-permute-start(bf16[32,2176]{1,0:T(8,128)(2,1)S(1)} %pad_maximum_fusion.14), channel_id=1, source_target_pairs={{0,1},{1,0},{2,6},{3,7},{4,5},{5,4},{6,2},{7,3},{8,9},{9,8},{10,14... | collective-permute-start | bytes 417800 | tf_op jit(solution)/shard_map/ppermute | solution.py:181
  17.7 0.9 collective-permute-done.9
  18.6 2.3 %collective-permute-done.2 = bf16[32,2176]{1,0:T(8,128)(2,1)S(1)} collective-permute-done((bf16[32,2176]{1,0:T(8,128)(2,1)S(1)}, bf16[32,2176]{1,0:T(8,128)(2,1)S(1)}, u32[]{:S(2)}, u32[]{:S(2)}) %collective-permute-start.2) | collective-permute-done | bytes 139296 | tf_op jit(solution)/shard_map/ppermute | solution.py:181
  21.0 7.5 %collective-permute-done.4 = bf16[32,3072]{1,0:T(8,128)(2,1)S(1)} collective-permute-done((bf16[32,3072]{1,0:T(8,128)(2,1)S(1)}, bf16[32,3072]{1,0:T(8,128)(2,1)S(1)}, u32[]{:S(2)}, u32[]{:S(2)}) %collective-permute-start.4) | collective-permute-done | bytes 196640 | tf_op jit(solution)/shard_map/ppermute | solution.py:181
  28.7 7.8 %slice_bitcast_fusion = bf16[2560,2,768]{2,1,0:T(2,128)(2,1)} fusion(bf16[5120,1,2,768]{3,2,1,0:T(2,128)(2,1)} %param.12), kind=kLoop, calls=%fused_computation.2 | loop fusion | bytes 15728640 | tf_op jit(solution)/shard_map/squeeze | solution.py:381
  37.2 1.5 %collective-permute-start.11 = (bf16[64,5120]{1,0:T(8,128)(2,1)S(1)}, bf16[64,5120]{1,0:T(8,128)(2,1)S(1)}, u32[]{:S(2)}, u32[]{:S(2)}) collective-permute-start(bf16[64,5120]{1,0:T(8,128)(2,1)S(1)} %pad_maximum_fusion.4), channel_id=1, source_target_pairs={{0,1},{1,0},{2,6},{3,7},{4,5},{5,4},{6,2},{7,3},{8,9},{9,8},{10,14... | collective-permute-start | bytes 1966088 | tf_op jit(solution)/shard_map/ppermute | solution.py:181
  38.7 2.1 %collective-permute-start.6 = (bf16[128,2176]{1,0:T(8,128)(2,1)S(1)}, bf16[128,2176]{1,0:T(8,128)(2,1)S(1)}, u32[]{:S(2)}, u32[]{:S(2)}) collective-permute-start(bf16[128,2176]{1,0:T(8,128)(2,1)S(1)} %pad_maximum_fusion.6.refs_0_), channel_id=1, source_target_pairs={{0,8},{1,9},{2,10},{3,11},{4,12},{5,13},{6,14},{7,15},{8,0},{9,1},... | collective-permute-start | bytes 1671176 | tf_op jit(solution)/shard_map/ppermute | solution.py:181
  41.0 0.9 collective-permute-start.14
  41.9 6.6 %slice_bitcast_fusion.1 = bf16[2560,2,768]{2,1,0:T(2,128)(2,1)} fusion(bf16[5120,1,2,768]{3,2,1,0:T(2,128)(2,1)S(1)} %copy-done.6), kind=kLoop, calls=%fused_computation.3 | loop fusion | bytes 15728640 | tf_op jit(solution)/shard_map/squeeze | solution.py:381
  48.5 5.5 %collective-permute-done.6.refs_1_ = bf16[128,2176]{1,0:T(8,128)(2,1)S(1)} collective-permute-done((bf16[128,2176]{1,0:T(8,128)(2,1)S(1)}, bf16[128,2176]{1,0:T(8,128)(2,1)S(1)}, u32[]{:S(2)}, u32[]{:S(2)}) %collective-permute-start.6) | collective-permute-done | bytes 557088 | tf_op jit(solution)/shard_map/ppermute | solution.py:181
  54.1 1.0 collective-permute-start.12
  55.1 1.1 collective-permute-start.16
  58.3 1.3 collective-permute-done.16.refs_3_
  59.6 3.7 %shard_map.102.refs_4_ = bf16[208,5120]{1,0:T(8,128)(2,1)S(1)} custom-call(bf16[208,512]{1,0:T(8,128)(2,1)S(1)} %get-tuple-element.46.place, bf16[128,3072]{1,0:T(8,128)(2,1)S(1)} %pad_maximum_fusion.2.refs_0_, bf16[128,3072]{1,0:T(8,128)(2,1)} %collective-permute-done.14.refs_1_, bf16[128,3072]{1,0:T(8,128)(2,1)S(1)} %collective-permute-done.15.refs_2_, ...), custom_call_target="tpu_custom_call" | custom-call | flops 1 | bytes 1 | tf_op jit(solution)/shard_map/pallas_call | solution.py:215
  63.4 1.3 shard_map.103.inputs
  64.7 1.8 %fusion.4 = f32[208,2,768]{2,0,1:T(8,128)S(1)} fusion(bf16[2560,2,768]{2,1,0:T(2,128)(2,1)S(1)} %bitcast.77, bf16[208,5120]{1,0:T(8,128)(2,1)S(1)} %shard_map.103.inputs), kind=kOutput, calls=%fused_computation.6 | convolution fusion | flops 1635778560 | bytes 10207232 | tf_op jit(solution)/shard_map/rd,djh->rjh/dot_general | solution.py:406
  66.9 1.9 %fusion.22 = f32[208,2,768]{2,0,1:T(8,128)S(1)} fusion(f32[208,2,768]{2,0,1:T(8,128)S(1)} %fusion.4, bf16[2560,2,768]{2,1,0:T(2,128)(2,1)S(1)} %bitcast.75, bf16[208,5120]{1,0:T(8,128)(2,1)S(1)} %shard_map.103.inputs), kind=kOutput, calls=%fused_computation.29 | convolution fusion | flops 1636098048 | bytes 11485184 | tf_op jit(solution)/shard_map/rd,djh->rjh/dot_general | solution.py:406
  68.8 3.1 %collective-permute-done.12.refs_1_ = bf16[128,5120]{1,0:T(8,128)(2,1)} collective-permute-done((bf16[128,5120]{1,0:T(8,128)(2,1)S(1)}, bf16[128,5120]{1,0:T(8,128)(2,1)}, u32[]{:S(2)}, u32[]{:S(2)}) %collective-permute-start.12) | collective-permute-done | bytes 1310752 | tf_op jit(solution)/shard_map/ppermute | solution.py:181
  72.5 2.6 %collective-permute-done.17.refs_3_ = bf16[128,5120]{1,0:T(8,128)(2,1)S(1)} collective-permute-done((bf16[128,5120]{1,0:T(8,128)(2,1)}, bf16[128,5120]{1,0:T(8,128)(2,1)S(1)}, u32[]{:S(2)}, u32[]{:S(2)}) %collective-permute-start.17) | collective-permute-done | bytes 1310752 | tf_op jit(solution)/shard_map/ppermute | solution.py:181
  75.1 4.7 %shard_map.104.cotangent = bf16[208,5120]{1,0:T(8,128)(2,1)S(1)} custom-call(bf16[208,512]{1,0:T(8,128)(2,1)S(1)} %get-tuple-element.46.place, bf16[128,5120]{1,0:T(8,128)(2,1)S(1)} %pad_maximum_fusion.1.refs_0_, bf16[128,5120]{1,0:T(8,128)(2,1)} %collective-permute-done.12.refs_1_, bf16[128,5120]{1,0:T(8,128)(2,1)} %collective-permute-done.13.refs_2_, ...), custom_call_target="tpu_custom_call" | custom-call | flops 1 | bytes 1 | tf_op jit(solution)/shard_map/pallas_call | solution.py:215
  79.8 2.1 %multiply_convert_fusion.2 = (bf16[208,768]{1,0:T(8,128)(2,1)S(1)}, bf16[208,768]{1,0:T(8,128)(2,1)S(1)}, bf16[208]{0:T(256)(128)(2,1)S(1)}, bf16[208,768]{1,0:T(8,128)(2,1)S(1)}) fusion(f32[208,2,768]{2,0,1:T(8,128)S(1)} %fusion.22, f32[208]{0:T(256)S(1)} %bitcast.83, bf16[208,5120]{1,0:T(8,128)(2,1)S(1)} %shard_map.104.cotangent, ...), kind=kOutput, calls=%fused_computation.78 | convolution fusion | flops 1638813440 | bytes 12231904 | tf_op jit(solution)/shard_map/dot_general | solution.py:412
  81.9 2.6 %fusion.19 = bf16[208,2560]{1,0:T(8,128)(2,1)S(1)} fusion(bf16[2560,2,768]{2,1,0:T(2,128)(2,1)S(1)} %bitcast.75, bf16[208,1,768]{2,0,1:T(8,128)(2,1)S(1)} %bitcast.70, bf16[208,1,768]{2,0,1:T(8,128)(2,1)S(1)} %bitcast.68), kind=kOutput, calls=%fused_computation.17 | convolution fusion | flops 1636630528 | bytes 9568256 | tf_op jit(solution)/shard_map/rjh,djh->rd/dot_general | solution.py:442
  85.8 2.6 %fusion.16 = bf16[208,2560]{1,0:T(8,128)(2,1)S(1)} fusion(bf16[208,2,768]{2,0,1:T(8,128)(2,1)S(1)} %pad_maximum_fusion.5, bf16[2560,2,768]{2,1,0:T(2,128)(2,1)S(1)} %bitcast.77), kind=kOutput, calls=%fused_computation.16 | convolution fusion | flops 1636311040 | bytes 9568256 | tf_op jit(solution)/shard_map/rjh,djh->rd/dot_general | solution.py:442
  90.1 1.8 %collective-permute-start.19 = (bf16[128,2560]{1,0:T(8,128)(2,1)S(1)}, bf16[128,2560]{1,0:T(8,128)(2,1)S(1)}, u32[]{:S(2)}, u32[]{:S(2)}) collective-permute-start(bf16[128,2560]{1,0:T(8,128)(2,1)S(1)} %slice.358), channel_id=1, source_target_pairs={{0,8},{1,9},{2,10},{3,11},{4,12},{5,13},{6,14},{7,15},{8,0},{9,1},... | collective-permute-start | bytes 1966088 | tf_op jit(solution)/shard_map/ppermute | solution.py:181
  93.0 1.0 collective-permute-start.24
  94.0 6.2 %shard_map.105 = (bf16[5120,2,768]{2,1,0:T(2,128)(2,1)}, bf16[5120,768]{1,0:T(8,128)(2,1)}) custom-call(bf16[208,5120]{1,0:T(8,128)(2,1)S(1)} %shard_map.103.inputs, bf16[208,5120]{1,0:T(8,128)(2,1)S(1)} %shard_map.104.cotangent, bf16[208,768]{1,0:T(8,128)(2,1)S(1)} %get-tuple-element.62.gate_grad, bf16[208,768]{1,0:T(8,128)(2,1)S(1)} %get-tuple-element.79.up_grad, ...), custom_call_target="tpu_custom_call" | custom-call | flops 1 | bytes 1 | tf_op jit(solution)/shard_map/pallas_call | solution.py:251
  100.2 6.8 %collective-permute-done.19 = bf16[128,2560]{1,0:T(8,128)(2,1)S(1)} collective-permute-done((bf16[128,2560]{1,0:T(8,128)(2,1)S(1)}, bf16[128,2560]{1,0:T(8,128)(2,1)S(1)}, u32[]{:S(2)}, u32[]{:S(2)}) %collective-permute-start.19) | collective-permute-done | bytes 655392 | tf_op jit(solution)/shard_map/ppermute | solution.py:181
  107.2 2.2 %collective-permute-start.20 = (bf16[64,2560]{1,0:T(8,128)(2,1)S(1)}, bf16[64,2560]{1,0:T(8,128)(2,1)S(1)}, u32[]{:S(2)}, u32[]{:S(2)}) collective-permute-start(bf16[64,2560]{1,0:T(8,128)(2,1)S(1)} %slice.360), channel_id=1, source_target_pairs={{0,1},{1,0},{2,6},{3,7},{4,5},{5,4},{6,2},{7,3},{8,9},{9,8},{10,14... | collective-permute-start | bytes 983048 | tf_op jit(solution)/shard_map/ppermute | solution.py:181
  109.7 3.7 %shard_map.106 = (bf16[5120,2,768]{2,1,0:T(2,128)(2,1)}, bf16[5120,768]{1,0:T(8,128)(2,1)}) custom-call(bf16[208,5120]{1,0:T(8,128)(2,1)S(1)} %shard_map.103.inputs, bf16[208,5120]{1,0:T(8,128)(2,1)S(1)} %shard_map.104.cotangent, bf16[208,768]{1,0:T(8,128)(2,1)S(1)} %get-tuple-element.62.gate_grad, ...), custom_call_target="tpu_custom_call", output_to_operand_aliasing={{0}: (5, {}), {1}: (6, {})} | custom-call | flops 1 | bytes 1 | tf_op jit(solution)/shard_map/pallas_call | solution.py:251
  113.4 1.0 collective-permute-done.20
  114.5 0.8 collective-permute-start.22
  115.4 3.7 %shard_map.107 = (bf16[5120,2,768]{2,1,0:T(2,128)(2,1)}, bf16[5120,768]{1,0:T(8,128)(2,1)}) custom-call(bf16[208,5120]{1,0:T(8,128)(2,1)S(1)} %shard_map.103.inputs, bf16[208,5120]{1,0:T(8,128)(2,1)S(1)} %shard_map.104.cotangent, bf16[208,768]{1,0:T(8,128)(2,1)S(1)} %get-tuple-element.62.gate_grad, ...), custom_call_target="tpu_custom_call", output_to_operand_aliasing={{0}: (5, {}), {1}: (6, {})} | custom-call | flops 1 | bytes 1 | tf_op jit(solution)/shard_map/pallas_call | solution.py:251
  119.1 0.8 collective-permute-done.25
  120.0 1.8 %collective-permute-start.26 = (bf16[32,2688]{1,0:T(8,128)(2,1)S(1)}, bf16[32,2688]{1,0:T(8,128)(2,1)S(1)}, u32[]{:S(2)}, u32[]{:S(2)}) collective-permute-start(bf16[32,2688]{1,0:T(8,128)(2,1)S(1)} %pad_maximum_fusion.12), channel_id=1, source_target_pairs={{0,8},{1,9},{2,10},{3,11},{4,12},{5,13},{6,14},{7,15},{8,0},{9,1},... | collective-permute-start | bytes 516104 | tf_op jit(solution)/shard_map/ppermute | solution.py:181
  121.9 3.9 %collective-permute-start.23 = (bf16[16,2560]{1,0:T(8,128)(2,1)S(1)}, bf16[16,2560]{1,0:T(8,128)(2,1)S(1)}, u32[]{:S(2)}, u32[]{:S(2)}) collective-permute-start(bf16[16,2560]{1,0:T(8,128)(2,1)S(1)} %slice.364), channel_id=1, source_target_pairs={{0,16},{1,17},{2,18},{3,19},{4,20},{5,21},{6,22},{7,23},{8,24},{9,... | collective-permute-start | bytes 245768 | tf_op jit(solution)/shard_map/ppermute | solution.py:181
  125.7 3.7 %shard_map.108 = (bf16[5120,2,768]{2,1,0:T(2,128)(2,1)}, bf16[5120,768]{1,0:T(8,128)(2,1)}) custom-call(bf16[208,5120]{1,0:T(8,128)(2,1)S(1)} %shard_map.103.inputs, bf16[208,5120]{1,0:T(8,128)(2,1)S(1)} %shard_map.104.cotangent, bf16[208,768]{1,0:T(8,128)(2,1)S(1)} %get-tuple-element.62.gate_grad, ...), custom_call_target="tpu_custom_call", output_to_operand_aliasing={{0}: (5, {}), {1}: (6, {})} | custom-call | flops 1 | bytes 1 | tf_op jit(solution)/shard_map/pallas_call | solution.py:251
  129.6 1.7 %collective-permute-start.27 = (bf16[16,2688]{1,0:T(8,128)(2,1)S(1)}, bf16[16,2688]{1,0:T(8,128)(2,1)S(1)}, u32[]{:S(2)}, u32[]{:S(2)}) collective-permute-start(bf16[16,2688]{1,0:T(8,128)(2,1)S(1)} %pad_maximum_fusion.15), channel_id=1, source_target_pairs={{0,16},{1,17},{2,18},{3,19},{4,20},{5,21},{6,22},{7,23},{8,24},{9,... | collective-permute-start | bytes 258056 | tf_op jit(solution)/shard_map/ppermute | solution.py:181
  131.3 4.7 %collective-permute-done.27 = bf16[16,2688]{1,0:T(8,128)(2,1)S(1)} collective-permute-done((bf16[16,2688]{1,0:T(8,128)(2,1)S(1)}, bf16[16,2688]{1,0:T(8,128)(2,1)S(1)}, u32[]{:S(2)}, u32[]{:S(2)}) %collective-permute-start.27) | collective-permute-done | bytes 86048 | tf_op jit(solution)/shard_map/ppermute | solution.py:181
  135.9 0.7 copy.32
  136.6 0.7 pad_maximum_fusion.13
  (135 shorter events, 9.6 us)
Async XLA Ops:
  0.6 18.0 %copy-start.7 = (bf16[16,5120]{1,0:T(8,128)(2,1)S(1)}, bf16[16,5120]{1,0:T(8,128)(2,1)}, u32[]{:S(2)}) copy-start(bf16[16,5120]{1,0:T(8,128)(2,1)} %param.11) | copy-start | bytes 491524
  2.5 13.3 %collective-permute-start.1 = (bf16[16,3072]{1,0:T(8,128)(2,1)S(1)}, bf16[16,3072]{1,0:T(8,128)(2,1)S(1)}, u32[]{:S(2)}, u32[]{:S(2)}) collective-permute-start(bf16[16,3072]{1,0:T(8,128)(2,1)S(1)} %slice.230), channel_id=1, source_target_pairs={{0,16},{1,17},{2,18},{3,19},{4,20},{5,21},{6,22},{7,23},{8,24},{9,... | collective-permute-start | bytes 294920 | tf_op jit(solution)/shard_map/ppermute | solution.py:181
  6.6 12.0 %collective-permute-start.9 = (bf16[16,5120]{1,0:T(8,128)(2,1)}, bf16[16,5120]{1,0:T(8,128)(2,1)S(1)}, u32[]{:S(2)}, u32[]{:S(2)}) collective-permute-start(bf16[16,5120]{1,0:T(8,128)(2,1)} %param.11), channel_id=1, source_target_pairs={{0,16},{1,17},{2,18},{3,19},{4,20},{5,21},{6,22},{7,23},{8,24},{9,... | collective-permute-start | bytes 491528 | tf_op jit(solution)/shard_map/ppermute | solution.py:181
  8.4 4.4 %collective-permute-start = (bf16[16,2176]{1,0:T(8,128)(2,1)S(1)}, bf16[16,2176]{1,0:T(8,128)(2,1)S(1)}, u32[]{:S(2)}, u32[]{:S(2)}) collective-permute-start(bf16[16,2176]{1,0:T(8,128)(2,1)S(1)} %pad_maximum_fusion.16), channel_id=1, source_target_pairs={{0,4},{1,5},{2,3},{3,2},{4,0},{5,1},{6,7},{7,6},{8,12},{9,13},{10,... | collective-permute-start | bytes 208904 | tf_op jit(solution)/shard_map/ppermute | solution.py:181
  15.9 5.1 %collective-permute-start.2 = (bf16[32,2176]{1,0:T(8,128)(2,1)S(1)}, bf16[32,2176]{1,0:T(8,128)(2,1)S(1)}, u32[]{:S(2)}, u32[]{:S(2)}) collective-permute-start(bf16[32,2176]{1,0:T(8,128)(2,1)S(1)} %pad_maximum_fusion.14), channel_id=1, source_target_pairs={{0,1},{1,0},{2,6},{3,7},{4,5},{5,4},{6,2},{7,3},{8,9},{9,8},{10,14... | collective-permute-start | bytes 417800 | tf_op jit(solution)/shard_map/ppermute | solution.py:181
  17.6 10.9 %collective-permute-start.4 = (bf16[32,3072]{1,0:T(8,128)(2,1)S(1)}, bf16[32,3072]{1,0:T(8,128)(2,1)S(1)}, u32[]{:S(2)}, u32[]{:S(2)}) collective-permute-start(bf16[32,3072]{1,0:T(8,128)(2,1)S(1)} %pad_maximum_fusion.11), channel_id=1, source_target_pairs={{0,8},{1,9},{2,10},{3,11},{4,12},{5,13},{6,14},{7,15},{8,0},{9,1},... | collective-permute-start | bytes 589832 | tf_op jit(solution)/shard_map/ppermute | solution.py:181
  20.9 15.5 %collective-permute-start.3 = (bf16[64,2176]{1,0:T(8,128)(2,1)S(1)}, bf16[64,2176]{1,0:T(8,128)(2,1)S(1)}, u32[]{:S(2)}, u32[]{:S(2)}) collective-permute-start(bf16[64,2176]{1,0:T(8,128)(2,1)S(1)} %pad_maximum_fusion.10), channel_id=1, source_target_pairs={{0,16},{1,17},{2,18},{3,19},{4,20},{5,21},{6,22},{7,23},{8,24},{9,... | collective-permute-start | bytes 835592 | tf_op jit(solution)/shard_map/ppermute | solution.py:181
  28.5 8.6 %collective-permute-start.10 = (bf16[32,5120]{1,0:T(8,128)(2,1)S(1)}, bf16[32,5120]{1,0:T(8,128)(2,1)S(1)}, u32[]{:S(2)}, u32[]{:S(2)}) collective-permute-start(bf16[32,5120]{1,0:T(8,128)(2,1)S(1)} %pad_maximum_fusion.9), channel_id=1, source_target_pairs={{0,8},{1,9},{2,10},{3,11},{4,12},{5,13},{6,14},{7,15},{8,0},{9,1},... | collective-permute-start | bytes 983048 | tf_op jit(solution)/shard_map/ppermute | solution.py:181
  28.5 10.1 %collective-permute-start.5 = (bf16[64,3072]{1,0:T(8,128)(2,1)S(1)}, bf16[64,3072]{1,0:T(8,128)(2,1)S(1)}, u32[]{:S(2)}, u32[]{:S(2)}) collective-permute-start(bf16[64,3072]{1,0:T(8,128)(2,1)S(1)} %pad_maximum_fusion.7), channel_id=1, source_target_pairs={{0,1},{1,0},{2,6},{3,7},{4,5},{5,4},{6,2},{7,3},{8,9},{9,8},{10,14... | collective-permute-start | bytes 1179656 | tf_op jit(solution)/shard_map/ppermute | solution.py:181
  28.7 13.2 %copy-start.6 = (bf16[5120,1,2,768]{3,2,1,0:T(2,128)(2,1)S(1)}, bf16[5120,1,2,768]{3,2,1,0:T(2,128)(2,1)}, u32[]{:S(2)}) copy-start(bf16[5120,1,2,768]{3,2,1,0:T(2,128)(2,1)} %param.12) | copy-start | bytes 47185924
  37.2 16.8 %collective-permute-start.11 = (bf16[64,5120]{1,0:T(8,128)(2,1)S(1)}, bf16[64,5120]{1,0:T(8,128)(2,1)S(1)}, u32[]{:S(2)}, u32[]{:S(2)}) collective-permute-start(bf16[64,5120]{1,0:T(8,128)(2,1)S(1)} %pad_maximum_fusion.4), channel_id=1, source_target_pairs={{0,1},{1,0},{2,6},{3,7},{4,5},{5,4},{6,2},{7,3},{8,9},{9,8},{10,14... | collective-permute-start | bytes 1966088 | tf_op jit(solution)/shard_map/ppermute | solution.py:181
  38.6 15.3 %collective-permute-start.7 = (bf16[128,2176]{1,0:T(8,128)(2,1)S(1)}, bf16[128,2176]{1,0:T(8,128)(2,1)S(1)}, u32[]{:S(2)}, u32[]{:S(2)}) collective-permute-start(bf16[128,2176]{1,0:T(8,128)(2,1)S(1)} %pad_maximum_fusion.6.refs_0_), channel_id=1, source_target_pairs={{0,2},{1,3},{2,0},{3,1},{4,6},{5,7},{6,4},{7,5},{8,10},{9,11},{10,... | collective-permute-start | bytes 1671176 | tf_op jit(solution)/shard_map/ppermute | solution.py:181
  38.7 15.3 %collective-permute-start.6 = (bf16[128,2176]{1,0:T(8,128)(2,1)S(1)}, bf16[128,2176]{1,0:T(8,128)(2,1)S(1)}, u32[]{:S(2)}, u32[]{:S(2)}) collective-permute-start(bf16[128,2176]{1,0:T(8,128)(2,1)S(1)} %pad_maximum_fusion.6.refs_0_), channel_id=1, source_target_pairs={{0,8},{1,9},{2,10},{3,11},{4,12},{5,13},{6,14},{7,15},{8,0},{9,1},... | collective-permute-start | bytes 1671176 | tf_op jit(solution)/shard_map/ppermute | solution.py:181
  40.8 17.5 %collective-permute-start.15 = (bf16[128,3072]{1,0:T(8,128)(2,1)S(1)}, bf16[128,3072]{1,0:T(8,128)(2,1)S(1)}, u32[]{:S(2)}, u32[]{:S(2)}) collective-permute-start(bf16[128,3072]{1,0:T(8,128)(2,1)S(1)} %pad_maximum_fusion.2.refs_0_), channel_id=1, source_target_pairs={{0,2},{1,3},{2,0},{3,1},{4,6},{5,7},{6,4},{7,5},{8,10},{9,11},{10,... | collective-permute-start | bytes 2359304 | tf_op jit(solution)/shard_map/ppermute | solution.py:181
  41.0 14.1 %collective-permute-start.14 = (bf16[128,3072]{1,0:T(8,128)(2,1)S(1)}, bf16[128,3072]{1,0:T(8,128)(2,1)}, u32[]{:S(2)}, u32[]{:S(2)}) collective-permute-start(bf16[128,3072]{1,0:T(8,128)(2,1)S(1)} %pad_maximum_fusion.2.refs_0_), channel_id=1, source_target_pairs={{0,4},{1,5},{2,3},{3,2},{4,0},{5,1},{6,7},{7,6},{8,12},{9,13},{10,... | collective-permute-start | bytes 2359304 | tf_op jit(solution)/shard_map/ppermute | solution.py:181
  53.9 2.6 %copy-start.2 = (bf16[128,2176]{1,0:T(8,128)(2,1)}, bf16[128,2176]{1,0:T(8,128)(2,1)S(1)}, u32[]{:S(2)}) copy-start(bf16[128,2176]{1,0:T(8,128)(2,1)S(1)} %collective-permute-done.6.refs_1_) | copy-start | bytes 1671172
  53.9 2.2 %collective-permute-start.8 = (bf16[128,2176]{1,0:T(8,128)(2,1)S(1)}, bf16[128,2176]{1,0:T(8,128)(2,1)S(1)}, u32[]{:S(2)}, u32[]{:S(2)}) collective-permute-start(bf16[128,2176]{1,0:T(8,128)(2,1)S(1)} %collective-permute-done.6.refs_1_), channel_id=1, source_target_pairs={{0,2},{1,3},{2,0},{3,1},{4,6},{5,7},{6,4},{7,5},{8,10},{9,11},{10,... | collective-permute-start | bytes 1671176 | tf_op jit(solution)/shard_map/ppermute | solution.py:181
  54.0 2.6 %copy-start = (bf16[128,2176]{1,0:T(8,128)(2,1)}, bf16[128,2176]{1,0:T(8,128)(2,1)S(1)}, u32[]{:S(2)}) copy-start(bf16[128,2176]{1,0:T(8,128)(2,1)S(1)} %collective-permute-done.7.refs_2_) | copy-start | bytes 1671172
  54.1 17.8 %collective-permute-start.12 = (bf16[128,5120]{1,0:T(8,128)(2,1)S(1)}, bf16[128,5120]{1,0:T(8,128)(2,1)}, u32[]{:S(2)}, u32[]{:S(2)}) collective-permute-start(bf16[128,5120]{1,0:T(8,128)(2,1)S(1)} %pad_maximum_fusion.1.refs_0_), channel_id=1, source_target_pairs={{0,4},{1,5},{2,3},{3,2},{4,0},{5,1},{6,7},{7,6},{8,12},{9,13},{10,... | collective-permute-start | bytes 3932168 | tf_op jit(solution)/shard_map/ppermute | solution.py:181
  55.1 17.5 %collective-permute-start.13 = (bf16[128,5120]{1,0:T(8,128)(2,1)S(1)}, bf16[128,5120]{1,0:T(8,128)(2,1)}, u32[]{:S(2)}, u32[]{:S(2)}) collective-permute-start(bf16[128,5120]{1,0:T(8,128)(2,1)S(1)} %pad_maximum_fusion.1.refs_0_), channel_id=1, source_target_pairs={{0,2},{1,3},{2,0},{3,1},{4,6},{5,7},{6,4},{7,5},{8,10},{9,11},{10,... | collective-permute-start | bytes 3932168 | tf_op jit(solution)/shard_map/ppermute | solution.py:181
  55.1 4.5 %collective-permute-start.16 = (bf16[128,3072]{1,0:T(8,128)(2,1)}, bf16[128,3072]{1,0:T(8,128)(2,1)}, u32[]{:S(2)}, u32[]{:S(2)}) collective-permute-start(bf16[128,3072]{1,0:T(8,128)(2,1)} %collective-permute-done.14.refs_1_), channel_id=1, source_target_pairs={{0,2},{1,3},{2,0},{3,1},{4,6},{5,7},{6,4},{7,5},{8,10},{9,11},{10,... | collective-permute-start | bytes 2359304 | tf_op jit(solution)/shard_map/ppermute | solution.py:181
  56.2 0.8 copy-start.4
  57.8 6.8 %slice-start.2 = ((s8[7864320]{0:T(1024)(128)(4,1)}), s8[4194304]{0:T(1024)(128)(4,1)S(1)}, s32[]{:S(2)}) async-start(s8[7864320]{0:T(1024)(128)(4,1)} %bitcast.76), calls=%async_computation.2 | async-start | bytes 8388608
  58.2 5.1 %copy-start.1 = (bf16[128,2176]{1,0:T(8,128)(2,1)S(1)}, bf16[128,2176]{1,0:T(8,128)(2,1)}, u32[]{:S(2)}) copy-start(bf16[128,2176]{1,0:T(8,128)(2,1)} %copy-done) | copy-start | bytes 1671172
  58.2 5.1 %copy-start.3 = (bf16[128,2176]{1,0:T(8,128)(2,1)S(1)}, bf16[128,2176]{1,0:T(8,128)(2,1)}, u32[]{:S(2)}) copy-start(bf16[128,2176]{1,0:T(8,128)(2,1)} %copy-done.2) | copy-start | bytes 1671172
  58.2 5.1 %copy-start.5 = (bf16[128,2176]{1,0:T(8,128)(2,1)S(1)}, bf16[128,2176]{1,0:T(8,128)(2,1)}, u32[]{:S(2)}) copy-start(bf16[128,2176]{1,0:T(8,128)(2,1)} %copy-done.4) | copy-start | bytes 1671172
  58.2 6.4 %slice-start.3 = ((s8[7864320]{0:T(1024)(128)(4,1)}), s8[3670016]{0:T(1024)(128)(4,1)S(1)}, s32[]{:S(2)}) async-start(s8[7864320]{0:T(1024)(128)(4,1)} %bitcast.76), calls=%async_computation.3 | async-start | bytes 7340032
  63.3 3.2 %slice-start = ((s8[7864320]{0:T(1024)(128)(4,1)}), s8[4194304]{0:T(1024)(128)(4,1)S(1)}, s32[]{:S(2)}) async-start(s8[7864320]{0:T(1024)(128)(4,1)} %bitcast.74), calls=%async_computation | async-start | bytes 8388608
  64.7 2.3 %slice-start.1 = ((s8[7864320]{0:T(1024)(128)(4,1)}), s8[3670016]{0:T(1024)(128)(4,1)S(1)}, s32[]{:S(2)}) async-start(s8[7864320]{0:T(1024)(128)(4,1)} %bitcast.74), calls=%async_computation.1 | async-start | bytes 7340032
  71.9 3.2 %collective-permute-start.17 = (bf16[128,5120]{1,0:T(8,128)(2,1)}, bf16[128,5120]{1,0:T(8,128)(2,1)S(1)}, u32[]{:S(2)}, u32[]{:S(2)}) collective-permute-start(bf16[128,5120]{1,0:T(8,128)(2,1)} %collective-permute-done.12.refs_1_), channel_id=1, source_target_pairs={{0,2},{1,3},{2,0},{3,1},{4,6},{5,7},{6,4},{7,5},{8,10},{9,11},{10,... | collective-permute-start | bytes 3932168 | tf_op jit(solution)/shard_map/ppermute | solution.py:181
  72.1 7.7 %slice-start.4 = ((s8[7864320]{0:T(1024)(128)(4,1)}), s8[4194304]{0:T(1024)(128)(4,1)S(1)}, s32[]{:S(2)}) async-start(s8[7864320]{0:T(1024)(128)(4,1)} %bitcast.81), calls=%async_computation.4 | async-start | bytes 8388608
  72.5 7.3 %slice-start.5 = ((s8[7864320]{0:T(1024)(128)(4,1)}), s8[3670016]{0:T(1024)(128)(4,1)S(1)}, s32[]{:S(2)}) async-start(s8[7864320]{0:T(1024)(128)(4,1)} %bitcast.81), calls=%async_computation.5 | async-start | bytes 7340032
  85.6 4.0 %collective-permute-start.18 = (bf16[256,2560]{1,0:T(8,128)(2,1)S(1)}, bf16[256,2560]{1,0:T(8,128)(2,1)S(1)}, u32[]{:S(2)}, u32[]{:S(2)}) collective-permute-start(bf16[256,2560]{1,0:T(8,128)(2,1)S(1)} %convolution_convert_fusion.1), channel_id=1, source_target_pairs={{0,2},{1,3},{2,0},{3,1},{4,6},{5,7},{6,4},{7,5},{8,10},{9,11},{10,... | collective-permute-start | bytes 3932168 | tf_op jit(solution)/shard_map/ppermute | solution.py:181
  89.1 3.2 %collective-permute-start.21 = (bf16[256,2688]{1,0:T(8,128)(2,1)S(1)}, bf16[256,2688]{1,0:T(8,128)(2,1)S(1)}, u32[]{:S(2)}, u32[]{:S(2)}) collective-permute-start(bf16[256,2688]{1,0:T(8,128)(2,1)S(1)} %pad_maximum_fusion), channel_id=1, source_target_pairs={{0,2},{1,3},{2,0},{3,1},{4,6},{5,7},{6,4},{7,5},{8,10},{9,11},{10,... | collective-permute-start | bytes 4128776 | tf_op jit(solution)/shard_map/ppermute | solution.py:181
  90.1 16.8 %collective-permute-start.19 = (bf16[128,2560]{1,0:T(8,128)(2,1)S(1)}, bf16[128,2560]{1,0:T(8,128)(2,1)S(1)}, u32[]{:S(2)}, u32[]{:S(2)}) collective-permute-start(bf16[128,2560]{1,0:T(8,128)(2,1)S(1)} %slice.358), channel_id=1, source_target_pairs={{0,8},{1,9},{2,10},{3,11},{4,12},{5,13},{6,14},{7,15},{8,0},{9,1},... | collective-permute-start | bytes 1966088 | tf_op jit(solution)/shard_map/ppermute | solution.py:181
  93.0 16.3 %collective-permute-start.24 = (bf16[128,2688]{1,0:T(8,128)(2,1)S(1)}, bf16[128,2688]{1,0:T(8,128)(2,1)S(1)}, u32[]{:S(2)}, u32[]{:S(2)}) collective-permute-start(bf16[128,2688]{1,0:T(8,128)(2,1)S(1)} %pad_maximum_fusion.3), channel_id=1, source_target_pairs={{0,4},{1,5},{2,3},{3,2},{4,0},{5,1},{6,7},{7,6},{8,12},{9,13},{10,... | collective-permute-start | bytes 2064392 | tf_op jit(solution)/shard_map/ppermute | solution.py:181
  107.2 7.3 %collective-permute-start.20 = (bf16[64,2560]{1,0:T(8,128)(2,1)S(1)}, bf16[64,2560]{1,0:T(8,128)(2,1)S(1)}, u32[]{:S(2)}, u32[]{:S(2)}) collective-permute-start(bf16[64,2560]{1,0:T(8,128)(2,1)S(1)} %slice.360), channel_id=1, source_target_pairs={{0,1},{1,0},{2,6},{3,7},{4,5},{5,4},{6,2},{7,3},{8,9},{9,8},{10,14... | collective-permute-start | bytes 983048 | tf_op jit(solution)/shard_map/ppermute | solution.py:181
  109.6 10.3 %collective-permute-start.25 = (bf16[64,2688]{1,0:T(8,128)(2,1)S(1)}, bf16[64,2688]{1,0:T(8,128)(2,1)S(1)}, u32[]{:S(2)}, u32[]{:S(2)}) collective-permute-start(bf16[64,2688]{1,0:T(8,128)(2,1)S(1)} %pad_maximum_fusion.8), channel_id=1, source_target_pairs={{0,1},{1,0},{2,6},{3,7},{4,5},{5,4},{6,2},{7,3},{8,9},{9,8},{10,14... | collective-permute-start | bytes 1032200 | tf_op jit(solution)/shard_map/ppermute | solution.py:181
  114.5 7.3 %collective-permute-start.22 = (bf16[32,2560]{1,0:T(8,128)(2,1)S(1)}, bf16[32,2560]{1,0:T(8,128)(2,1)S(1)}, u32[]{:S(2)}, u32[]{:S(2)}) collective-permute-start(bf16[32,2560]{1,0:T(8,128)(2,1)S(1)} %slice.362), channel_id=1, source_target_pairs={{0,4},{1,5},{2,3},{3,2},{4,0},{5,1},{6,7},{7,6},{8,12},{9,13},{10,... | collective-permute-start | bytes 491528 | tf_op jit(solution)/shard_map/ppermute | solution.py:181
  120.0 9.5 %collective-permute-start.26 = (bf16[32,2688]{1,0:T(8,128)(2,1)S(1)}, bf16[32,2688]{1,0:T(8,128)(2,1)S(1)}, u32[]{:S(2)}, u32[]{:S(2)}) collective-permute-start(bf16[32,2688]{1,0:T(8,128)(2,1)S(1)} %pad_maximum_fusion.12), channel_id=1, source_target_pairs={{0,8},{1,9},{2,10},{3,11},{4,12},{5,13},{6,14},{7,15},{8,0},{9,1},... | collective-permute-start | bytes 516104 | tf_op jit(solution)/shard_map/ppermute | solution.py:181
  121.9 7.6 %collective-permute-start.23 = (bf16[16,2560]{1,0:T(8,128)(2,1)S(1)}, bf16[16,2560]{1,0:T(8,128)(2,1)S(1)}, u32[]{:S(2)}, u32[]{:S(2)}) collective-permute-start(bf16[16,2560]{1,0:T(8,128)(2,1)S(1)} %slice.364), channel_id=1, source_target_pairs={{0,16},{1,17},{2,18},{3,19},{4,20},{5,21},{6,22},{7,23},{8,24},{9,... | collective-permute-start | bytes 245768 | tf_op jit(solution)/shard_map/ppermute | solution.py:181
  129.6 6.4 %collective-permute-start.27 = (bf16[16,2688]{1,0:T(8,128)(2,1)S(1)}, bf16[16,2688]{1,0:T(8,128)(2,1)S(1)}, u32[]{:S(2)}, u32[]{:S(2)}) collective-permute-start(bf16[16,2688]{1,0:T(8,128)(2,1)S(1)} %pad_maximum_fusion.15), channel_id=1, source_target_pairs={{0,16},{1,17},{2,18},{3,19},{4,20},{5,21},{6,22},{7,23},{8,24},{9,... | collective-permute-start | bytes 258056 | tf_op jit(solution)/shard_map/ppermute | solution.py:181

commit v5 on v4

--- a/solution.py
+++ b/solution.py
@@ -477,18 +477,17 @@
     ss = piece_step("s", sr)
     r3 = sum_step("r")
     s3 = sum_step("s")
-    g1 = grad_step(0, 4 * unit, s3)
+    g1 = grad_step(0, 7 * unit, s3)
     s2 = sum_step("s", g1)
     r2 = sum_step("r")
-    g2 = grad_step(4 * unit, 6 * unit, r2)
+    g2 = grad_step(7 * unit, 9 * unit, r2)
     s1 = sum_step("s")
     r1 = sum_step("r", g2)
-    g3 = grad_step(6 * unit, 8 * unit, r1)
+    g3 = grad_step(9 * unit, 10 * unit, r1)
     s0 = sum_step("s")
     r0 = sum_step("r", g3)
-    g4 = grad_step(8 * unit, 10 * unit, r0)
     sum_step("s")
-    sum_step("r", g4)
+    sum_step("r")
 
     grad_gates = sums["s"][0][1][:, :top]
     grad_tokens = jnp.concatenate([sums[n][0][0].astype(jnp.bfloat16) for n in "rs"], axis=1)

time: 138 us -> 135 us (0.978)
  waiting for transfers between devices: 42.9 us -> 38.8 us
  starting transfers between devices: 28.7 us -> 30.7 us
    ppermute x28, waiting for transfers between devices: 42.9 us -> 38.8 us  [swap(): return lax.ppermute(array, ('expert', 'tensor'), pairs)]
    ppermute x28, starting transfers between devices: 28.7 us -> 30.7 us  [swap(): return lax.ppermute(array, ('expert', 'tensor'), pairs)]
    pallas_call x4 -> x3, Pallas kernels: 17.3 us -> 16.2 us  [weight_grads(): pl.pallas_call(weight_grad_kernel, grid=(columns // tile,), in_specs=[str...]
  transfers between devices with their start and end apart: 28 -> 28, of which waited for: 15 -> 17; matrix products, arithmetic and copies ran while one was open for 20% -> 20% of each run, Pallas kernels for 16% -> 16%
where the time goes in v5:
time: 135 us; the launch traced here: 134 us
  waiting for transfers between devices  38.8 us (29%)
  starting transfers between devices  30.7 us (23%)
  Pallas kernels  25.8 us (19%)
  local copies, waits for them, and re-layouts  18.2 us (13%)
  matrix products  15 us (11%)
  other arithmetic  4.14 us (3%)
  between operations  1.35 us (1%)
    ppermute x28, waiting for transfers between devices, swap(): return lax.ppermute(array, ('expert', 'tensor'), pairs)  38.8 us
    ppermute x28, starting transfers between devices, swap(): return lax.ppermute(array, ('expert', 'tensor'), pairs)  30.7 us
    pallas_call x3, Pallas kernels, weight_grads(): pl.pallas_call(weight_grad_kernel, grid=(columns // tile,), in_specs=[str...  16.2 us
    squeeze x2, local copies, waits for them, and re-layouts, cut(): return lax.optimization_barrier(after(w_in, *others)[lo:hi, 0])  14.4 us
    pallas_call x3, Pallas kernels, pick(): pl.pallas_call(pick_kernel, grid=(columns // tile,), in_specs=[pl.BlockSp...  9.59 us
    dot_general x2, matrix products, piece_step(): jnp.einsum('rjh,djh->rd', left, halves[name], preferred_element_type=jnp....  5.26 us
    dot_general x2, matrix products, gathered_body(): jnp.einsum('rd,djh->rjh', inputs[:, lo:hi], halves[name], preferred_eleme...  3.7 us
  transfers between devices with their start and end apart: 28, of which 17 were waited for; matrix products, arithmetic and copies ran while one was open for 20% of the time, Pallas kernels for 16%

profile of v5, /device:TPU:0, one launch (start us, length us, event | category | flops | bytes accessed | tf_op | source)
XLA Modules:
  0.0 133.9 jit_solution(14792254174373210761)
XLA Ops:
  0.6 0.9 mul.59
  1.5 1.0 fusion.71
  2.5 4.1 %collective-permute-start.1 = (bf16[16,3072]{1,0:T(8,128)(2,1)S(1)}, bf16[16,3072]{1,0:T(8,128)(2,1)S(1)}, u32[]{:S(2)}, u32[]{:S(2)}) collective-permute-start(bf16[16,3072]{1,0:T(8,128)(2,1)S(1)} %slice.230), channel_id=1, source_target_pairs={{0,16},{1,17},{2,18},{3,19},{4,20},{5,21},{6,22},{7,23},{8,24},{9,... | collective-permute-start | bytes 294920 | tf_op jit(solution)/shard_map/ppermute | solution.py:181
  6.7 0.7 convert_element_type.139
  7.5 0.8 copy.25
  8.4 1.8 %collective-permute-start = (bf16[16,2176]{1,0:T(8,128)(2,1)S(1)}, bf16[16,2176]{1,0:T(8,128)(2,1)S(1)}, u32[]{:S(2)}, u32[]{:S(2)}) collective-permute-start(bf16[16,2176]{1,0:T(8,128)(2,1)S(1)} %pad_maximum_fusion.16), channel_id=1, source_target_pairs={{0,4},{1,5},{2,3},{3,2},{4,0},{5,1},{6,7},{7,6},{8,12},{9,13},{10,... | collective-permute-start | bytes 208904 | tf_op jit(solution)/shard_map/ppermute | solution.py:181
  10.2 2.5 %collective-permute-done = bf16[16,2176]{1,0:T(8,128)(2,1)S(1)} collective-permute-done((bf16[16,2176]{1,0:T(8,128)(2,1)S(1)}, bf16[16,2176]{1,0:T(8,128)(2,1)S(1)}, u32[]{:S(2)}, u32[]{:S(2)}) %collective-permute-start) | collective-permute-done | bytes 69664 | tf_op jit(solution)/shard_map/ppermute | solution.py:181
  12.7 3.1 %collective-permute-done.1 = bf16[16,3072]{1,0:T(8,128)(2,1)S(1)} collective-permute-done((bf16[16,3072]{1,0:T(8,128)(2,1)S(1)}, bf16[16,3072]{1,0:T(8,128)(2,1)S(1)}, u32[]{:S(2)}, u32[]{:S(2)}) %collective-permute-start.1) | collective-permute-done | bytes 98336 | tf_op jit(solution)/shard_map/ppermute | solution.py:181
  15.9 1.7 %collective-permute-start.2 = (bf16[32,2176]{1,0:T(8,128)(2,1)S(1)}, bf16[32,2176]{1,0:T(8,128)(2,1)S(1)}, u32[]{:S(2)}, u32[]{:S(2)}) collective-permute-start(bf16[32,2176]{1,0:T(8,128)(2,1)S(1)} %pad_maximum_fusion.14), channel_id=1, source_target_pairs={{0,1},{1,0},{2,6},{3,7},{4,5},{5,4},{6,2},{7,3},{8,9},{9,8},{10,14... | collective-permute-start | bytes 417800 | tf_op jit(solution)/shard_map/ppermute | solution.py:181
  17.7 0.9 collective-permute-done.9
  18.6 2.3 %collective-permute-done.2 = bf16[32,2176]{1,0:T(8,128)(2,1)S(1)} collective-permute-done((bf16[32,2176]{1,0:T(8,128)(2,1)S(1)}, bf16[32,2176]{1,0:T(8,128)(2,1)S(1)}, u32[]{:S(2)}, u32[]{:S(2)}) %collective-permute-start.2) | collective-permute-done | bytes 139296 | tf_op jit(solution)/shard_map/ppermute | solution.py:181
  21.0 7.5 %collective-permute-done.4 = bf16[32,3072]{1,0:T(8,128)(2,1)S(1)} collective-permute-done((bf16[32,3072]{1,0:T(8,128)(2,1)S(1)}, bf16[32,3072]{1,0:T(8,128)(2,1)S(1)}, u32[]{:S(2)}, u32[]{:S(2)}) %collective-permute-start.4) | collective-permute-done | bytes 196640 | tf_op jit(solution)/shard_map/ppermute | solution.py:181
  28.7 7.8 %slice_bitcast_fusion = bf16[2560,2,768]{2,1,0:T(2,128)(2,1)} fusion(bf16[5120,1,2,768]{3,2,1,0:T(2,128)(2,1)} %param.12), kind=kLoop, calls=%fused_computation.2 | loop fusion | bytes 15728640 | tf_op jit(solution)/shard_map/squeeze | solution.py:381
  37.2 1.5 %collective-permute-start.11 = (bf16[64,5120]{1,0:T(8,128)(2,1)S(1)}, bf16[64,5120]{1,0:T(8,128)(2,1)S(1)}, u32[]{:S(2)}, u32[]{:S(2)}) collective-permute-start(bf16[64,5120]{1,0:T(8,128)(2,1)S(1)} %pad_maximum_fusion.4), channel_id=1, source_target_pairs={{0,1},{1,0},{2,6},{3,7},{4,5},{5,4},{6,2},{7,3},{8,9},{9,8},{10,14... | collective-permute-start | bytes 1966088 | tf_op jit(solution)/shard_map/ppermute | solution.py:181
  38.7 2.1 %collective-permute-start.6 = (bf16[128,2176]{1,0:T(8,128)(2,1)S(1)}, bf16[128,2176]{1,0:T(8,128)(2,1)S(1)}, u32[]{:S(2)}, u32[]{:S(2)}) collective-permute-start(bf16[128,2176]{1,0:T(8,128)(2,1)S(1)} %pad_maximum_fusion.6.refs_0_), channel_id=1, source_target_pairs={{0,8},{1,9},{2,10},{3,11},{4,12},{5,13},{6,14},{7,15},{8,0},{9,1},... | collective-permute-start | bytes 1671176 | tf_op jit(solution)/shard_map/ppermute | solution.py:181
  41.0 0.9 collective-permute-start.14
  41.9 6.6 %slice_bitcast_fusion.1 = bf16[2560,2,768]{2,1,0:T(2,128)(2,1)} fusion(bf16[5120,1,2,768]{3,2,1,0:T(2,128)(2,1)S(1)} %copy-done.6), kind=kLoop, calls=%fused_computation.3 | loop fusion | bytes 15728640 | tf_op jit(solution)/shard_map/squeeze | solution.py:381
  48.5 5.5 %collective-permute-done.6.refs_1_ = bf16[128,2176]{1,0:T(8,128)(2,1)S(1)} collective-permute-done((bf16[128,2176]{1,0:T(8,128)(2,1)S(1)}, bf16[128,2176]{1,0:T(8,128)(2,1)S(1)}, u32[]{:S(2)}, u32[]{:S(2)}) %collective-permute-start.6) | collective-permute-done | bytes 557088 | tf_op jit(solution)/shard_map/ppermute | solution.py:181
  54.1 1.0 collective-permute-start.12
  55.1 1.1 collective-permute-start.16
  58.3 1.3 collective-permute-done.16.refs_3_
  59.6 3.7 %shard_map.102.refs_4_ = bf16[208,5120]{1,0:T(8,128)(2,1)S(1)} custom-call(bf16[208,512]{1,0:T(8,128)(2,1)S(1)} %get-tuple-element.42.place, bf16[128,3072]{1,0:T(8,128)(2,1)S(1)} %pad_maximum_fusion.2.refs_0_, bf16[128,3072]{1,0:T(8,128)(2,1)} %collective-permute-done.14.refs_1_, bf16[128,3072]{1,0:T(8,128)(2,1)S(1)} %collective-permute-done.15.refs_2_, ...), custom_call_target="tpu_custom_call" | custom-call | flops 1 | bytes 1 | tf_op jit(solution)/shard_map/pallas_call | solution.py:215
  63.3 1.3 shard_map.103.inputs
  64.6 1.8 %fusion.4 = f32[208,2,768]{2,0,1:T(8,128)S(1)} fusion(bf16[2560,2,768]{2,1,0:T(2,128)(2,1)S(1)} %bitcast.77, bf16[208,5120]{1,0:T(8,128)(2,1)S(1)} %shard_map.103.inputs), kind=kOutput, calls=%fused_computation.6 | convolution fusion | flops 1635778560 | bytes 10207232 | tf_op jit(solution)/shard_map/rd,djh->rjh/dot_general | solution.py:406
  66.9 1.9 %fusion.22 = f32[208,2,768]{2,0,1:T(8,128)S(1)} fusion(f32[208,2,768]{2,0,1:T(8,128)S(1)} %fusion.4, bf16[2560,2,768]{2,1,0:T(2,128)(2,1)S(1)} %bitcast.75, bf16[208,5120]{1,0:T(8,128)(2,1)S(1)} %shard_map.103.inputs), kind=kOutput, calls=%fused_computation.29 | convolution fusion | flops 1636098048 | bytes 11485184 | tf_op jit(solution)/shard_map/rd,djh->rjh/dot_general | solution.py:406
  68.8 3.1 %collective-permute-done.12.refs_1_ = bf16[128,5120]{1,0:T(8,128)(2,1)} collective-permute-done((bf16[128,5120]{1,0:T(8,128)(2,1)S(1)}, bf16[128,5120]{1,0:T(8,128)(2,1)}, u32[]{:S(2)}, u32[]{:S(2)}) %collective-permute-start.12) | collective-permute-done | bytes 1310752 | tf_op jit(solution)/shard_map/ppermute | solution.py:181
  72.5 2.6 %collective-permute-done.17.refs_3_ = bf16[128,5120]{1,0:T(8,128)(2,1)S(1)} collective-permute-done((bf16[128,5120]{1,0:T(8,128)(2,1)}, bf16[128,5120]{1,0:T(8,128)(2,1)S(1)}, u32[]{:S(2)}, u32[]{:S(2)}) %collective-permute-start.17) | collective-permute-done | bytes 1310752 | tf_op jit(solution)/shard_map/ppermute | solution.py:181
  75.1 4.6 %shard_map.104.cotangent = bf16[208,5120]{1,0:T(8,128)(2,1)S(1)} custom-call(bf16[208,512]{1,0:T(8,128)(2,1)S(1)} %get-tuple-element.42.place, bf16[128,5120]{1,0:T(8,128)(2,1)S(1)} %pad_maximum_fusion.1.refs_0_, bf16[128,5120]{1,0:T(8,128)(2,1)} %collective-permute-done.12.refs_1_, bf16[128,5120]{1,0:T(8,128)(2,1)} %collective-permute-done.13.refs_2_, ...), custom_call_target="tpu_custom_call" | custom-call | flops 1 | bytes 1 | tf_op jit(solution)/shard_map/pallas_call | solution.py:215
  79.8 2.1 %multiply_convert_fusion.2 = (bf16[208,768]{1,0:T(8,128)(2,1)S(1)}, bf16[208,768]{1,0:T(8,128)(2,1)S(1)}, bf16[208]{0:T(256)(128)(2,1)S(1)}, bf16[208,768]{1,0:T(8,128)(2,1)S(1)}) fusion(f32[208,2,768]{2,0,1:T(8,128)S(1)} %fusion.22, f32[208]{0:T(256)S(1)} %bitcast.83, bf16[208,5120]{1,0:T(8,128)(2,1)S(1)} %shard_map.104.cotangent, ...), kind=kOutput, calls=%fused_computation.78 | convolution fusion | flops 1638813440 | bytes 12231904 | tf_op jit(solution)/shard_map/dot_general | solution.py:412
  81.9 2.6 %fusion.19 = bf16[208,2560]{1,0:T(8,128)(2,1)S(1)} fusion(bf16[2560,2,768]{2,1,0:T(2,128)(2,1)S(1)} %bitcast.75, bf16[208,1,768]{2,0,1:T(8,128)(2,1)S(1)} %bitcast.70, bf16[208,1,768]{2,0,1:T(8,128)(2,1)S(1)} %bitcast.68), kind=kOutput, calls=%fused_computation.17 | convolution fusion | flops 1636630528 | bytes 9568256 | tf_op jit(solution)/shard_map/rjh,djh->rd/dot_general | solution.py:442
  85.8 2.6 %fusion.16 = bf16[208,2560]{1,0:T(8,128)(2,1)S(1)} fusion(bf16[208,2,768]{2,0,1:T(8,128)(2,1)S(1)} %pad_maximum_fusion.5, bf16[2560,2,768]{2,1,0:T(2,128)(2,1)S(1)} %bitcast.77), kind=kOutput, calls=%fused_computation.16 | convolution fusion | flops 1636311040 | bytes 9568256 | tf_op jit(solution)/shard_map/rjh,djh->rd/dot_general | solution.py:442
  90.1 1.8 %collective-permute-start.19 = (bf16[128,2560]{1,0:T(8,128)(2,1)S(1)}, bf16[128,2560]{1,0:T(8,128)(2,1)S(1)}, u32[]{:S(2)}, u32[]{:S(2)}) collective-permute-start(bf16[128,2560]{1,0:T(8,128)(2,1)S(1)} %slice.358), channel_id=1, source_target_pairs={{0,8},{1,9},{2,10},{3,11},{4,12},{5,13},{6,14},{7,15},{8,0},{9,1},... | collective-permute-start | bytes 1966088 | tf_op jit(solution)/shard_map/ppermute | solution.py:181
  93.0 1.0 collective-permute-start.24
  94.0 10.0 %shard_map.105 = (bf16[5120,2,768]{2,1,0:T(2,128)(2,1)}, bf16[5120,768]{1,0:T(8,128)(2,1)}) custom-call(bf16[208,5120]{1,0:T(8,128)(2,1)S(1)} %shard_map.103.inputs, bf16[208,5120]{1,0:T(8,128)(2,1)S(1)} %shard_map.104.cotangent, bf16[208,768]{1,0:T(8,128)(2,1)S(1)} %get-tuple-element.54.gate_grad, bf16[208,768]{1,0:T(8,128)(2,1)S(1)} %get-tuple-element.71.up_grad, ...), custom_call_target="tpu_custom_call" | custom-call | flops 1 | bytes 1 | tf_op jit(solution)/shard_map/pallas_call | solution.py:251
  104.0 3.0 %collective-permute-done.19 = bf16[128,2560]{1,0:T(8,128)(2,1)S(1)} collective-permute-done((bf16[128,2560]{1,0:T(8,128)(2,1)S(1)}, bf16[128,2560]{1,0:T(8,128)(2,1)S(1)}, u32[]{:S(2)}, u32[]{:S(2)}) %collective-permute-start.19) | collective-permute-done | bytes 655392 | tf_op jit(solution)/shard_map/ppermute | solution.py:181
  107.2 2.2 %collective-permute-start.20 = (bf16[64,2560]{1,0:T(8,128)(2,1)S(1)}, bf16[64,2560]{1,0:T(8,128)(2,1)S(1)}, u32[]{:S(2)}, u32[]{:S(2)}) collective-permute-start(bf16[64,2560]{1,0:T(8,128)(2,1)S(1)} %slice.360), channel_id=1, source_target_pairs={{0,1},{1,0},{2,6},{3,7},{4,5},{5,4},{6,2},{7,3},{8,9},{9,8},{10,14... | collective-permute-start | bytes 983048 | tf_op jit(solution)/shard_map/ppermute | solution.py:181
  109.7 3.7 %shard_map.106 = (bf16[5120,2,768]{2,1,0:T(2,128)(2,1)}, bf16[5120,768]{1,0:T(8,128)(2,1)}) custom-call(bf16[208,5120]{1,0:T(8,128)(2,1)S(1)} %shard_map.103.inputs, bf16[208,5120]{1,0:T(8,128)(2,1)S(1)} %shard_map.104.cotangent, bf16[208,768]{1,0:T(8,128)(2,1)S(1)} %get-tuple-element.54.gate_grad, ...), custom_call_target="tpu_custom_call", output_to_operand_aliasing={{0}: (5, {}), {1}: (6, {})} | custom-call | flops 1 | bytes 1 | tf_op jit(solution)/shard_map/pallas_call | solution.py:251
  113.4 1.0 collective-permute-done.20
  114.5 0.8 collective-permute-start.22
  115.4 2.5 %shard_map.107 = (bf16[5120,2,768]{2,1,0:T(2,128)(2,1)}, bf16[5120,768]{1,0:T(8,128)(2,1)}) custom-call(bf16[208,5120]{1,0:T(8,128)(2,1)S(1)} %shard_map.103.inputs, bf16[208,5120]{1,0:T(8,128)(2,1)S(1)} %shard_map.104.cotangent, bf16[208,768]{1,0:T(8,128)(2,1)S(1)} %get-tuple-element.54.gate_grad, ...), custom_call_target="tpu_custom_call", output_to_operand_aliasing={{0}: (5, {}), {1}: (6, {})} | custom-call | flops 1 | bytes 1 | tf_op jit(solution)/shard_map/pallas_call | solution.py:251
  117.8 2.1 %collective-permute-done.25 = bf16[64,2688]{1,0:T(8,128)(2,1)S(1)} collective-permute-done((bf16[64,2688]{1,0:T(8,128)(2,1)S(1)}, bf16[64,2688]{1,0:T(8,128)(2,1)S(1)}, u32[]{:S(2)}, u32[]{:S(2)}) %collective-permute-start.25) | collective-permute-done | bytes 344096 | tf_op jit(solution)/shard_map/ppermute | solution.py:181
  120.0 1.8 %collective-permute-start.26 = (bf16[32,2688]{1,0:T(8,128)(2,1)S(1)}, bf16[32,2688]{1,0:T(8,128)(2,1)S(1)}, u32[]{:S(2)}, u32[]{:S(2)}) collective-permute-start(bf16[32,2688]{1,0:T(8,128)(2,1)S(1)} %pad_maximum_fusion.12), channel_id=1, source_target_pairs={{0,8},{1,9},{2,10},{3,11},{4,12},{5,13},{6,14},{7,15},{8,0},{9,1},... | collective-permute-start | bytes 516104 | tf_op jit(solution)/shard_map/ppermute | solution.py:181
  121.9 3.9 %collective-permute-start.23 = (bf16[16,2560]{1,0:T(8,128)(2,1)S(1)}, bf16[16,2560]{1,0:T(8,128)(2,1)S(1)}, u32[]{:S(2)}, u32[]{:S(2)}) collective-permute-start(bf16[16,2560]{1,0:T(8,128)(2,1)S(1)} %slice.364), channel_id=1, source_target_pairs={{0,16},{1,17},{2,18},{3,19},{4,20},{5,21},{6,22},{7,23},{8,24},{9,... | collective-permute-start | bytes 245768 | tf_op jit(solution)/shard_map/ppermute | solution.py:181
  126.4 3.6 %collective-permute-start.27 = (bf16[16,2688]{1,0:T(8,128)(2,1)S(1)}, bf16[16,2688]{1,0:T(8,128)(2,1)S(1)}, u32[]{:S(2)}, u32[]{:S(2)}) collective-permute-start(bf16[16,2688]{1,0:T(8,128)(2,1)S(1)} %pad_maximum_fusion.15), channel_id=1, source_target_pairs={{0,16},{1,17},{2,18},{3,19},{4,20},{5,21},{6,22},{7,23},{8,24},{9,... | collective-permute-start | bytes 258056 | tf_op jit(solution)/shard_map/ppermute | solution.py:181
  130.1 0.7 collective-permute-done.23
  130.8 1.7 %collective-permute-done.27 = bf16[16,2688]{1,0:T(8,128)(2,1)S(1)} collective-permute-done((bf16[16,2688]{1,0:T(8,128)(2,1)S(1)}, bf16[16,2688]{1,0:T(8,128)(2,1)S(1)}, u32[]{:S(2)}, u32[]{:S(2)}) %collective-permute-start.27) | collective-permute-done | bytes 86048 | tf_op jit(solution)/shard_map/ppermute | solution.py:181
  132.5 0.7 copy.30
  133.2 0.7 pad_maximum_fusion.13
  (134 shorter events, 10.2 us)
Async XLA Ops:
  0.6 18.0 %copy-start.7 = (bf16[16,5120]{1,0:T(8,128)(2,1)S(1)}, bf16[16,5120]{1,0:T(8,128)(2,1)}, u32[]{:S(2)}) copy-start(bf16[16,5120]{1,0:T(8,128)(2,1)} %param.11) | copy-start | bytes 491524
  2.5 13.3 %collective-permute-start.1 = (bf16[16,3072]{1,0:T(8,128)(2,1)S(1)}, bf16[16,3072]{1,0:T(8,128)(2,1)S(1)}, u32[]{:S(2)}, u32[]{:S(2)}) collective-permute-start(bf16[16,3072]{1,0:T(8,128)(2,1)S(1)} %slice.230), channel_id=1, source_target_pairs={{0,16},{1,17},{2,18},{3,19},{4,20},{5,21},{6,22},{7,23},{8,24},{9,... | collective-permute-start | bytes 294920 | tf_op jit(solution)/shard_map/ppermute | solution.py:181
  6.6 12.0 %collective-permute-start.9 = (bf16[16,5120]{1,0:T(8,128)(2,1)}, bf16[16,5120]{1,0:T(8,128)(2,1)S(1)}, u32[]{:S(2)}, u32[]{:S(2)}) collective-permute-start(bf16[16,5120]{1,0:T(8,128)(2,1)} %param.11), channel_id=1, source_target_pairs={{0,16},{1,17},{2,18},{3,19},{4,20},{5,21},{6,22},{7,23},{8,24},{9,... | collective-permute-start | bytes 491528 | tf_op jit(solution)/shard_map/ppermute | solution.py:181
  8.4 4.4 %collective-permute-start = (bf16[16,2176]{1,0:T(8,128)(2,1)S(1)}, bf16[16,2176]{1,0:T(8,128)(2,1)S(1)}, u32[]{:S(2)}, u32[]{:S(2)}) collective-permute-start(bf16[16,2176]{1,0:T(8,128)(2,1)S(1)} %pad_maximum_fusion.16), channel_id=1, source_target_pairs={{0,4},{1,5},{2,3},{3,2},{4,0},{5,1},{6,7},{7,6},{8,12},{9,13},{10,... | collective-permute-start | bytes 208904 | tf_op jit(solution)/shard_map/ppermute | solution.py:181
  15.9 5.1 %collective-permute-start.2 = (bf16[32,2176]{1,0:T(8,128)(2,1)S(1)}, bf16[32,2176]{1,0:T(8,128)(2,1)S(1)}, u32[]{:S(2)}, u32[]{:S(2)}) collective-permute-start(bf16[32,2176]{1,0:T(8,128)(2,1)S(1)} %pad_maximum_fusion.14), channel_id=1, source_target_pairs={{0,1},{1,0},{2,6},{3,7},{4,5},{5,4},{6,2},{7,3},{8,9},{9,8},{10,14... | collective-permute-start | bytes 417800 | tf_op jit(solution)/shard_map/ppermute | solution.py:181
  17.6 10.9 %collective-permute-start.4 = (bf16[32,3072]{1,0:T(8,128)(2,1)S(1)}, bf16[32,3072]{1,0:T(8,128)(2,1)S(1)}, u32[]{:S(2)}, u32[]{:S(2)}) collective-permute-start(bf16[32,3072]{1,0:T(8,128)(2,1)S(1)} %pad_maximum_fusion.11), channel_id=1, source_target_pairs={{0,8},{1,9},{2,10},{3,11},{4,12},{5,13},{6,14},{7,15},{8,0},{9,1},... | collective-permute-start | bytes 589832 | tf_op jit(solution)/shard_map/ppermute | solution.py:181
  20.9 15.5 %collective-permute-start.3 = (bf16[64,2176]{1,0:T(8,128)(2,1)S(1)}, bf16[64,2176]{1,0:T(8,128)(2,1)S(1)}, u32[]{:S(2)}, u32[]{:S(2)}) collective-permute-start(bf16[64,2176]{1,0:T(8,128)(2,1)S(1)} %pad_maximum_fusion.10), channel_id=1, source_target_pairs={{0,16},{1,17},{2,18},{3,19},{4,20},{5,21},{6,22},{7,23},{8,24},{9,... | collective-permute-start | bytes 835592 | tf_op jit(solution)/shard_map/ppermute | solution.py:181
  28.5 8.6 %collective-permute-start.10 = (bf16[32,5120]{1,0:T(8,128)(2,1)S(1)}, bf16[32,5120]{1,0:T(8,128)(2,1)S(1)}, u32[]{:S(2)}, u32[]{:S(2)}) collective-permute-start(bf16[32,5120]{1,0:T(8,128)(2,1)S(1)} %pad_maximum_fusion.9), channel_id=1, source_target_pairs={{0,8},{1,9},{2,10},{3,11},{4,12},{5,13},{6,14},{7,15},{8,0},{9,1},... | collective-permute-start | bytes 983048 | tf_op jit(solution)/shard_map/ppermute | solution.py:181
  28.5 10.1 %collective-permute-start.5 = (bf16[64,3072]{1,0:T(8,128)(2,1)S(1)}, bf16[64,3072]{1,0:T(8,128)(2,1)S(1)}, u32[]{:S(2)}, u32[]{:S(2)}) collective-permute-start(bf16[64,3072]{1,0:T(8,128)(2,1)S(1)} %pad_maximum_fusion.7), channel_id=1, source_target_pairs={{0,1},{1,0},{2,6},{3,7},{4,5},{5,4},{6,2},{7,3},{8,9},{9,8},{10,14... | collective-permute-start | bytes 1179656 | tf_op jit(solution)/shard_map/ppermute | solution.py:181
  28.7 13.2 %copy-start.6 = (bf16[5120,1,2,768]{3,2,1,0:T(2,128)(2,1)S(1)}, bf16[5120,1,2,768]{3,2,1,0:T(2,128)(2,1)}, u32[]{:S(2)}) copy-start(bf16[5120,1,2,768]{3,2,1,0:T(2,128)(2,1)} %param.12) | copy-start | bytes 47185924
  37.2 16.8 %collective-permute-start.11 = (bf16[64,5120]{1,0:T(8,128)(2,1)S(1)}, bf16[64,5120]{1,0:T(8,128)(2,1)S(1)}, u32[]{:S(2)}, u32[]{:S(2)}) collective-permute-start(bf16[64,5120]{1,0:T(8,128)(2,1)S(1)} %pad_maximum_fusion.4), channel_id=1, source_target_pairs={{0,1},{1,0},{2,6},{3,7},{4,5},{5,4},{6,2},{7,3},{8,9},{9,8},{10,14... | collective-permute-start | bytes 1966088 | tf_op jit(solution)/shard_map/ppermute | solution.py:181
  38.6 15.3 %collective-permute-start.7 = (bf16[128,2176]{1,0:T(8,128)(2,1)S(1)}, bf16[128,2176]{1,0:T(8,128)(2,1)S(1)}, u32[]{:S(2)}, u32[]{:S(2)}) collective-permute-start(bf16[128,2176]{1,0:T(8,128)(2,1)S(1)} %pad_maximum_fusion.6.refs_0_), channel_id=1, source_target_pairs={{0,2},{1,3},{2,0},{3,1},{4,6},{5,7},{6,4},{7,5},{8,10},{9,11},{10,... | collective-permute-start | bytes 1671176 | tf_op jit(solution)/shard_map/ppermute | solution.py:181
  38.7 15.3 %collective-permute-start.6 = (bf16[128,2176]{1,0:T(8,128)(2,1)S(1)}, bf16[128,2176]{1,0:T(8,128)(2,1)S(1)}, u32[]{:S(2)}, u32[]{:S(2)}) collective-permute-start(bf16[128,2176]{1,0:T(8,128)(2,1)S(1)} %pad_maximum_fusion.6.refs_0_), channel_id=1, source_target_pairs={{0,8},{1,9},{2,10},{3,11},{4,12},{5,13},{6,14},{7,15},{8,0},{9,1},... | collective-permute-start | bytes 1671176 | tf_op jit(solution)/shard_map/ppermute | solution.py:181
  40.8 17.5 %collective-permute-start.15 = (bf16[128,3072]{1,0:T(8,128)(2,1)S(1)}, bf16[128,3072]{1,0:T(8,128)(2,1)S(1)}, u32[]{:S(2)}, u32[]{:S(2)}) collective-permute-start(bf16[128,3072]{1,0:T(8,128)(2,1)S(1)} %pad_maximum_fusion.2.refs_0_), channel_id=1, source_target_pairs={{0,2},{1,3},{2,0},{3,1},{4,6},{5,7},{6,4},{7,5},{8,10},{9,11},{10,... | collective-permute-start | bytes 2359304 | tf_op jit(solution)/shard_map/ppermute | solution.py:181
  41.0 14.1 %collective-permute-start.14 = (bf16[128,3072]{1,0:T(8,128)(2,1)S(1)}, bf16[128,3072]{1,0:T(8,128)(2,1)}, u32[]{:S(2)}, u32[]{:S(2)}) collective-permute-start(bf16[128,3072]{1,0:T(8,128)(2,1)S(1)} %pad_maximum_fusion.2.refs_0_), channel_id=1, source_target_pairs={{0,4},{1,5},{2,3},{3,2},{4,0},{5,1},{6,7},{7,6},{8,12},{9,13},{10,... | collective-permute-start | bytes 2359304 | tf_op jit(solution)/shard_map/ppermute | solution.py:181
  53.9 2.6 %copy-start.2 = (bf16[128,2176]{1,0:T(8,128)(2,1)}, bf16[128,2176]{1,0:T(8,128)(2,1)S(1)}, u32[]{:S(2)}) copy-start(bf16[128,2176]{1,0:T(8,128)(2,1)S(1)} %collective-permute-done.6.refs_1_) | copy-start | bytes 1671172
  53.9 2.2 %collective-permute-start.8 = (bf16[128,2176]{1,0:T(8,128)(2,1)S(1)}, bf16[128,2176]{1,0:T(8,128)(2,1)S(1)}, u32[]{:S(2)}, u32[]{:S(2)}) collective-permute-start(bf16[128,2176]{1,0:T(8,128)(2,1)S(1)} %collective-permute-done.6.refs_1_), channel_id=1, source_target_pairs={{0,2},{1,3},{2,0},{3,1},{4,6},{5,7},{6,4},{7,5},{8,10},{9,11},{10,... | collective-permute-start | bytes 1671176 | tf_op jit(solution)/shard_map/ppermute | solution.py:181
  54.0 2.6 %copy-start = (bf16[128,2176]{1,0:T(8,128)(2,1)}, bf16[128,2176]{1,0:T(8,128)(2,1)S(1)}, u32[]{:S(2)}) copy-start(bf16[128,2176]{1,0:T(8,128)(2,1)S(1)} %collective-permute-done.7.refs_2_) | copy-start | bytes 1671172
  54.1 17.8 %collective-permute-start.12 = (bf16[128,5120]{1,0:T(8,128)(2,1)S(1)}, bf16[128,5120]{1,0:T(8,128)(2,1)}, u32[]{:S(2)}, u32[]{:S(2)}) collective-permute-start(bf16[128,5120]{1,0:T(8,128)(2,1)S(1)} %pad_maximum_fusion.1.refs_0_), channel_id=1, source_target_pairs={{0,4},{1,5},{2,3},{3,2},{4,0},{5,1},{6,7},{7,6},{8,12},{9,13},{10,... | collective-permute-start | bytes 3932168 | tf_op jit(solution)/shard_map/ppermute | solution.py:181
  55.1 17.5 %collective-permute-start.13 = (bf16[128,5120]{1,0:T(8,128)(2,1)S(1)}, bf16[128,5120]{1,0:T(8,128)(2,1)}, u32[]{:S(2)}, u32[]{:S(2)}) collective-permute-start(bf16[128,5120]{1,0:T(8,128)(2,1)S(1)} %pad_maximum_fusion.1.refs_0_), channel_id=1, source_target_pairs={{0,2},{1,3},{2,0},{3,1},{4,6},{5,7},{6,4},{7,5},{8,10},{9,11},{10,... | collective-permute-start | bytes 3932168 | tf_op jit(solution)/shard_map/ppermute | solution.py:181
  55.1 4.5 %collective-permute-start.16 = (bf16[128,3072]{1,0:T(8,128)(2,1)}, bf16[128,3072]{1,0:T(8,128)(2,1)}, u32[]{:S(2)}, u32[]{:S(2)}) collective-permute-start(bf16[128,3072]{1,0:T(8,128)(2,1)} %collective-permute-done.14.refs_1_), channel_id=1, source_target_pairs={{0,2},{1,3},{2,0},{3,1},{4,6},{5,7},{6,4},{7,5},{8,10},{9,11},{10,... | collective-permute-start | bytes 2359304 | tf_op jit(solution)/shard_map/ppermute | solution.py:181
  56.2 0.8 copy-start.4
  57.8 6.8 %slice-start.2 = ((s8[7864320]{0:T(1024)(128)(4,1)}), s8[4194304]{0:T(1024)(128)(4,1)S(1)}, s32[]{:S(2)}) async-start(s8[7864320]{0:T(1024)(128)(4,1)} %bitcast.76), calls=%async_computation.2 | async-start | bytes 8388608
  58.2 5.1 %copy-start.1 = (bf16[128,2176]{1,0:T(8,128)(2,1)S(1)}, bf16[128,2176]{1,0:T(8,128)(2,1)}, u32[]{:S(2)}) copy-start(bf16[128,2176]{1,0:T(8,128)(2,1)} %copy-done) | copy-start | bytes 1671172
  58.2 5.1 %copy-start.3 = (bf16[128,2176]{1,0:T(8,128)(2,1)S(1)}, bf16[128,2176]{1,0:T(8,128)(2,1)}, u32[]{:S(2)}) copy-start(bf16[128,2176]{1,0:T(8,128)(2,1)} %copy-done.2) | copy-start | bytes 1671172
  58.2 5.1 %copy-start.5 = (bf16[128,2176]{1,0:T(8,128)(2,1)S(1)}, bf16[128,2176]{1,0:T(8,128)(2,1)}, u32[]{:S(2)}) copy-start(bf16[128,2176]{1,0:T(8,128)(2,1)} %copy-done.4) | copy-start | bytes 1671172
  58.2 6.4 %slice-start.3 = ((s8[7864320]{0:T(1024)(128)(4,1)}), s8[3670016]{0:T(1024)(128)(4,1)S(1)}, s32[]{:S(2)}) async-start(s8[7864320]{0:T(1024)(128)(4,1)} %bitcast.76), calls=%async_computation.3 | async-start | bytes 7340032
  63.3 3.1 %slice-start = ((s8[7864320]{0:T(1024)(128)(4,1)}), s8[4194304]{0:T(1024)(128)(4,1)S(1)}, s32[]{:S(2)}) async-start(s8[7864320]{0:T(1024)(128)(4,1)} %bitcast.74), calls=%async_computation | async-start | bytes 8388608
  64.6 2.3 %slice-start.1 = ((s8[7864320]{0:T(1024)(128)(4,1)}), s8[3670016]{0:T(1024)(128)(4,1)S(1)}, s32[]{:S(2)}) async-start(s8[7864320]{0:T(1024)(128)(4,1)} %bitcast.74), calls=%async_computation.1 | async-start | bytes 7340032
  71.9 3.2 %collective-permute-start.17 = (bf16[128,5120]{1,0:T(8,128)(2,1)}, bf16[128,5120]{1,0:T(8,128)(2,1)S(1)}, u32[]{:S(2)}, u32[]{:S(2)}) collective-permute-start(bf16[128,5120]{1,0:T(8,128)(2,1)} %collective-permute-done.12.refs_1_), channel_id=1, source_target_pairs={{0,2},{1,3},{2,0},{3,1},{4,6},{5,7},{6,4},{7,5},{8,10},{9,11},{10,... | collective-permute-start | bytes 3932168 | tf_op jit(solution)/shard_map/ppermute | solution.py:181
  72.1 7.6 %slice-start.4 = ((s8[7864320]{0:T(1024)(128)(4,1)}), s8[4194304]{0:T(1024)(128)(4,1)S(1)}, s32[]{:S(2)}) async-start(s8[7864320]{0:T(1024)(128)(4,1)} %bitcast.81), calls=%async_computation.4 | async-start | bytes 8388608
  72.5 7.2 %slice-start.5 = ((s8[7864320]{0:T(1024)(128)(4,1)}), s8[3670016]{0:T(1024)(128)(4,1)S(1)}, s32[]{:S(2)}) async-start(s8[7864320]{0:T(1024)(128)(4,1)} %bitcast.81), calls=%async_computation.5 | async-start | bytes 7340032
  85.6 4.0 %collective-permute-start.18 = (bf16[256,2560]{1,0:T(8,128)(2,1)S(1)}, bf16[256,2560]{1,0:T(8,128)(2,1)S(1)}, u32[]{:S(2)}, u32[]{:S(2)}) collective-permute-start(bf16[256,2560]{1,0:T(8,128)(2,1)S(1)} %convolution_convert_fusion.1), channel_id=1, source_target_pairs={{0,2},{1,3},{2,0},{3,1},{4,6},{5,7},{6,4},{7,5},{8,10},{9,11},{10,... | collective-permute-start | bytes 3932168 | tf_op jit(solution)/shard_map/ppermute | solution.py:181
  89.1 3.2 %collective-permute-start.21 = (bf16[256,2688]{1,0:T(8,128)(2,1)S(1)}, bf16[256,2688]{1,0:T(8,128)(2,1)S(1)}, u32[]{:S(2)}, u32[]{:S(2)}) collective-permute-start(bf16[256,2688]{1,0:T(8,128)(2,1)S(1)} %pad_maximum_fusion), channel_id=1, source_target_pairs={{0,2},{1,3},{2,0},{3,1},{4,6},{5,7},{6,4},{7,5},{8,10},{9,11},{10,... | collective-permute-start | bytes 4128776 | tf_op jit(solution)/shard_map/ppermute | solution.py:181
  90.1 16.8 %collective-permute-start.19 = (bf16[128,2560]{1,0:T(8,128)(2,1)S(1)}, bf16[128,2560]{1,0:T(8,128)(2,1)S(1)}, u32[]{:S(2)}, u32[]{:S(2)}) collective-permute-start(bf16[128,2560]{1,0:T(8,128)(2,1)S(1)} %slice.358), channel_id=1, source_target_pairs={{0,8},{1,9},{2,10},{3,11},{4,12},{5,13},{6,14},{7,15},{8,0},{9,1},... | collective-permute-start | bytes 1966088 | tf_op jit(solution)/shard_map/ppermute | solution.py:181
  93.0 16.3 %collective-permute-start.24 = (bf16[128,2688]{1,0:T(8,128)(2,1)S(1)}, bf16[128,2688]{1,0:T(8,128)(2,1)S(1)}, u32[]{:S(2)}, u32[]{:S(2)}) collective-permute-start(bf16[128,2688]{1,0:T(8,128)(2,1)S(1)} %pad_maximum_fusion.3), channel_id=1, source_target_pairs={{0,4},{1,5},{2,3},{3,2},{4,0},{5,1},{6,7},{7,6},{8,12},{9,13},{10,... | collective-permute-start | bytes 2064392 | tf_op jit(solution)/shard_map/ppermute | solution.py:181
  107.2 7.3 %collective-permute-start.20 = (bf16[64,2560]{1,0:T(8,128)(2,1)S(1)}, bf16[64,2560]{1,0:T(8,128)(2,1)S(1)}, u32[]{:S(2)}, u32[]{:S(2)}) collective-permute-start(bf16[64,2560]{1,0:T(8,128)(2,1)S(1)} %slice.360), channel_id=1, source_target_pairs={{0,1},{1,0},{2,6},{3,7},{4,5},{5,4},{6,2},{7,3},{8,9},{9,8},{10,14... | collective-permute-start | bytes 983048 | tf_op jit(solution)/shard_map/ppermute | solution.py:181
  109.6 10.3 %collective-permute-start.25 = (bf16[64,2688]{1,0:T(8,128)(2,1)S(1)}, bf16[64,2688]{1,0:T(8,128)(2,1)S(1)}, u32[]{:S(2)}, u32[]{:S(2)}) collective-permute-start(bf16[64,2688]{1,0:T(8,128)(2,1)S(1)} %pad_maximum_fusion.8), channel_id=1, source_target_pairs={{0,1},{1,0},{2,6},{3,7},{4,5},{5,4},{6,2},{7,3},{8,9},{9,8},{10,14... | collective-permute-start | bytes 1032200 | tf_op jit(solution)/shard_map/ppermute | solution.py:181
  114.5 7.3 %collective-permute-start.22 = (bf16[32,2560]{1,0:T(8,128)(2,1)S(1)}, bf16[32,2560]{1,0:T(8,128)(2,1)S(1)}, u32[]{:S(2)}, u32[]{:S(2)}) collective-permute-start(bf16[32,2560]{1,0:T(8,128)(2,1)S(1)} %slice.362), channel_id=1, source_target_pairs={{0,4},{1,5},{2,3},{3,2},{4,0},{5,1},{6,7},{7,6},{8,12},{9,13},{10,... | collective-permute-start | bytes 491528 | tf_op jit(solution)/shard_map/ppermute | solution.py:181
  120.0 6.3 %collective-permute-start.26 = (bf16[32,2688]{1,0:T(8,128)(2,1)S(1)}, bf16[32,2688]{1,0:T(8,128)(2,1)S(1)}, u32[]{:S(2)}, u32[]{:S(2)}) collective-permute-start(bf16[32,2688]{1,0:T(8,128)(2,1)S(1)} %pad_maximum_fusion.12), channel_id=1, source_target_pairs={{0,8},{1,9},{2,10},{3,11},{4,12},{5,13},{6,14},{7,15},{8,0},{9,1},... | collective-permute-start | bytes 516104 | tf_op jit(solution)/shard_map/ppermute | solution.py:181
  121.9 8.9 %collective-permute-start.23 = (bf16[16,2560]{1,0:T(8,128)(2,1)S(1)}, bf16[16,2560]{1,0:T(8,128)(2,1)S(1)}, u32[]{:S(2)}, u32[]{:S(2)}) collective-permute-start(bf16[16,2560]{1,0:T(8,128)(2,1)S(1)} %slice.364), channel_id=1, source_target_pairs={{0,16},{1,17},{2,18},{3,19},{4,20},{5,21},{6,22},{7,23},{8,24},{9,... | collective-permute-start | bytes 245768 | tf_op jit(solution)/shard_map/ppermute | solution.py:181
  126.4 6.1 %collective-permute-start.27 = (bf16[16,2688]{1,0:T(8,128)(2,1)S(1)}, bf16[16,2688]{1,0:T(8,128)(2,1)S(1)}, u32[]{:S(2)}, u32[]{:S(2)}) collective-permute-start(bf16[16,2688]{1,0:T(8,128)(2,1)S(1)} %pad_maximum_fusion.15), channel_id=1, source_target_pairs={{0,16},{1,17},{2,18},{3,19},{4,20},{5,21},{6,22},{7,23},{8,24},{9,... | collective-permute-start | bytes 258056 | tf_op jit(solution)/shard_map/ppermute | solution.py:181
